TPU v7x, 32 devices: a whole 2x2x4 slice. The times are simulated.
32 devices in a mesh: seg: 8 (over z, core), seq: 4 (over y, x).
Axes of the slice: x: 2, y: 2, z: 4, core: 2. Of those that a mesh axis runs over, the one named last changes fastest.
Arguments:
- layer_input: bfloat16 [8, 2048, 1024], P('seg', 'seq'), may hold values from -6 to 6
- output_grad: bfloat16 [8, 2048, 1024], P('seg', 'seq'), may hold values from -6 to 6
- norm1_gain: float32 [1024], replicated, may hold values from 0.5 to 1.5
- norm2_gain: float32 [1024], replicated, may hold values from 0.5 to 1.5
- w_qkv: bfloat16 [1024, 3072], replicated, may hold values from -0.25 to 0.25
- w_out: bfloat16 [1024, 1024], replicated, may hold values from -0.75 to 0.75
- w_gate: bfloat16 [1024, 2816], replicated, may hold values from -0.1875 to 0.1875
- w_up: bfloat16 [1024, 2816], replicated, may hold values from -0.1875 to 0.1875
- w_down: bfloat16 [2816, 1024], replicated, may hold values from -0.109375 to 0.109375
- mem_keys: bfloat16 [8, 1024, 1024], P('seg', 'seq'), may hold values from -8 to 8
- mem_values: bfloat16 [8, 1024, 1024], P('seg', 'seq'), may hold values from -8 to 8
- memory_flags: int32 [8], replicated, may hold values from 0 to 1, as said below
- sources: int32 [8, 3], replicated, may hold values from 0 to 7, as said below
Outputs:
- output: bfloat16 [8, 2048, 1024], P('seg', 'seq')
- input_grad: float32 [8, 2048, 1024], P('seg', 'seq')
- grad_norm1: float32 [1024], P('seq')
- grad_norm2: float32 [1024], P('seq')
- grad_qkv: float32 [1024, 3072], P('seq')
- grad_out: float32 [1024, 1024], P('seq')
- grad_gate: float32 [1024, 2816], P('seq')
- grad_up: float32 [1024, 2816], P('seq')
- grad_down: float32 [2816, 1024], P('seq')
Inputs may be any that keep to these rules, and one draw needn't show every extreme that they name: `memory_flags`: exactly half of the segments have flag 1. `sources`: row s lists 3 different segments, none of them s. The first column is a permutation of the segments, and the first source of a segment has the other flag than the segment.
All inputs are finite; a program needn't handle non-finite values.
Results may differ from a plain program's by a relative error of at most 0.023.
Values may be sent and summed in bfloat16 or wider, within the bound.
A program may use at most 256 MiB of HBM per device.

v0:
```python
import functools
import math

import jax
import jax.numpy as jnp
from jax import lax
from jax.experimental import pallas as pl
from jax.experimental.pallas import tpu as pltpu
from jax.sharding import PartitionSpec as P

D = 1024
HEADS = 8
HEAD_DIM = 128


masked_score = -1e30
epsilon = 1e-06
rotary_base = 10000.0


def product(former, latter):
    return jnp.dot(former, latter, preferred_element_type=jnp.float32)


def product_nt(former, latter):
    return lax.dot_general(
        former, latter, (((1,), (1,)), ((), ())), preferred_element_type=jnp.float32
    )


def product_tn(former, latter):
    return lax.dot_general(
        former, latter, (((0,), (0,)), ((), ())), preferred_element_type=jnp.float32
    )


def norm_forward(values, norm_gain):
    inverse = lax.rsqrt(jnp.mean(values * values, axis=-1, keepdims=True) + epsilon)
    return (values * inverse * norm_gain, inverse)


def norm_backward(values, inverse, norm_gain, upstream):
    weighted = upstream * norm_gain
    inner_mean = jnp.mean(weighted * values, axis=-1, keepdims=True)
    grad_values = inverse * weighted - inverse * inverse * inverse * values * inner_mean
    grad_gain = jnp.sum(upstream * values * inverse, axis=0)
    return (grad_values, grad_gain)


def turn_tables(positions):
    half_dim = HEAD_DIM // 2
    exponent = -2.0 * jnp.arange(half_dim, dtype=jnp.float32) / HEAD_DIM
    angles = positions[:, None] * jnp.power(rotary_base, exponent)[None, :]
    angles = jnp.concatenate([angles, angles], axis=1)
    return (jnp.cos(angles)[:, None, :], jnp.sin(angles)[:, None, :])


def rotate(matrix, cosine_table, sine_table, direction):
    row_count = matrix.shape[0]
    half_dim = HEAD_DIM // 2
    shaped = matrix.reshape(row_count, HEADS, HEAD_DIM)
    turned = jnp.concatenate([-shaped[..., half_dim:], shaped[..., :half_dim]], axis=-1)
    return (shaped * cosine_table + direction * turned * sine_table).reshape(
        row_count, HEADS * HEAD_DIM
    )


def general_plan(
    layer_input,
    output_grad,
    norm1_gain,
    norm2_gain,
    w_qkv,
    w_out,
    w_gate,
    w_up,
    w_down,
    mem_keys,
    mem_values,
    memory_flags,
    sources,
):
    seg_index = lax.axis_index("seg")
    seq_index = lax.axis_index("seq")
    tokens = layer_input.shape[1]
    score_scale = HEAD_DIM ** (-0.5)
    flag_on = lax.dynamic_index_in_dim(memory_flags, seg_index, 0, keepdims=False) > 0
    listed = lax.dynamic_index_in_dim(sources, seg_index, 0, keepdims=False)
    picked = jnp.concatenate([jnp.reshape(seg_index, (1,)), listed])
    every_keys, every_values = (
        lax.all_gather(mem_keys, "seg", axis=0, tiled=True),
        lax.all_gather(mem_values, "seg", axis=0, tiled=True),
    )
    chosen_keys = jnp.take(every_keys, picked, axis=0)
    chosen_values = jnp.take(every_values, picked, axis=0)
    memory_keys, memory_values = (
        lax.all_gather(chosen_keys, "seq", axis=1, tiled=True),
        lax.all_gather(chosen_values, "seq", axis=1, tiled=True),
    )
    memory_key_blocks = memory_keys.reshape(-1, tokens, HEADS, HEAD_DIM)
    memory_value_blocks = memory_values.reshape(-1, tokens, HEADS, HEAD_DIM)
    memory_blocks = memory_key_blocks.shape[0]
    inputs = layer_input[0].astype(jnp.float32)
    first_norm, first_inverse = norm_forward(inputs, norm1_gain)
    first_low = first_norm.astype(jnp.bfloat16)
    projected = product(first_low, w_qkv)
    positions = seq_index * tokens + lax.iota(jnp.int32, tokens)
    cosine_table, sine_table = turn_tables(positions.astype(jnp.float32))
    queries = rotate(projected[:, :D], cosine_table, sine_table, 1.0).astype(jnp.bfloat16)
    own_keys = rotate(projected[:, D : 2 * D], cosine_table, sine_table, 1.0).astype(jnp.bfloat16)
    own_values = projected[:, 2 * D :].astype(jnp.bfloat16)
    all_keys, all_values = (
        lax.all_gather(own_keys, "seq", axis=0, tiled=True),
        lax.all_gather(own_values, "seq", axis=0, tiled=True),
    )
    key_blocks = all_keys.reshape(-1, tokens, HEADS, HEAD_DIM)
    value_blocks = all_values.reshape(-1, tokens, HEADS, HEAD_DIM)
    query_heads = queries.reshape(tokens, HEADS, HEAD_DIM)
    memory_open = jnp.broadcast_to(flag_on, (tokens, tokens))
    own_count = seq_index + 1
    key_offsets = lax.iota(jnp.int32, tokens)

    def own_open(block):
        return (block * tokens + key_offsets)[None, :] <= positions[:, None]

    def block_scores(key_block, open_mask):
        raw = (
            jnp.einsum("qhd,khd->hqk", query_heads, key_block, preferred_element_type=jnp.float32)
            * score_scale
        )
        return jnp.where(open_mask[None], raw, masked_score)

    def sweep(step, carry):

        def memory_turn(block, state):
            return step(
                state,
                block,
                memory_key_blocks[block],
                memory_value_blocks[block],
                memory_open,
                False,
            )

        def own_turn(block, state):
            return step(state, block, key_blocks[block], value_blocks[block], own_open(block), True)

        carry = lax.fori_loop(0, memory_blocks, memory_turn, carry)
        return lax.fori_loop(0, own_count, own_turn, carry)

    def max_step(carry, block, key_block, value_block, open_mask, own):
        row_max, row_sum = carry
        scores = block_scores(key_block, open_mask)
        new_max = jnp.maximum(row_max, jnp.max(scores, axis=2))
        row_sum = row_sum * jnp.exp(row_max - new_max) + jnp.sum(
            jnp.exp(scores - new_max[..., None]), axis=2
        )
        return (new_max, row_sum)

    start_max = jnp.full((HEADS, tokens), masked_score, jnp.float32)
    row_max, row_sum = sweep(max_step, (start_max, jnp.zeros((HEADS, tokens), jnp.float32)))
    log_totals = row_max + jnp.log(row_sum)

    def mix_step(total, block, key_block, value_block, open_mask, own):
        weights_low = jnp.exp(block_scores(key_block, open_mask) - log_totals[..., None]).astype(
            jnp.bfloat16
        )
        return total + jnp.einsum(
            "hqk,khd->qhd", weights_low, value_block, preferred_element_type=jnp.float32
        )

    attended = sweep(mix_step, jnp.zeros((tokens, HEADS, HEAD_DIM), jnp.float32))
    attended_low = attended.reshape(tokens, D).astype(jnp.bfloat16)
    residual = inputs + product(attended_low, w_out)
    second_norm, second_inverse = norm_forward(residual, norm2_gain)
    second_low = second_norm.astype(jnp.bfloat16)
    gate_values = product(second_low, w_gate)
    up_values = product(second_low, w_up)
    sigmoid_gate = jax.nn.sigmoid(gate_values)
    activated = gate_values * sigmoid_gate
    hidden_low = (activated * up_values).astype(jnp.bfloat16)
    output = (residual + product(hidden_low, w_down)).astype(jnp.bfloat16)
    upstream = output_grad[0]
    grad_down = product_tn(hidden_low, upstream)
    grad_hidden = product_nt(upstream, w_down)
    grad_gate_low = (
        grad_hidden * up_values * sigmoid_gate * (1.0 + gate_values * (1.0 - sigmoid_gate))
    ).astype(jnp.bfloat16)
    grad_up_low = (grad_hidden * activated).astype(jnp.bfloat16)
    grad_gate = product_tn(second_low, grad_gate_low)
    grad_up = product_tn(second_low, grad_up_low)
    grad_second = product_nt(grad_gate_low, w_gate) + product_nt(grad_up_low, w_up)
    grad_residual, grad_norm2 = norm_backward(residual, second_inverse, norm2_gain, grad_second)
    grad_residual = grad_residual + upstream.astype(jnp.float32)
    residual_low = grad_residual.astype(jnp.bfloat16)
    grad_out = product_tn(attended_low, residual_low)
    grad_attended = product_nt(residual_low, w_out).astype(jnp.bfloat16)
    grad_heads = grad_attended.reshape(tokens, HEADS, HEAD_DIM)

    def probs_pair(key_block, value_block, open_mask):
        probs = jnp.exp(block_scores(key_block, open_mask) - log_totals[..., None])
        dprobs = jnp.einsum(
            "qhd,khd->hqk", grad_heads, value_block, preferred_element_type=jnp.float32
        )
        return (probs, dprobs)

    def delta_step(total, block, key_block, value_block, open_mask, own):
        probs, dprobs = probs_pair(key_block, value_block, open_mask)
        return total + jnp.sum(probs * dprobs, axis=2)

    delta_rows = sweep(delta_step, jnp.zeros((HEADS, tokens), jnp.float32))

    def grad_step(carry, block, key_block, value_block, open_mask, own):
        grad_query, key_terms, value_terms = carry
        probs, dprobs = probs_pair(key_block, value_block, open_mask)
        dscores = (probs * (dprobs - delta_rows[..., None])).astype(jnp.bfloat16)
        grad_query = grad_query + jnp.einsum(
            "hqk,khd->qhd", dscores, key_block, preferred_element_type=jnp.float32
        )
        if own:
            key_part = (
                jnp.einsum("hqk,qhd->khd", dscores, query_heads, preferred_element_type=jnp.float32)
                * score_scale
            )
            value_part = jnp.einsum(
                "hqk,qhd->khd",
                probs.astype(jnp.bfloat16),
                grad_heads,
                preferred_element_type=jnp.float32,
            )
            key_terms = lax.dynamic_update_index_in_dim(key_terms, key_part, block, 0)
            value_terms = lax.dynamic_update_index_in_dim(value_terms, value_part, block, 0)
        return (grad_query, key_terms, value_terms)

    term_shape = key_blocks.shape
    start_grads = (
        jnp.zeros((tokens, HEADS, HEAD_DIM), jnp.float32),
        jnp.zeros(term_shape, jnp.float32),
        jnp.zeros(term_shape, jnp.float32),
    )
    grad_query, key_terms, value_terms = sweep(grad_step, start_grads)
    grad_queries = (grad_query * score_scale).reshape(tokens, D)
    grad_keys, grad_values = (
        lax.psum_scatter(
            key_terms.astype(jnp.bfloat16), "seq", scatter_dimension=0, tiled=True
        ).astype(jnp.float32),
        lax.psum_scatter(
            value_terms.astype(jnp.bfloat16), "seq", scatter_dimension=0, tiled=True
        ).astype(jnp.float32),
    )
    grad_projected = jnp.concatenate(
        [
            rotate(grad_queries, cosine_table, sine_table, -1.0),
            rotate(grad_keys.reshape(tokens, D), cosine_table, sine_table, -1.0),
            grad_values.reshape(tokens, D),
        ],
        axis=1,
    ).astype(jnp.bfloat16)
    grad_qkv = product_tn(first_low, grad_projected)
    grad_first = product_nt(grad_projected, w_qkv)
    grad_inputs, grad_norm1 = norm_backward(inputs, first_inverse, norm1_gain, grad_first)
    input_grad = (grad_inputs + grad_residual)[None]
    shares = (
        lax.psum_scatter(
            grad_norm1.astype(jnp.bfloat16), "seq", scatter_dimension=0, tiled=True
        ).astype(jnp.float32),
        lax.psum_scatter(
            grad_norm2.astype(jnp.bfloat16), "seq", scatter_dimension=0, tiled=True
        ).astype(jnp.float32),
        lax.psum_scatter(
            grad_qkv.astype(jnp.bfloat16), "seq", scatter_dimension=0, tiled=True
        ).astype(jnp.float32),
        lax.psum_scatter(
            grad_out.astype(jnp.bfloat16), "seq", scatter_dimension=0, tiled=True
        ).astype(jnp.float32),
        lax.psum_scatter(
            grad_gate.astype(jnp.bfloat16), "seq", scatter_dimension=0, tiled=True
        ).astype(jnp.float32),
        lax.psum_scatter(
            grad_up.astype(jnp.bfloat16), "seq", scatter_dimension=0, tiled=True
        ).astype(jnp.float32),
        lax.psum_scatter(
            grad_down.astype(jnp.bfloat16), "seq", scatter_dimension=0, tiled=True
        ).astype(jnp.float32),
    )
    totals = (
        lax.psum(shares[0].astype(jnp.bfloat16), "seg").astype(jnp.float32),
        lax.psum(shares[1].astype(jnp.bfloat16), "seg").astype(jnp.float32),
        lax.psum(shares[2].astype(jnp.bfloat16), "seg").astype(jnp.float32),
        lax.psum(shares[3].astype(jnp.bfloat16), "seg").astype(jnp.float32),
        lax.psum(shares[4].astype(jnp.bfloat16), "seg").astype(jnp.float32),
        lax.psum(shares[5].astype(jnp.bfloat16), "seg").astype(jnp.float32),
        lax.psum(shares[6].astype(jnp.bfloat16), "seg").astype(jnp.float32),
    )
    return (
        output[None],
        input_grad,
        totals[0],
        totals[1],
        totals[2],
        totals[3],
        totals[4],
        totals[5],
        totals[6],
    )


VMEM_BYTES = 60 * 1024 * 1024
LN2 = math.log(2.0)
SCORE_SCALE = HEAD_DIM ** (-0.5)


def lane_fold(op, tile, running):
    for column in range(tile.shape[1] // HEAD_DIM):
        piece = tile[:, column * HEAD_DIM : (column + 1) * HEAD_DIM]
        running = piece if running is None else op(running, piece)
    return running


def causal(scores):
    rows = lax.broadcasted_iota(jnp.int32, scores.shape, 0)
    columns = lax.broadcasted_iota(jnp.int32, scores.shape, 1)
    return jnp.where(columns <= rows, scores, masked_score)


def attend(query, pairs, diagonal, carried):
    every, lane_max = [], None
    for index, (keys, _) in enumerate(pairs):
        scores = product_nt(query, keys)
        if diagonal and index == len(pairs) - 1:
            scores = causal(scores)
        lane_max = lane_fold(jnp.maximum, scores, lane_max)
        every.append(scores)
    row_max = jnp.max(lane_max, axis=1, keepdims=True)
    if carried is not None:
        row_max = jnp.maximum(row_max, carried[0])
    lane_sum, mixed = None, None
    for scores, (_, values) in zip(every, pairs):
        probs = jnp.exp2(scores - row_max)
        lane_sum = lane_fold(jnp.add, probs, lane_sum)
        part = product(probs.astype(jnp.bfloat16), values)
        mixed = part if mixed is None else mixed + part
    row_sum = jnp.sum(lane_sum, axis=1, keepdims=True)
    if carried is not None:
        shrink = jnp.exp2(carried[0] - row_max)
        row_sum = carried[1] * shrink + row_sum
        mixed = carried[2] * shrink + mixed
    return row_max, row_sum, mixed


def memory_specs(heads, rows, count):
    specs = []
    for slot in range(count):
        specs.append(
            pl.BlockSpec((1, rows, HEAD_DIM), lambda h, i, chosen, slot=slot: (chosen[slot], 0, h))
        )
        specs.append(
            pl.BlockSpec(
                (1, rows, HEAD_DIM), lambda h, i, chosen, slot=slot: (chosen[slot], 0, heads + h)
            )
        )
    return specs


def memory_forward_kernel(count, chosen, q_ref, mix_ref, max_ref, sum_ref, *rest):
    blocks = rest[: 2 * count]
    low_ref, out_ref, log_ref = rest[2 * count :]
    carried = (max_ref[:, :1], sum_ref[:, :1], mix_ref[...])

    def finish(row_max, row_sum, mixed):
        out = mixed * (1.0 / row_sum)
        out_ref[...] = out
        low_ref[...] = out.astype(jnp.bfloat16)
        log_ref[...] = jnp.broadcast_to(row_max + jnp.log2(row_sum), log_ref.shape)

    @pl.when(chosen[count] > 0)
    def _():
        pairs = [(blocks[2 * n][0], blocks[2 * n + 1][0]) for n in range(count)]
        finish(*attend(q_ref[...], pairs, False, carried))

    @pl.when(chosen[count] <= 0)
    def _():
        finish(*carried)


def memory_forward(chosen, queries, mixed, row_max, row_sum, memory, rows=512):
    length, width = queries.shape
    heads, count = width // HEAD_DIM, chosen.shape[0] - 1
    block = pl.BlockSpec((rows, HEAD_DIM), lambda h, i, chosen: (i, h))
    pairs = heads * length * count * memory.shape[1]
    return pl.pallas_call(
        functools.partial(memory_forward_kernel, count),
        grid_spec=pltpu.PrefetchScalarGridSpec(
            num_scalar_prefetch=1,
            grid=(heads, length // rows),
            in_specs=[block] * 4 + memory_specs(heads, memory.shape[1], count),
            out_specs=[block] * 3,
        ),
        out_shape=[
            jax.ShapeDtypeStruct((length, width), jnp.bfloat16),
            jax.ShapeDtypeStruct((length, width), jnp.float32),
            jax.ShapeDtypeStruct((length, width), jnp.float32),
        ],
        compiler_params=pltpu.CompilerParams(vmem_limit_bytes=VMEM_BYTES),
        cost_estimate=pl.CostEstimate(
            flops=8 * pairs * HEAD_DIM, transcendentals=pairs, bytes_accessed=36 * length * width
        ),
        name="memory_forward",
    )(chosen, queries, mixed, row_max, row_sum, *[memory] * (2 * count))


def memory_backward_kernel(count, tile, chosen, q_ref, g_ref, out_ref, log_ref, *rest):
    blocks = rest[: 2 * count]
    dq_ref, delta_ref = rest[2 * count :]
    query, upstream = q_ref[...], g_ref[...]
    delta = jnp.sum(upstream.astype(jnp.float32) * out_ref[...], axis=1, keepdims=True)
    delta_ref[...] = jnp.broadcast_to(delta, delta_ref.shape)
    log_total = log_ref[:, :1]

    @pl.when(chosen[count] > 0)
    def _():
        total = jnp.zeros(dq_ref.shape, jnp.float32)
        for n in range(count):
            for start in range(0, blocks[0].shape[1], tile):
                keys = blocks[2 * n][0, start : start + tile, :]
                values = blocks[2 * n + 1][0, start : start + tile, :]
                probs = jnp.exp2(product_nt(query, keys) - log_total)
                dscores = probs * (product_nt(upstream, values) - delta)
                total = total + product(dscores.astype(jnp.bfloat16), keys)
        dq_ref[...] = total

    @pl.when(chosen[count] <= 0)
    def _():
        dq_ref[...] = jnp.zeros(dq_ref.shape, jnp.float32)


def memory_backward(chosen, queries, upstream, out, log_totals, memory, rows=512, tile=512):
    length, width = queries.shape
    heads, count = width // HEAD_DIM, chosen.shape[0] - 1
    block = pl.BlockSpec((rows, HEAD_DIM), lambda h, i, chosen: (i, h))
    pairs = heads * length * count * memory.shape[1]
    return pl.pallas_call(
        functools.partial(memory_backward_kernel, count, math.gcd(tile, memory.shape[1])),
        grid_spec=pltpu.PrefetchScalarGridSpec(
            num_scalar_prefetch=1,
            grid=(heads, length // rows),
            in_specs=[block] * 4 + memory_specs(heads, memory.shape[1], count),
            out_specs=[block] * 2,
        ),
        out_shape=[jax.ShapeDtypeStruct((length, width), jnp.float32)] * 2,
        compiler_params=pltpu.CompilerParams(vmem_limit_bytes=VMEM_BYTES),
        cost_estimate=pl.CostEstimate(
            flops=12 * pairs * HEAD_DIM, transcendentals=pairs, bytes_accessed=36 * length * width
        ),
        name="memory_backward",
    )(chosen, queries, upstream, out, log_totals, *[memory] * (2 * count))


def own_backward_kernel(
    rows, heads, q_ref, k_ref, v_ref, g_ref, log_ref, delta_ref, start_ref, cos_ref, sin_ref, d_ref, dk, dv
):
    head, block = pl.program_id(0), pl.program_id(1)

    def lanes(part):
        return pl.ds(pl.multiple_of((part * heads + head) * HEAD_DIM, HEAD_DIM), HEAD_DIM)

    @pl.when(block == 0)
    def _():
        dk[...] = jnp.zeros_like(dk)
        dv[...] = jnp.zeros_like(dv)

    query, upstream = q_ref[...], g_ref[...]
    log_total, delta = log_ref[:, :1], delta_ref[:, :1]

    def turn(other, total, diagonal):
        span = pl.ds(pl.multiple_of(other * rows, rows), rows)
        keys = k_ref[span, :]
        scores = product_nt(query, keys)
        if diagonal:
            scores = causal(scores)
        probs = jnp.exp2(scores - log_total)
        dscores = (probs * (product_nt(upstream, v_ref[span, :]) - delta)).astype(jnp.bfloat16)
        dv[span, :] += product_tn(probs.astype(jnp.bfloat16), upstream)
        dk[span, :] += product_tn(dscores, query)
        return total + product(dscores, keys)

    total = turn(block, start_ref[...], True)
    total = lax.fori_loop(0, block, lambda other, total: turn(other, total, False), total)
    mine = pl.ds(pl.multiple_of(block * rows, rows), rows)
    d_ref[mine, lanes(0)] = turn_block(
        total * SCORE_SCALE, cos_ref[mine, :], -sin_ref[mine, :]
    ).astype(jnp.bfloat16)

    @pl.when(block == pl.num_programs(1) - 1)
    def _():
        d_ref[:, lanes(1)] = turn_block(dk[...] * LN2, cos_ref[...], -sin_ref[...]).astype(
            jnp.bfloat16
        )
        d_ref[:, lanes(2)] = dv[...].astype(jnp.bfloat16)


def own_backward(
    queries, keys, values, upstream, log_totals, delta, start, cosine, sine, rows=512
):
    length, width = queries.shape
    block = pl.BlockSpec((rows, HEAD_DIM), lambda h, i: (i, h))
    whole = pl.BlockSpec((length, HEAD_DIM), lambda h, i: (0, h))
    table = pl.BlockSpec((length, HEAD_DIM), lambda h, i: (0, 0))
    heads = width // HEAD_DIM
    pairs = heads * length * length // 2
    return pl.pallas_call(
        functools.partial(own_backward_kernel, rows, heads),
        grid=(heads, length // rows),
        in_specs=[block, whole, whole, block, block, block, block, table, table],
        out_specs=pl.BlockSpec((length, 3 * width), lambda h, i: (0, 0)),
        out_shape=jax.ShapeDtypeStruct((length, 3 * width), jnp.bfloat16),
        scratch_shapes=[pltpu.VMEM((length, HEAD_DIM), jnp.float32)] * 2,
        compiler_params=pltpu.CompilerParams(vmem_limit_bytes=VMEM_BYTES),
        cost_estimate=pl.CostEstimate(
            flops=20 * pairs * HEAD_DIM, transcendentals=pairs, bytes_accessed=36 * length * width
        ),
        name="own_backward",
    )(queries, keys, values, upstream, log_totals, delta, start, cosine, sine)


def turn_block(matrix, cosine, sine):
    return matrix * cosine + pltpu.roll(matrix, HEAD_DIM // 2, 1) * sine


LINK_RATE = {"core": 300e3, "x": 45e3, "y": 45e3, "z": 45e3}


class Place:
    def __init__(self):
        seg, seq = lax.axis_index("seg"), lax.axis_index("seq")
        self.core, self.z = lax.rem(seg, 2), lax.div(seg, 2)
        self.x, self.y = lax.rem(seq, 2), lax.div(seq, 2)
        odd = lax.rem(self.z, 2)
        self.inner = jnp.logical_or(self.z == 1, self.z == 2)
        self.outer = jnp.logical_not(self.inner)
        self.peer = {
            "core": (seg + 1 - 2 * self.core, seq),
            "x": (seg, seq + 1 - 2 * self.x),
            "y": (seg, seq + 2 - 4 * self.y),
            "xy": (seg, 3 - seq),
            "pair": (seg + 2 - 4 * odd, seq),
            "middle": (seg - 2 + 4 * odd, seq),
        }

    def greet(self, names):
        barrier = pltpu.get_barrier_semaphore()

        def hail(name):
            pl.semaphore_signal(
                barrier, inc=1, device_id=self.peer[name], device_id_type=pl.DeviceIdType.MESH
            )

        for name in names:
            hail(name)

        @pl.when(self.inner)
        def _():
            hail("middle")

        pl.semaphore_wait(barrier, len(names) + self.inner.astype(jnp.int32))


def add_into(total, addend, step=16):
    def turn(index, carry):
        rows = pl.ds(pl.multiple_of(index * step, step), step)
        total[rows, :] = total[rows, :] + addend[rows, :]
        return carry

    lax.fori_loop(0, total.shape[0] // step, turn, 0)


def add_to(result, former, latter, step=16):
    def turn(index, carry):
        rows = pl.ds(pl.multiple_of(index * step, step), step)
        result[rows, :] = former[rows, :] + latter[rows, :]
        return carry

    lax.fori_loop(0, result.shape[0] // step, turn, 0)


class Chunk:
    def __init__(self, term, offset, rows, columns, gather=False):
        self.term, self.offset, self.rows, self.columns = term, offset, rows, columns
        self.gather = gather

    def scratch(self):
        rows, columns, half = self.rows, self.columns, self.columns // 2
        low = jnp.bfloat16
        four = pltpu.VMEM((2, 2, rows, columns), low)
        one = four if self.gather else pltpu.VMEM((rows, columns), low)
        last = pltpu.VMEM((rows, 4 * columns), low) if self.gather else one
        if self.gather:
            middle = [four]
        else:
            middle = [
                pltpu.VMEM((2, rows, half), low),
                pltpu.VMEM((2, rows, half), low),
                pltpu.VMEM((rows, half), low),
                pltpu.VMEM((rows, half), low),
            ]
        return [four, four] + middle + [one, one, last] + [
            pltpu.SemaphoreType.DMA((9,)),
            pltpu.SemaphoreType.DMA((9,)),
            pltpu.SemaphoreType.DMA((3,)),
        ]

    def bind(self, place, source, result, refs):
        self.place, self.source, self.result = place, source, result
        self.mine, self.core_in = refs[0], refs[1]
        self.middle = refs[2:-6]
        self.z_first, self.z_second, self.z_last = refs[-6:-3]
        self.sent, self.received, self.local = refs[-3:]

    def remote(self, slot, source, target, peer):
        return pltpu.make_async_remote_copy(
            src_ref=source,
            dst_ref=target,
            send_sem=self.sent.at[slot],
            recv_sem=self.received.at[slot],
            device_id=self.place.peer[peer],
            device_id_type=pl.DeviceIdType.MESH,
        )

    def core_copy(self):
        rows = pl.ds(self.offset, self.rows)
        return self.remote(
            0, self.source.at[:, :, 1 - self.place.core, rows, :], self.core_in, "core"
        )

    def load(self):
        rows = pl.ds(self.offset, self.rows)
        return pltpu.make_async_copy(
            self.source.at[:, :, self.place.core, rows, :], self.mine, self.local.at[0]
        )

    def halves(self):
        half = self.columns // 2
        return pl.ds(0, half), pl.ds(half, half)

    def wide_copies(self):
        p, (left, right) = self.place, self.halves()
        if self.gather:
            return [
                self.remote(1, self.mine.at[p.y, 1 - p.x], self.middle[0].at[p.y, p.x], "x"),
                self.remote(2, self.mine.at[1 - p.y, p.x], self.middle[0].at[p.y, p.x], "y"),
                self.remote(3, self.mine.at[1 - p.y, 1 - p.x], self.middle[0].at[p.y, p.x], "xy"),
            ]
        return [
            self.remote(1, self.mine.at[:, 1 - p.x, :, left], self.middle[0], "x"),
            self.remote(2, self.mine.at[1 - p.y, :, :, right], self.middle[1], "y"),
        ]

    def narrow_copies(self):
        p, (left, right) = self.place, self.halves()
        return [
            self.remote(3, self.mine.at[1 - p.y, p.x, :, left], self.middle[2], "y"),
            self.remote(4, self.mine.at[p.y, 1 - p.x, :, right], self.middle[3], "x"),
        ]

    def summed(self):
        return self.middle[0] if self.gather else self.mine.at[self.place.y, self.place.x]

    def pair_copy(self):
        return self.remote(5, self.summed(), self.z_first, "pair")

    def middle_copy(self):
        return self.remote(6, self.summed(), self.z_second, "middle")

    def last_copy(self):
        return self.remote(7, self.z_last, self.z_last, "pair")

    def out_copies(self):
        rows = pl.ds(self.offset, self.rows)
        core = self.place.core
        target = self.result.at[core, rows, :]
        return (
            self.remote(8, self.z_last, target, "core"),
            pltpu.make_async_copy(self.z_last, target, self.local.at[1]),
        )

    def parts(self, ref):
        if self.gather:
            return [ref.at[a, b] for a in range(2) for b in range(2)]
        return [ref]

    def lay_out(self):
        part = self.columns // 3
        for owner in range(4):
            for kind in range(3):
                lanes = pl.ds(kind * part, part)
                former = self.middle[0].at[owner // 2, owner % 2, :, lanes]
                latter = self.z_second.at[owner // 2, owner % 2, :, lanes]
                add_to(self.z_last.at[:, pl.ds((4 * kind + owner) * part, part)], former, latter)

    def stage_start(self):
        self.core_copy().start()
        self.load().start()

    def stage_core(self):
        self.core_copy().wait_recv()
        self.load().wait()
        for a in range(2):
            for b in range(2):
                add_into(self.mine.at[a, b], self.core_in.at[a, b])
        for copy in self.wide_copies():
            copy.start()

    def stage_wide(self):
        p, (left, right) = self.place, self.halves()
        if self.gather:
            stay = pltpu.make_async_copy(
                self.mine.at[p.y, p.x], self.middle[0].at[p.y, p.x], self.local.at[2]
            )
            stay.start()
            for copy in self.wide_copies():
                copy.wait_recv()
            stay.wait()
            self.z_start()
            return
        for copy in self.wide_copies():
            copy.wait_recv()
        for a in range(2):
            add_into(self.mine.at[a, p.x, :, left], self.middle[0].at[a])
            add_into(self.mine.at[p.y, a, :, right], self.middle[1].at[a])
        for copy in self.narrow_copies():
            copy.start()

    def stage_narrow(self):
        p, (left, right) = self.place, self.halves()
        for copy in self.narrow_copies():
            copy.wait_recv()
        add_into(self.mine.at[p.y, p.x, :, left], self.middle[2])
        add_into(self.mine.at[p.y, p.x, :, right], self.middle[3])
        self.z_start()

    def z_start(self):
        @pl.when(self.place.outer)
        def _():
            self.pair_copy().start()

    def stage_pair(self):
        @pl.when(self.place.inner)
        def _():
            self.pair_copy().wait_recv()
            for total, addend in zip(self.parts(self.summed()), self.parts(self.z_first)):
                add_into(total, addend)
            self.middle_copy().start()

    def stage_middle(self):
        @pl.when(self.place.inner)
        def _():
            self.middle_copy().wait_recv()
            if self.gather:
                self.lay_out()
            else:
                add_to(self.z_last, self.summed(), self.z_second)
            self.last_copy().start()
            for copy in self.out_copies():
                copy.start()

    def stage_last(self):
        @pl.when(self.place.outer)
        def _():
            self.last_copy().wait_recv()
            for copy in self.out_copies():
                copy.start()

    def stage_end(self):
        remote_out, local_out = self.out_copies()
        remote_out.wait()
        local_out.wait()
        self.core_copy().wait_send()
        for copy in self.wide_copies():
            copy.wait_send()
        if not self.gather:
            for copy in self.narrow_copies():
                copy.wait_send()

        @pl.when(self.place.outer)
        def _():
            self.pair_copy().wait_send()

        @pl.when(self.place.inner)
        def _():
            self.middle_copy().wait_send()
            self.last_copy().wait_send()

    def plan(self):
        piece = 2 * self.rows * self.columns
        if self.gather:
            return [
                (self.stage_core, [("x", 1.5 * piece), ("y", 1.5 * piece)]),
                (self.stage_wide, [("z", 4 * piece)]),
                (self.stage_pair, [("z", 4 * piece)]),
                (self.stage_middle, [("z", 4 * piece)]),
                (self.stage_last, [("core", 4 * piece)]),
                (self.stage_end, []),
            ]
        return [
            (self.stage_core, [("x", piece), ("y", piece)]),
            (self.stage_wide, [("x", piece / 2), ("y", piece / 2)]),
            (self.stage_narrow, [("z1", piece)]),
            (self.stage_pair, [("z2", piece)]),
            (self.stage_middle, [("z3", piece)]),
            (self.stage_last, [("core", piece)]),
            (self.stage_end, []),
        ]

    def opening(self):
        return [("core", 8 * self.rows * self.columns)]


class RowChunk:
    def __init__(self, term, offset, rows, columns):
        self.term, self.offset, self.rows, self.columns = term, offset, rows, columns

    def scratch(self):
        rows, columns, half = self.rows, self.columns, self.columns // 2
        low = jnp.bfloat16
        return [
            pltpu.VMEM((2, 2, rows, columns), low),
            pltpu.VMEM((2, rows, half), low),
            pltpu.VMEM((2, rows, half), low),
            pltpu.VMEM((rows, half), low),
            pltpu.VMEM((rows, half), low),
            pltpu.SemaphoreType.DMA((4,)),
            pltpu.SemaphoreType.DMA((4,)),
            pltpu.SemaphoreType.DMA((2,)),
        ]

    def bind(self, place, source, result, refs):
        self.place, self.source, self.result = place, source, result
        self.mine, self.middle = refs[0], refs[1:5]
        self.sent, self.received, self.local = refs[5:]

    remote = Chunk.remote
    halves = Chunk.halves

    def load(self):
        rows = pl.ds(self.offset, self.rows)
        return pltpu.make_async_copy(self.source.at[:, :, rows, :], self.mine, self.local.at[0])

    def wide_copies(self):
        p, (left, right) = self.place, self.halves()
        return [
            self.remote(0, self.mine.at[:, 1 - p.x, :, left], self.middle[0], "x"),
            self.remote(1, self.mine.at[1 - p.y, :, :, right], self.middle[1], "y"),
        ]

    def narrow_copies(self):
        p, (left, right) = self.place, self.halves()
        return [
            self.remote(2, self.mine.at[1 - p.y, p.x, :, left], self.middle[2], "y"),
            self.remote(3, self.mine.at[p.y, 1 - p.x, :, right], self.middle[3], "x"),
        ]

    def out_copy(self):
        p = self.place
        return pltpu.make_async_copy(
            self.mine.at[p.y, p.x], self.result.at[pl.ds(self.offset, self.rows), :], self.local.at[1]
        )

    def stage_start(self):
        self.load().start()

    def stage_load(self):
        self.load().wait()
        for copy in self.wide_copies():
            copy.start()

    def stage_wide(self):
        p, (left, right) = self.place, self.halves()
        for copy in self.wide_copies():
            copy.wait_recv()
        for a in range(2):
            add_into(self.mine.at[a, p.x, :, left], self.middle[0].at[a])
            add_into(self.mine.at[p.y, a, :, right], self.middle[1].at[a])
        for copy in self.narrow_copies():
            copy.start()

    def stage_narrow(self):
        p, (left, right) = self.place, self.halves()
        for copy in self.narrow_copies():
            copy.wait_recv()
        add_into(self.mine.at[p.y, p.x, :, left], self.middle[2])
        add_into(self.mine.at[p.y, p.x, :, right], self.middle[3])
        self.out_copy().start()

    def stage_end(self):
        self.out_copy().wait()
        for copy in self.wide_copies() + self.narrow_copies():
            copy.wait_send()

    def plan(self):
        piece = 2 * self.rows * self.columns
        return [
            (self.stage_load, [("x", piece), ("y", piece)]),
            (self.stage_wide, [("x", piece / 2), ("y", piece / 2)]),
            (self.stage_narrow, [("core", 0.0)]),
            (self.stage_end, []),
        ]

    def opening(self):
        return [("core", 0.0)]


def stage_order(chunks):
    free, ready, order = {}, [], []

    def send(transfers, now):
        ends = [now]
        for link, size in transfers:
            start = max(now, free.get(link, 0.0))
            free[link] = start + size / LINK_RATE.get(link, LINK_RATE["z"])
            ends.append(free[link] + 2.0)
        return max(ends)

    for number, chunk in enumerate(chunks):
        ready.append((send(chunk.opening(), 0.0), number, 0))
    now = 0.0
    while ready:
        ready.sort()
        when, number, index = ready.pop(0)
        now = max(now, when) + 0.3
        stage, transfers = chunks[number].plan()[index]
        order.append((now, stage))
        if index + 1 < len(chunks[number].plan()):
            ready.append((send(transfers, now), number, index + 1))
    return order


def bind_chunks(chunks, place, sources, results, refs):
    used = 0
    for chunk in chunks:
        count = len(chunk.scratch())
        chunk.bind(place, sources[chunk.term], results[chunk.term], refs[used : used + count])
        used += count


def exchange_kernel(chunks, peers, count, *refs):
    sources, results = refs[:count], refs[count : 2 * count]
    place = Place()
    bind_chunks(chunks, place, sources, results, refs[2 * count :])
    place.greet(peers)
    for chunk in chunks:
        chunk.stage_start()
    for _, stage in stage_order(chunks):
        stage()


def exchange(chunks, terms, shapes, collective_id, name):
    anywhere = pl.BlockSpec(memory_space=pl.ANY)
    return pl.pallas_call(
        functools.partial(exchange_kernel, chunks, ("core", "x", "y", "xy", "pair"), len(terms)),
        in_specs=[anywhere] * len(terms),
        out_specs=[anywhere] * len(terms),
        out_shape=[jax.ShapeDtypeStruct(shape, jnp.bfloat16) for shape in shapes],
        scratch_shapes=[ref for chunk in chunks for ref in chunk.scratch()],
        compiler_params=pltpu.CompilerParams(
            collective_id=collective_id, has_side_effects=True, vmem_limit_bytes=VMEM_BYTES
        ),
        name=name,
    )(*terms)


class Line:
    def __init__(self, place, seg, slab, memory, runs, refs):
        self.place, self.seg, self.slab, self.memory, self.runs = place, seg, slab, memory, runs
        self.sent, self.received, self.core_sent, self.core_received = refs
        self.rows = slab.shape[0] // runs

    def span(self, run):
        return pl.ds(run * self.rows, self.rows)

    def there(self, way, step):
        return self.place.z >= step if way == 0 else self.place.z + step <= 3

    def goes(self, way, step):
        has = self.there(way, step - 1)
        return jnp.logical_and(has, self.place.z <= 2 if way == 0 else self.place.z >= 1)

    def index(self, way, step):
        return self.seg - 2 * step if way == 0 else self.seg + 2 * step

    def hop(self, way, step, run):
        name = self.index(way, step - 1)
        target = self.memory.at[name, self.span(run), :]
        slot = (way * 3 + step - 1) * self.runs + run
        seg, seq = lax.axis_index("seg"), lax.axis_index("seq")
        return pltpu.make_async_remote_copy(
            src_ref=self.slab.at[self.span(run), :] if step == 1 else target,
            dst_ref=target,
            send_sem=self.sent.at[slot],
            recv_sem=self.received.at[slot],
            device_id=(seg + 2 - 4 * way, seq),
            device_id_type=pl.DeviceIdType.MESH,
        )

    def arrival(self, way, step, run):
        target = self.memory.at[self.index(way, step), self.span(run), :]
        slot = (way * 3 + step - 1) * self.runs + run
        return pltpu.make_async_remote_copy(
            src_ref=target,
            dst_ref=target,
            send_sem=self.sent.at[slot],
            recv_sem=self.received.at[slot],
            device_id=self.place.peer["core"],
            device_id_type=pl.DeviceIdType.MESH,
        )

    def share(self, way, step, run):
        name = self.index(way, step)
        target = self.memory.at[name, self.span(run), :]
        slot = (way * 3 + step) * self.runs + run
        return pltpu.make_async_remote_copy(
            src_ref=self.slab.at[self.span(run), :] if step == 0 else target,
            dst_ref=target,
            send_sem=self.core_sent.at[slot],
            recv_sem=self.core_received.at[slot],
            device_id=self.place.peer["core"],
            device_id_type=pl.DeviceIdType.MESH,
        )

    def start(self):
        for run in range(self.runs):
            for way in range(2):

                @pl.when(self.goes(way, 1))
                def _(way=way, run=run):
                    self.hop(way, 1, run).start()

        for run in range(self.runs):
            self.share(0, 0, run).start()

    def advance(self, step, run):
        for way in range(2):

            @pl.when(self.there(way, step))
            def _(way=way):
                self.arrival(way, step, run).wait_recv()

            if step < 3:

                @pl.when(self.goes(way, step + 1))
                def _(way=way):
                    self.hop(way, step + 1, run).start()

            @pl.when(self.there(way, step))
            def _(way=way):
                self.share(way, step, run).start()

    def finish(self):
        for run in range(self.runs):
            self.share(0, 0, run).wait()
            for way in range(2):
                for step in range(1, 4):

                    @pl.when(self.there(way, step))
                    def _(way=way, step=step, run=run):
                        self.share(way, step, run).wait()

                    @pl.when(self.goes(way, step))
                    def _(way=way, step=step, run=run):
                        self.hop(way, step, run).wait_send()


def front_kernel(
    heads,
    x_ref,
    mem_k_ref,
    mem_v_ref,
    w_ref,
    cos_ref,
    sin_ref,
    every_ref,
    memory_ref,
    q_ref,
    k_ref,
    v_ref,
    mix_ref,
    max_ref,
    sum_ref,
    rows,
    slab,
    trade_sent,
    trade_received,
    rows_sent,
    rows_received,
    line_sent,
    line_received,
    core_sent,
    core_received,
    local,
):
    place = Place()
    seg, seq = lax.axis_index("seg"), lax.axis_index("seq")
    width = heads * HEAD_DIM
    count = mem_k_ref.shape[0]
    tokens, depth = x_ref.shape
    across = {"x": seq + 1 - 2 * place.x, "y": seq + 2 - 4 * place.y, "xy": 3 - seq}

    def remote(source, target, sent, received, slot, peer):
        return pltpu.make_async_remote_copy(
            src_ref=source,
            dst_ref=target,
            send_sem=sent.at[slot],
            recv_sem=received.at[slot],
            device_id=place.peer[peer],
            device_id_type=pl.DeviceIdType.MESH,
        )

    def columns(owner, start=0):
        return pl.ds(pl.multiple_of(start + owner * width, HEAD_DIM), width)

    def seat(owner):
        return pl.ds(pl.multiple_of(owner * count, 16), count)

    trades, arrivals = [], []
    for number, peer in enumerate(("x", "y", "xy")):
        for kind, source in enumerate((mem_k_ref, mem_v_ref)):
            lanes = pl.ds(kind * width, width)
            trades.append(
                remote(
                    source.at[:, columns(across[peer])],
                    slab.at[seat(seq), lanes],
                    trade_sent,
                    trade_received,
                    2 * number + kind,
                    peer,
                )
            )

    def trade_arrivals():
        for copy in trades:
            copy.wait_recv()

    keeps = [
        pltpu.make_async_copy(
            source.at[:, columns(seq)],
            slab.at[seat(seq), pl.ds(kind * width, width)],
            local.at[kind],
        )
        for kind, source in enumerate((mem_k_ref, mem_v_ref))
    ]
    half = depth // 2
    left, right = pl.ds(0, half), pl.ds(half, half)
    load = pltpu.make_async_copy(x_ref, rows.at[seq], local.at[2])
    direct = [
        remote(x_ref.at[:, left], rows.at[seq, :, left], rows_sent, rows_received, 0, "x"),
        remote(x_ref.at[:, right], rows.at[seq, :, right], rows_sent, rows_received, 1, "y"),
        remote(x_ref.at[:, right], rows.at[seq, :, right], rows_sent, rows_received, 2, "x"),
        remote(x_ref.at[:, left], rows.at[seq, :, left], rows_sent, rows_received, 3, "y"),
    ]
    onward = [
        remote(
            rows.at[across["x"], :, left], rows.at[across["x"], :, left], rows_sent, rows_received, 4, "y"
        ),
        remote(
            rows.at[across["y"], :, right], rows.at[across["y"], :, right], rows_sent, rows_received, 5, "x"
        ),
    ]
    line = Line(
        place, seg, slab, memory_ref, 2, (line_sent, line_received, core_sent, core_received)
    )
    keep_slab = pltpu.make_async_copy(slab, memory_ref.at[seg], local.at[3])
    keep_rows = pltpu.make_async_copy(rows, every_ref, local.at[4])

    def project_rows(owner):
        block = rows[owner]
        span = pl.ds(pl.multiple_of(owner * tokens, 16), tokens)
        cosine, sine = cos_ref[span, :], sin_ref[span, :]
        scale = SCORE_SCALE / LN2
        queries = product(block, w_ref[:, :width])
        keys = product(block, w_ref[:, width : 2 * width])
        for head in range(heads):
            lanes = slice(head * HEAD_DIM, (head + 1) * HEAD_DIM)
            q_ref[span, lanes] = turn_block(queries[:, lanes], cosine * scale, sine * scale).astype(
                jnp.bfloat16
            )
            k_ref[span, lanes] = turn_block(keys[:, lanes], cosine, sine).astype(jnp.bfloat16)
        v_ref[span, :] = product(block, w_ref[:, 2 * width :]).astype(jnp.bfloat16)

    def own_rows(block):
        def turn(head, carry):
            lanes = pl.ds(pl.multiple_of(head * HEAD_DIM, HEAD_DIM), HEAD_DIM)
            span = pl.ds(block * tokens, tokens)
            pairs = [
                (k_ref[pl.ds(n * tokens, tokens), lanes], v_ref[pl.ds(n * tokens, tokens), lanes])
                for n in range(block + 1)
            ]
            row_max, row_sum, mixed = attend(q_ref[span, lanes], pairs, True, None)
            mix_ref[span, lanes] = mixed
            max_ref[span, lanes] = jnp.broadcast_to(row_max, mixed.shape)
            sum_ref[span, lanes] = jnp.broadcast_to(row_sum, mixed.shape)
            return carry

        lax.fori_loop(0, heads, turn, 0)

    barrier = pltpu.get_barrier_semaphore()

    def hail(device):
        pl.semaphore_signal(barrier, inc=1, device_id=device, device_id_type=pl.DeviceIdType.MESH)

    for peer in ("x", "y", "xy", "core"):
        hail(place.peer[peer])
    below, above = place.z >= 1, place.z <= 2

    @pl.when(below)
    def _():
        hail((seg - 2, seq))

    @pl.when(above)
    def _():
        hail((seg + 2, seq))

    pl.semaphore_wait(barrier, 4 + below.astype(jnp.int32) + above.astype(jnp.int32))

    for copy in keeps + trades:
        copy.start()
    load.start()
    for copy in direct:
        copy.start()
    load.wait()
    project_rows(seq)
    for copy in keeps:
        copy.wait()
    trade_arrivals()
    line.start()
    keep_slab.start()
    direct[0].wait_recv()
    direct[1].wait_recv()
    for copy in onward:
        copy.start()
    line.advance(1, 0)
    direct[2].wait_recv()
    direct[3].wait_recv()
    project_rows(across["x"])
    line.advance(1, 1)
    project_rows(across["y"])
    for copy in onward:
        copy.wait_recv()
    project_rows(3 - seq)
    keep_rows.start()
    line.advance(2, 0)
    own_rows(0)
    own_rows(1)
    line.advance(2, 1)
    own_rows(2)
    own_rows(3)
    line.advance(3, 0)
    line.advance(3, 1)
    keep_slab.wait()
    keep_rows.wait()
    for copy in trades + direct + onward:
        copy.wait_send()
    line.finish()


def front(first_low, mem_keys, mem_values, w_heads, cosine, sine, seg_size, seq_size, collective_id):
    tokens, depth = first_low.shape
    length = tokens * seq_size
    width = w_heads.shape[1] // 3
    count = mem_keys.shape[0]
    anywhere = pl.BlockSpec(memory_space=pl.ANY)
    inside = pl.BlockSpec(memory_space=pltpu.VMEM)
    low = jnp.bfloat16
    shape = jax.ShapeDtypeStruct
    dma = pltpu.SemaphoreType.DMA
    return pl.pallas_call(
        functools.partial(front_kernel, width // HEAD_DIM),
        in_specs=[anywhere] * 3 + [inside] * 3,
        out_specs=[anywhere] * 2 + [inside] * 6,
        out_shape=[
            shape((seq_size, tokens, depth), low),
            shape((seg_size, count * seq_size, 2 * width), low),
        ]
        + [shape((length, width), low)] * 3
        + [shape((length, width), jnp.float32)] * 3,
        scratch_shapes=[
            pltpu.VMEM((seq_size, tokens, depth), low),
            pltpu.VMEM((count * seq_size, 2 * width), low),
            dma((6,)),
            dma((6,)),
            dma((6,)),
            dma((6,)),
            dma((12,)),
            dma((12,)),
            dma((16,)),
            dma((16,)),
            dma((5,)),
        ],
        compiler_params=pltpu.CompilerParams(
            collective_id=collective_id, has_side_effects=True, vmem_limit_bytes=VMEM_BYTES
        ),
        name="front",
    )(first_low, mem_keys, mem_values, w_heads, cosine, sine)


def norm_input_grad(values, inverse, norm_gain, upstream):
    weighted = upstream * norm_gain
    inner_mean = jnp.mean(weighted * values, axis=-1, keepdims=True)
    return inverse * weighted - inverse * inverse * inverse * values * inner_mean


def head_plan(
    seg_size,
    seq_size,
    layer_input,
    output_grad,
    norm1_gain,
    norm2_gain,
    w_qkv,
    w_out,
    w_gate,
    w_up,
    w_down,
    mem_keys,
    mem_values,
    memory_flags,
    sources,
):
    seg_index = lax.axis_index("seg")
    seq_index = lax.axis_index("seq")
    tokens = layer_input.shape[1]
    length = tokens * seq_size
    width = D // seq_size
    flag = lax.dynamic_index_in_dim(memory_flags, seg_index, 0, keepdims=True)
    listed = lax.dynamic_index_in_dim(sources, seg_index, 0, keepdims=False)
    chosen = jnp.concatenate([jnp.reshape(seg_index, (1,)), listed, flag]).astype(jnp.int32)

    inputs = layer_input[0].astype(jnp.float32)
    first_norm, first_inverse = norm_forward(inputs, norm1_gain)
    first_low = first_norm.astype(jnp.bfloat16)
    w_heads = lax.dynamic_index_in_dim(
        w_qkv.reshape(D, 3, seq_size, width), seq_index, 2, keepdims=False
    ).reshape(D, 3 * width)
    cosine, sine = turn_tables(lax.iota(jnp.int32, length).astype(jnp.float32))
    cosine, sine = cosine[:, 0, :], sine[:, 0, :]
    first_half = lax.broadcasted_iota(jnp.int32, sine.shape, 1) < HEAD_DIM // 2
    sine = jnp.where(first_half, -sine, sine)
    every_low, memory, queries, keys, values, mixed, row_max, row_sum = front(
        first_low, mem_keys[0], mem_values[0], w_heads, cosine, sine, seg_size, seq_size, 3
    )
    every_low = every_low.reshape(length, D)
    heads_low, heads_out, log_totals = memory_forward(
        chosen, queries, mixed, row_max, row_sum, memory
    )
    attended_low = lax.all_to_all(heads_low, "seq", 0, 1, tiled=True)

    residual = inputs + product(attended_low, w_out)
    second_norm, second_inverse = norm_forward(residual, norm2_gain)
    second_low = second_norm.astype(jnp.bfloat16)
    gate_values = product(second_low, w_gate)
    up_values = product(second_low, w_up)
    sigmoid_gate = jax.nn.sigmoid(gate_values)
    activated = gate_values * sigmoid_gate
    hidden_low = (activated * up_values).astype(jnp.bfloat16)
    output = (residual + product(hidden_low, w_down)).astype(jnp.bfloat16)
    upstream = output_grad[0]
    low = jnp.bfloat16
    term_down = product_tn(hidden_low, upstream).astype(low)
    grad_hidden = product_nt(upstream, w_down)
    grad_gate_low = (
        grad_hidden * up_values * sigmoid_gate * (1.0 + gate_values * (1.0 - sigmoid_gate))
    ).astype(low)
    grad_up_low = (grad_hidden * activated).astype(low)
    term_gate = product_tn(second_low, grad_gate_low).astype(low)
    term_up = product_tn(second_low, grad_up_low).astype(low)
    grad_second = product_nt(grad_gate_low, w_gate) + product_nt(grad_up_low, w_up)
    grad_residual = norm_input_grad(residual, second_inverse, norm2_gain, grad_second)
    grad_residual = grad_residual + upstream.astype(jnp.float32)
    residual_low = grad_residual.astype(low)
    term_out = product_tn(attended_low, residual_low).astype(low)
    grad_attended = product_nt(residual_low, w_out).astype(low)
    grad_heads = lax.all_to_all(grad_attended, "seq", 1, 0, tiled=True)

    start, delta = memory_backward(chosen, queries, grad_heads, heads_out, log_totals, memory)
    grad_projected = own_backward(
        queries, keys, values, grad_heads, log_totals, delta, start, cosine, sine
    )
    terms = [term_down, term_gate, term_up, term_out]
    pieces = [(term.shape[0] // (2 * seq_size), term.shape[1]) for term in terms]
    chunks = []
    for index, (rows, columns) in enumerate(pieces):
        parts = 2 if rows % 32 == 0 and index < 3 else 1
        chunks += [Chunk(index, n * rows // parts, rows // parts, columns) for n in range(parts)]
    sums = exchange(
        chunks,
        [term.reshape((2, 2, 2) + piece) for term, piece in zip(terms, pieces)],
        [(2,) + piece for piece in pieces],
        1,
        "sum_terms",
    )
    grad_down, grad_gate, grad_up, grad_out = [
        total.reshape(2 * piece[0], piece[1]).astype(jnp.float32) for total, piece in zip(sums, pieces)
    ]

    part_first = product_nt(grad_projected, w_heads).astype(low)
    part_qkv = product_tn(every_low, grad_projected).astype(low)
    rows = D // (2 * seq_size)
    qkv_rows, first_rows = exchange(
        [Chunk(0, n * rows // 2, rows // 2, 3 * width, True) for n in range(2)]
        + [RowChunk(1, n * tokens // 4, tokens // 4, D) for n in range(4)],
        [part_qkv.reshape(2, 2, 2, rows, 3 * width), part_first.reshape(2, 2, tokens, D)],
        [(2, rows, 3 * D), (tokens, D)],
        2,
        "sum_first",
    )
    grad_qkv = qkv_rows.reshape(2 * rows, 3 * D).astype(jnp.float32)
    grad_inputs = norm_input_grad(
        inputs, first_inverse, norm1_gain, first_rows.astype(jnp.float32)
    )
    input_grad = (grad_inputs + grad_residual)[None]

    def row_block(whole):
        return lax.dynamic_slice_in_dim(whole, seq_index * width, width, 0)

    def gain_rows(weights, grads, gain):
        dots = [
            jnp.sum(row_block(weight).astype(jnp.float32) * grad, axis=1)
            for weight, grad in zip(weights, grads)
        ]
        return sum(dots[1:], dots[0]) / row_block(gain)

    grad_norm1 = gain_rows([w_qkv], [grad_qkv], norm1_gain)
    grad_norm2 = gain_rows([w_gate, w_up], [grad_gate, grad_up], norm2_gain)
    return (
        output[None],
        input_grad,
        grad_norm1,
        grad_norm2,
        grad_qkv,
        grad_out,
        grad_gate,
        grad_up,
        grad_down,
    )


def solution(mesh):
    seq_size = mesh.shape["seq"]
    heads_fit = seq_size == 4 and mesh.shape["seg"] == 8
    plan = functools.partial(head_plan, mesh.shape["seg"], seq_size) if heads_fit else general_plan
    placed = (
        P("seg", "seq", None),
        P("seg", "seq", None),
        P(),
        P(),
        P(),
        P(),
        P(),
        P(),
        P(),
        P("seg", "seq", None),
        P("seg", "seq", None),
        P(),
        P(),
    )
    return jax.shard_map(
        plan,
        mesh=mesh,
        in_specs=placed,
        out_specs=(
            P("seg", "seq", None),
            P("seg", "seq", None),
            P("seq"),
            P("seq"),
            P("seq", None),
            P("seq", None),
            P("seq", None),
            P("seq", None),
            P("seq", None),
        ),
        check_vma=False,
    )
```

profile of v0, /device:TPU:0, one launch (start us, length us, event | category | flops | bytes accessed | tf_op | source)
XLA Modules:
  0.0 514.1 jit_solution(16719996861320485095)
XLA Ops:
  5.1 8.6 %copy.27 = bf16[1024,3072]{0,1:T(8,128)(2,1)} copy(bf16[1024,3072]{1,0:T(8,128)(2,1)} %param.17) | data formatting | bytes 12582912 | tf_op args[4]
  13.7 2.7 constant_dynamic-slice_fusion
  16.4 2.6 copy.28.w_ref
  19.4 4.9 negate_select_fusion
  26.8 94.5 %front.1 = (bf16[4,512,1024]{2,1,0:T(8,128)(2,1)}, bf16[8,1024,512]{2,1,0:T(8,128)(2,1)}, bf16[2048,256]{1,0:T(8,128)(2,1)}, bf16[2048,256]{1,0:T(8,128)(2,1)}, ...) custom-call(bf16[512,1024]{1,0:T(8,128)(2,1)} %fusion.3.x_ref, ...), custom_call_target="tpu_custom_call" | custom-call | tf_op jit(solution)/shard_map/front/pallas_call | solution.py:1274
  121.4 10.5 %memory_forward.1 = (bf16[2048,256]{1,0:T(8,128)(2,1)}, f32[2048,256]{1,0:T(8,128)}, f32[2048,256]{1,0:T(8,128)}) custom-call(s32[5]{0:T(128)} %pad_add_fusion.chosen, bf16[2048,256]{1,0:T(8,128)(2,1)} %get-tuple-element.28.q_ref, f32[2048,256]{1,0:T(8,128)} %get-tuple-element.29.mix_ref, f32[2048,256]{1,0:T(8,128)} %get-tuple-element.30.max_ref, ...), custom_call_target="tpu_custom_call" | custom-call | flops 17179869184 | bytes 18874368 | tf_op jit(solution)/shard_map/memory_forward/pallas_call | solution.py:391
  131.8 2.3 copy.29
  134.1 4.4 all-to-all-start
  138.6 9.5 %all-to-all-done = bf16[4,512,256]{1,2,0:T(8,128)(2,1)} async-done(((bf16[4,512,256]{1,2,0:T(8,128)(2,1)}), bf16[4,512,256]{1,2,0:T(8,128)(2,1)}, u32[]{:S(2)}, u32[]{:S(2)}) %all-to-all-start) | async-done | bytes 1048608 | tf_op jit(solution)/shard_map/all_to_all | solution.py:1353
  148.0 2.6 multiply_reduce_fusion.4
  150.9 8.5 %fusion.17 = f32[512,2816]{1,0:T(8,128)} fusion(bf16[512,1024]{1,0:T(8,128)(2,1)S(1)} %multiply_convert_fusion.3, bf16[1024,2816]{1,0:T(8,128)(2,1)} %param.20), kind=kOutput, calls=%fused_computation.66 | convolution fusion | flops 2952790016 | bytes 12582912 | tf_op jit(solution)/shard_map/dot_general | solution.py:22
  159.4 5.0 fusion.16
  164.5 11.3 %multiply_convert_fusion = (bf16[512,2816]{1,0:T(8,128)(2,1)S(1)}, bf16[512,2816]{1,0:T(8,128)(2,1)}, bf16[512,2816]{1,0:T(8,128)(2,1)}) fusion(f32[512,2816]{1,0:T(8,128)} %fusion.16, f32[512,2816]{1,0:T(8,128)} %fusion.17, bf16[2816,1024]{1,0:T(8,128)(2,1)} %param.21, bf16[1,512,1024]{2,1,0:T(8,128)(2,1)S(1)} %copy-done.12), kind=kOutput, calls=%fused_computation | convolution fusion | flops 2974416896 | bytes 27000832 | tf_op jit(solution)/shard_map/dot_general | solution.py:26
  175.7 5.0 fusion.18
  180.7 5.4 %multiply_reduce_fusion.3 = (f32[512]{0:T(512)S(1)}, f32[512,1024]{1,0:T(8,128)S(1)}) fusion(f32[512,1024]{1,0:T(8,128)S(1)} %get-tuple-element.63, f32[1024]{0:T(1024)S(1)} %copy-done.19, f32[512,1024]{1,0:T(8,128)S(1)} %fusion.18, bf16[512,2816]{1,0:T(8,128)(2,1)S(1)} %get-tuple-element.53, bf16[1024,2816]{1,0:T(8,128)(2,1)} %param.20), kind=kOutput, calls=%fused_computation.27 | convolution fusion | flops 2954886656 | bytes 14948352 | tf_op jit(solution)/shard_map/dot_general | solution.py:26
  186.7 4.6 convolution_convert_fusion.4
  192.6 5.2 %convolution_convert_fusion = bf16[1024,2816]{1,0:T(8,128)(2,1)} fusion(bf16[512,1024]{1,0:T(8,128)(2,1)S(1)} %multiply_convert_fusion.3, bf16[512,2816]{1,0:T(8,128)(2,1)S(1)} %get-tuple-element.53), kind=kOutput, calls=%fused_computation.5 | convolution fusion | flops 2955673600 | bytes 9699328 | tf_op jit(solution)/shard_map/dot_general | solution.py:32
  197.9 5.1 %convolution_convert_fusion.1 = bf16[1024,2816]{1,0:T(8,128)(2,1)} fusion(bf16[512,1024]{1,0:T(8,128)(2,1)S(1)} %multiply_convert_fusion.3, bf16[512,2816]{1,0:T(8,128)(2,1)S(1)} %copy-done.23), kind=kOutput, calls=%fused_computation.6 | convolution fusion | flops 2955673600 | bytes 9699328 | tf_op jit(solution)/shard_map/dot_general | solution.py:32
  204.1 4.2 all-to-all-start.1
  208.3 6.9 %convolution_convert_fusion.2 = bf16[2816,1024]{1,0:T(8,128)(2,1)} fusion(bf16[512,2816]{1,0:T(8,128)(2,1)} %get-tuple-element.55, bf16[1,512,1024]{2,1,0:T(8,128)(2,1)S(1)} %copy-done.13), kind=kOutput, calls=%fused_computation.7 | convolution fusion | flops 2955673600 | bytes 9699328 | tf_op jit(solution)/shard_map/dot_general | solution.py:32
  215.2 145.8 %sum_terms.1 = (bf16[2,352,1024]{2,1,0:T(8,128)(2,1)}, bf16[2,128,2816]{2,1,0:T(8,128)(2,1)}, bf16[2,128,2816]{2,1,0:T(8,128)(2,1)}, bf16[2,128,1024]{2,1,0:T(8,128)(2,1)}) custom-call(bf16[2,2,2,352,1024]{4,3,2,1,0:T(8,128)(2,1)} %bitcast.89, bf16[2,2,2,128,2816]{4,3,2,1,0:T(8,128)(2,1)} %bitcast.88, bf16[2,2,2,128,2816]{4,3,2,1,0:T(8,128)(2,1)} %bitcast.87, ...), custom_call_target="tpu_custom_call" | custom-call | tf_op jit(solution)/shard_map/sum_terms/pallas_call | solution.py:958
  361.1 2.3 bitcast_convert_fusion.4
  363.4 3.5 bitcast_convert_fusion.1
  366.8 4.9 multiply_reduce_fusion.1
  372.4 4.1 fusion.9
  376.5 10.2 %memory_backward.1 = (f32[2048,256]{1,0:T(8,128)}, f32[2048,256]{1,0:T(8,128)}) custom-call(s32[5]{0:T(128)} %pad_add_fusion.chosen, bf16[2048,256]{1,0:T(8,128)(2,1)} %get-tuple-element.28.q_ref, bf16[2048,256]{1,0:T(8,128)(2,1)} %bitcast.14.g_ref, f32[2048,256]{1,0:T(8,128)} %get-tuple-element.38.out_ref, f32[2048,256]{1,0:T(8,128)} %get-tuple-element.37.log_ref, ...), custom_call_target="tpu_custom_call" | custom-call | flops 25769803776 | bytes 18874368 | tf_op jit(solution)/shard_map/memory_backward/pallas_call | solution.py:442
  386.7 25.5 %own_backward.1 = bf16[2048,768]{1,0:T(8,128)(2,1)} custom-call(bf16[2048,256]{1,0:T(8,128)(2,1)} %get-tuple-element.28.q_ref, bf16[2048,256]{1,0:T(8,128)(2,1)} %get-tuple-element.35.k_ref, bf16[2048,256]{1,0:T(8,128)(2,1)} %get-tuple-element.36.v_ref, bf16[2048,256]{1,0:T(8,128)(2,1)} %bitcast.14.g_ref, f32[2048,256]{1,0:T(8,128)} %get-tuple-element.37.log_ref, ...), custom_call_target="tpu_custom_call" | custom-call | flops 10737418240 | bytes 18874368 | tf_op jit(solution)/shard_map/own_backward/pallas_call | solution.py:511
  412.2 7.1 %convolution_convert_fusion.3 = bf16[2048,1024]{1,0:T(8,128)(2,1)} fusion(bf16[2048,768]{1,0:T(8,128)(2,1)} %own_backward.1, bf16[1024,768]{0,1:T(8,128)(2,1)S(1)} %bitcast.86), kind=kOutput, calls=%fused_computation.13 | convolution fusion | flops 3223322624 | bytes 8912896 | tf_op jit(solution)/shard_map/dot_general | solution.py:26
  419.3 4.6 convolution_convert_fusion.5
  423.9 81.7 %sum_first.1 = (bf16[2,128,3072]{2,1,0:T(8,128)(2,1)}, bf16[512,1024]{1,0:T(8,128)(2,1)}) custom-call(bf16[2,2,2,128,768]{4,3,2,1,0:T(8,128)(2,1)} %bitcast.92, bf16[2,2,512,1024]{3,2,1,0:T(8,128)(2,1)} %bitcast.90), custom_call_target="tpu_custom_call" | custom-call | tf_op jit(solution)/shard_map/sum_first/pallas_call | solution.py:958
  507.5 3.6 multiply_reduce_fusion
  511.7 1.9 fusion.7
  (79 shorter events, 13.6 us)
Async XLA Ops:
  0.6 147.4 %copy-start = (bf16[1024,1024]{1,0:T(8,128)(2,1)S(1)}, bf16[1024,1024]{1,0:T(8,128)(2,1)}, u32[]{:S(2)}) copy-start(bf16[1024,1024]{1,0:T(8,128)(2,1)} %param.18) | copy-start | bytes 6291460
  5.1 19.2 %copy-start.16 = (f32[512]{0:T(512)}, f32[512]{0:T(512)S(1)}, u32[]{:S(2)}) copy-start(f32[512]{0:T(512)S(1)} %get-tuple-element.59) | copy-start | bytes 6148
  19.0 5.3 %copy-start.2 = (bf16[1,512,1024]{2,1,0:T(8,128)(2,1)S(1)}, bf16[1,512,1024]{2,1,0:T(8,128)(2,1)}, u32[]{:S(2)}) copy-start(bf16[1,512,1024]{2,1,0:T(8,128)(2,1)} %param.13) | copy-start | bytes 3145732
  19.0 5.3 %copy-start.14 = (f32[1024]{0:T(1024)S(1)}, f32[1024]{0:T(1024)}, u32[]{:S(2)}) copy-start(f32[1024]{0:T(1024)} %param.15) | copy-start | bytes 12292
  134.1 13.9 %all-to-all-start = ((bf16[4,512,256]{1,2,0:T(8,128)(2,1)}), bf16[4,512,256]{1,2,0:T(8,128)(2,1)}, u32[]{:S(2)}, u32[]{:S(2)}) async-start(bf16[4,512,256]{1,2,0:T(8,128)(2,1)} %copy.29), calls=%async_computation | async-start | bytes 2097152 | tf_op jit(solution)/shard_map/all_to_all | solution.py:1353
  148.0 2.6 copy-start.19
  150.6 35.5 %copy-start.3 = (f32[512,1024]{1,0:T(8,128)}, f32[512,1024]{1,0:T(8,128)S(1)}, u32[]{:S(2)}) copy-start(f32[512,1024]{1,0:T(8,128)S(1)} %get-tuple-element.63) | copy-start | bytes 6291460
  150.7 8.8 %slice-start = ((s8[5767168]{0:T(1024)(128)(4,1)}), s8[4194304]{0:T(1024)(128)(4,1)S(1)}, s32[]{:S(2)}) async-start(s8[5767168]{0:T(1024)(128)(4,1)} %bitcast.97), calls=%async_computation.2 | async-start | bytes 8388608
  150.9 8.5 %slice-start.1 = ((s8[5767168]{0:T(1024)(128)(4,1)}), s8[1572864]{0:T(1024)(128)(4,1)S(1)}, s32[]{:S(2)}) async-start(s8[5767168]{0:T(1024)(128)(4,1)} %bitcast.97), calls=%async_computation.3 | async-start | bytes 3145728
  159.4 5.1 copy-start.12
  186.7 4.6 copy-start.5
  192.6 5.3 %copy-start.23 = (bf16[512,2816]{1,0:T(8,128)(2,1)S(1)}, bf16[512,2816]{1,0:T(8,128)(2,1)}, u32[]{:S(2)}) copy-start(bf16[512,2816]{1,0:T(8,128)(2,1)} %get-tuple-element.54) | copy-start | bytes 8650756
  203.0 5.3 %copy-start.13 = (bf16[1,512,1024]{2,1,0:T(8,128)(2,1)S(1)}, bf16[1,512,1024]{2,1,0:T(8,128)(2,1)}, u32[]{:S(2)}) copy-start(bf16[1,512,1024]{2,1,0:T(8,128)(2,1)} %param.14) | copy-start | bytes 3145732
  204.1 172.4 %all-to-all-start.1 = ((bf16[512,4,256]{2,0,1:T(8,128)(2,1)}), bf16[512,4,256]{2,0,1:T(8,128)(2,1)}, u32[]{:S(2)}, u32[]{:S(2)}) async-start(bf16[512,4,256]{2,0,1:T(8,128)(2,1)} %bitcast.83), calls=%async_computation.1 | async-start | bytes 2097152 | tf_op jit(solution)/shard_map/all_to_all | solution.py:1380
  361.1 5.8 %copy-start.10 = (bf16[2,128,2816]{2,1,0:T(8,128)(2,1)S(1)}, bf16[2,128,2816]{2,1,0:T(8,128)(2,1)}, u32[]{:S(2)}) copy-start(bf16[2,128,2816]{2,1,0:T(8,128)(2,1)} %get-tuple-element.43) | copy-start | bytes 4325380
  361.1 5.7 %copy-start.11 = (bf16[2,128,2816]{2,1,0:T(8,128)(2,1)S(1)}, bf16[2,128,2816]{2,1,0:T(8,128)(2,1)}, u32[]{:S(2)}) copy-start(bf16[2,128,2816]{2,1,0:T(8,128)(2,1)} %get-tuple-element.44) | copy-start | bytes 4325380
  363.4 9.0 %slice-start.2 = ((s8[5767168]{0:T(1024)(128)(4,1)}), s8[4194304]{0:T(1024)(128)(4,1)S(1)}, s32[]{:S(2)}) async-start(s8[5767168]{0:T(1024)(128)(4,1)} %bitcast.99), calls=%async_computation.4 | async-start | bytes 8388608
  366.8 5.5 %copy-start.4 = (f32[512,1024]{1,0:T(8,128)S(1)}, f32[512,1024]{1,0:T(8,128)}, u32[]{:S(2)}) copy-start(f32[512,1024]{1,0:T(8,128)} %copy-done.3) | copy-start | bytes 6291460
  366.8 5.5 %slice-start.3 = ((s8[5767168]{0:T(1024)(128)(4,1)}), s8[1572864]{0:T(1024)(128)(4,1)S(1)}, s32[]{:S(2)}) async-start(s8[5767168]{0:T(1024)(128)(4,1)} %bitcast.99), calls=%async_computation.5 | async-start | bytes 3145728
  366.8 5.5 %copy-start.22 = (bf16[512,2816]{1,0:T(8,128)(2,1)S(1)}, bf16[512,2816]{1,0:T(8,128)(2,1)}, u32[]{:S(2)}) copy-start(bf16[512,2816]{1,0:T(8,128)(2,1)} %get-tuple-element.55) | copy-start | bytes 8650756
  386.7 25.5 %copy-start.7 = (bf16[1024,3,1,256]{0,3,2,1:T(8,128)(2,1)S(1)}, bf16[1024,3,1,256]{0,3,2,1:T(8,128)(2,1)}, u32[]{:S(2)}) copy-start(bf16[1024,3,1,256]{0,3,2,1:T(8,128)(2,1)} %constant_dynamic-slice_fusion) | copy-start | bytes 4718596
  412.2 7.1 %copy-start.20 = (bf16[4,512,1024]{2,1,0:T(8,128)(2,1)S(1)}, bf16[4,512,1024]{2,1,0:T(8,128)(2,1)}, u32[]{:S(2)}) copy-start(bf16[4,512,1024]{2,1,0:T(8,128)(2,1)} %get-tuple-element.34) | copy-start | bytes 12582916
  412.2 7.1 %copy-start.21 = (bf16[2048,768]{1,0:T(8,128)(2,1)S(1)}, bf16[2048,768]{1,0:T(8,128)(2,1)}, u32[]{:S(2)}) copy-start(bf16[2048,768]{1,0:T(8,128)(2,1)} %own_backward.1) | copy-start | bytes 9437188
  423.9 81.7 %copy-start.15 = (f32[1024]{0:T(1024)S(1)}, f32[1024]{0:T(1024)}, u32[]{:S(2)}) copy-start(f32[1024]{0:T(1024)} %param.15) | copy-start | bytes 12292
  505.6 1.8 copy-start.9
  507.4 4.3 copy-start.6
  507.4 4.3 copy-start.8
  507.4 4.3 copy-start.17
  507.4 4.3 copy-start.18
  511.7 2.0 copy-start.1
where the time goes:
time: 523 us; the launch traced here: 514 us
  Pallas kernels  368 us (70%)
  matrix products  76.8 us (15%)
  other arithmetic  29.9 us (6%)
  local copies, waits for them, and re-layouts  19.6 us (4%)
  waiting for transfers between devices  9.47 us (2%)
  starting transfers between devices  8.66 us (2%)
    pallas_call x2, Pallas kernels, exchange(): pl.pallas_call(functools.partial(exchange_kernel, chunks, ('core', 'x', '...  228 us
    pallas_call x1, Pallas kernels, front(): pl.pallas_call(functools.partial(front_kernel, width // HEAD_DIM), in_spe...  94.5 us
    dot_general x5, matrix products, product_nt(): lax.dot_general(former, latter, (((1,), (1,)), ((), ())), preferred_eleme...  30.1 us
    dot_general x5, matrix products, product_tn(): lax.dot_general(former, latter, (((0,), (0,)), ((), ())), preferred_eleme...  26.5 us
    pallas_call x1, Pallas kernels, own_backward(): pl.pallas_call(functools.partial(own_backward_kernel, rows, heads), grid=...  25.5 us
    dot_general x4, matrix products, product(): return jnp.dot(former, latter, preferred_element_type=jnp.float32)  20.2 us
    pallas_call x1, Pallas kernels, memory_forward(): pl.pallas_call(functools.partial(memory_forward_kernel, count), grid_spec...  10.5 us
  transfers between devices with their start and end apart: 2, of which 1 were waited for; matrix products, arithmetic and copies ran while one was open for 4% of the time, Pallas kernels for 28%

commit v1 on v0

--- a/solution.py
+++ b/solution.py
@@ -306,6 +306,7 @@
 
 
 VMEM_BYTES = 60 * 1024 * 1024
+VMEM_MOST = 67043328
 LN2 = math.log(2.0)
 SCORE_SCALE = HEAD_DIM ** (-0.5)
 
@@ -364,14 +365,25 @@
 
 def memory_forward_kernel(count, chosen, q_ref, mix_ref, max_ref, sum_ref, *rest):
     blocks = rest[: 2 * count]
-    low_ref, out_ref, log_ref = rest[2 * count :]
+    low_ref, copy_ref, log_ref = rest[2 * count :]
+    head = pl.program_id(0)
     carried = (max_ref[:, :1], sum_ref[:, :1], mix_ref[...])
 
     def finish(row_max, row_sum, mixed):
-        out = mixed * (1.0 / row_sum)
-        out_ref[...] = out
-        low_ref[...] = out.astype(jnp.bfloat16)
+        low_ref[...] = (mixed * (1.0 / row_sum)).astype(jnp.bfloat16)
         log_ref[...] = jnp.broadcast_to(row_max + jnp.log2(row_sum), log_ref.shape)
+
+    @pl.when(pl.program_id(1) == 0)
+    def _():
+        rows = copy_ref.shape[1]
+        width = copy_ref.shape[2] // 4
+        for n in range(count):
+            for run in range(2):
+                for kind in range(2):
+                    start = pl.multiple_of((2 * run + kind) * width + head * HEAD_DIM, HEAD_DIM)
+                    copy_ref[n, :, pl.ds(start, HEAD_DIM)] = blocks[2 * n + kind][
+                        0, run * rows : (run + 1) * rows, :
+                    ]
 
     @pl.when(chosen[count] > 0)
     def _():
@@ -394,11 +406,15 @@
             num_scalar_prefetch=1,
             grid=(heads, length // rows),
             in_specs=[block] * 4 + memory_specs(heads, memory.shape[1], count),
-            out_specs=[block] * 3,
+            out_specs=[
+                block,
+                pl.BlockSpec((count, memory.shape[1] // 2, 4 * width), lambda h, i, chosen: (0, 0, 0)),
+                block,
+            ],
         ),
         out_shape=[
             jax.ShapeDtypeStruct((length, width), jnp.bfloat16),
-            jax.ShapeDtypeStruct((length, width), jnp.float32),
+            jax.ShapeDtypeStruct((count, memory.shape[1] // 2, 4 * width), jnp.bfloat16),
             jax.ShapeDtypeStruct((length, width), jnp.float32),
         ],
         compiler_params=pltpu.CompilerParams(vmem_limit_bytes=VMEM_BYTES),
@@ -409,125 +425,11 @@
     )(chosen, queries, mixed, row_max, row_sum, *[memory] * (2 * count))
 
 
-def memory_backward_kernel(count, tile, chosen, q_ref, g_ref, out_ref, log_ref, *rest):
-    blocks = rest[: 2 * count]
-    dq_ref, delta_ref = rest[2 * count :]
-    query, upstream = q_ref[...], g_ref[...]
-    delta = jnp.sum(upstream.astype(jnp.float32) * out_ref[...], axis=1, keepdims=True)
-    delta_ref[...] = jnp.broadcast_to(delta, delta_ref.shape)
-    log_total = log_ref[:, :1]
-
-    @pl.when(chosen[count] > 0)
-    def _():
-        total = jnp.zeros(dq_ref.shape, jnp.float32)
-        for n in range(count):
-            for start in range(0, blocks[0].shape[1], tile):
-                keys = blocks[2 * n][0, start : start + tile, :]
-                values = blocks[2 * n + 1][0, start : start + tile, :]
-                probs = jnp.exp2(product_nt(query, keys) - log_total)
-                dscores = probs * (product_nt(upstream, values) - delta)
-                total = total + product(dscores.astype(jnp.bfloat16), keys)
-        dq_ref[...] = total
-
-    @pl.when(chosen[count] <= 0)
-    def _():
-        dq_ref[...] = jnp.zeros(dq_ref.shape, jnp.float32)
-
-
-def memory_backward(chosen, queries, upstream, out, log_totals, memory, rows=512, tile=512):
-    length, width = queries.shape
-    heads, count = width // HEAD_DIM, chosen.shape[0] - 1
-    block = pl.BlockSpec((rows, HEAD_DIM), lambda h, i, chosen: (i, h))
-    pairs = heads * length * count * memory.shape[1]
-    return pl.pallas_call(
-        functools.partial(memory_backward_kernel, count, math.gcd(tile, memory.shape[1])),
-        grid_spec=pltpu.PrefetchScalarGridSpec(
-            num_scalar_prefetch=1,
-            grid=(heads, length // rows),
-            in_specs=[block] * 4 + memory_specs(heads, memory.shape[1], count),
-            out_specs=[block] * 2,
-        ),
-        out_shape=[jax.ShapeDtypeStruct((length, width), jnp.float32)] * 2,
-        compiler_params=pltpu.CompilerParams(vmem_limit_bytes=VMEM_BYTES),
-        cost_estimate=pl.CostEstimate(
-            flops=12 * pairs * HEAD_DIM, transcendentals=pairs, bytes_accessed=36 * length * width
-        ),
-        name="memory_backward",
-    )(chosen, queries, upstream, out, log_totals, *[memory] * (2 * count))
-
-
-def own_backward_kernel(
-    rows, heads, q_ref, k_ref, v_ref, g_ref, log_ref, delta_ref, start_ref, cos_ref, sin_ref, d_ref, dk, dv
-):
-    head, block = pl.program_id(0), pl.program_id(1)
-
-    def lanes(part):
-        return pl.ds(pl.multiple_of((part * heads + head) * HEAD_DIM, HEAD_DIM), HEAD_DIM)
-
-    @pl.when(block == 0)
-    def _():
-        dk[...] = jnp.zeros_like(dk)
-        dv[...] = jnp.zeros_like(dv)
-
-    query, upstream = q_ref[...], g_ref[...]
-    log_total, delta = log_ref[:, :1], delta_ref[:, :1]
-
-    def turn(other, total, diagonal):
-        span = pl.ds(pl.multiple_of(other * rows, rows), rows)
-        keys = k_ref[span, :]
-        scores = product_nt(query, keys)
-        if diagonal:
-            scores = causal(scores)
-        probs = jnp.exp2(scores - log_total)
-        dscores = (probs * (product_nt(upstream, v_ref[span, :]) - delta)).astype(jnp.bfloat16)
-        dv[span, :] += product_tn(probs.astype(jnp.bfloat16), upstream)
-        dk[span, :] += product_tn(dscores, query)
-        return total + product(dscores, keys)
-
-    total = turn(block, start_ref[...], True)
-    total = lax.fori_loop(0, block, lambda other, total: turn(other, total, False), total)
-    mine = pl.ds(pl.multiple_of(block * rows, rows), rows)
-    d_ref[mine, lanes(0)] = turn_block(
-        total * SCORE_SCALE, cos_ref[mine, :], -sin_ref[mine, :]
-    ).astype(jnp.bfloat16)
-
-    @pl.when(block == pl.num_programs(1) - 1)
-    def _():
-        d_ref[:, lanes(1)] = turn_block(dk[...] * LN2, cos_ref[...], -sin_ref[...]).astype(
-            jnp.bfloat16
-        )
-        d_ref[:, lanes(2)] = dv[...].astype(jnp.bfloat16)
-
-
-def own_backward(
-    queries, keys, values, upstream, log_totals, delta, start, cosine, sine, rows=512
-):
-    length, width = queries.shape
-    block = pl.BlockSpec((rows, HEAD_DIM), lambda h, i: (i, h))
-    whole = pl.BlockSpec((length, HEAD_DIM), lambda h, i: (0, h))
-    table = pl.BlockSpec((length, HEAD_DIM), lambda h, i: (0, 0))
-    heads = width // HEAD_DIM
-    pairs = heads * length * length // 2
-    return pl.pallas_call(
-        functools.partial(own_backward_kernel, rows, heads),
-        grid=(heads, length // rows),
-        in_specs=[block, whole, whole, block, block, block, block, table, table],
-        out_specs=pl.BlockSpec((length, 3 * width), lambda h, i: (0, 0)),
-        out_shape=jax.ShapeDtypeStruct((length, 3 * width), jnp.bfloat16),
-        scratch_shapes=[pltpu.VMEM((length, HEAD_DIM), jnp.float32)] * 2,
-        compiler_params=pltpu.CompilerParams(vmem_limit_bytes=VMEM_BYTES),
-        cost_estimate=pl.CostEstimate(
-            flops=20 * pairs * HEAD_DIM, transcendentals=pairs, bytes_accessed=36 * length * width
-        ),
-        name="own_backward",
-    )(queries, keys, values, upstream, log_totals, delta, start, cosine, sine)
-
-
 def turn_block(matrix, cosine, sine):
     return matrix * cosine + pltpu.roll(matrix, HEAD_DIM // 2, 1) * sine
 
 
-LINK_RATE = {"core": 300e3, "x": 45e3, "y": 45e3, "z": 45e3}
+LINK_RATE = {"core": 300e3, "x": 49e3, "y": 49e3, "z": 49e3}
 
 
 class Place:
@@ -603,7 +505,8 @@
                 pltpu.VMEM((rows, half), low),
                 pltpu.VMEM((rows, half), low),
             ]
-        return [four, four] + middle + [one, one, last] + [
+        ends = [one, one, last] if self.gather else [one, one]
+        return [four, four] + middle + ends + [
             pltpu.SemaphoreType.DMA((9,)),
             pltpu.SemaphoreType.DMA((9,)),
             pltpu.SemaphoreType.DMA((3,)),
@@ -612,8 +515,10 @@
     def bind(self, place, source, result, refs):
         self.place, self.source, self.result = place, source, result
         self.mine, self.core_in = refs[0], refs[1]
-        self.middle = refs[2:-6]
-        self.z_first, self.z_second, self.z_last = refs[-6:-3]
+        ends = 3 if self.gather else 2
+        self.middle = refs[2 : -3 - ends]
+        self.z_last, self.z_second = refs[-4], refs[-5]
+        self.z_first = refs[-6] if self.gather else self.z_last
         self.sent, self.received, self.local = refs[-3:]
 
     def remote(self, slot, source, target, peer):
@@ -823,53 +728,56 @@
         rows, columns, half = self.rows, self.columns, self.columns // 2
         low = jnp.bfloat16
         return [
-            pltpu.VMEM((2, 2, rows, columns), low),
             pltpu.VMEM((2, rows, half), low),
             pltpu.VMEM((2, rows, half), low),
             pltpu.VMEM((rows, half), low),
             pltpu.VMEM((rows, half), low),
-            pltpu.SemaphoreType.DMA((4,)),
-            pltpu.SemaphoreType.DMA((4,)),
-            pltpu.SemaphoreType.DMA((2,)),
+            pltpu.SemaphoreType.DMA((6,)),
+            pltpu.SemaphoreType.DMA((6,)),
+            pltpu.SemaphoreType.DMA((1,)),
         ]
 
     def bind(self, place, source, result, refs):
-        self.place, self.source, self.result = place, source, result
-        self.mine, self.middle = refs[0], refs[1:5]
-        self.sent, self.received, self.local = refs[5:]
+        self.place, self.result = place, result
+        self.blocks = source
+        self.middle = refs[:4]
+        self.sent, self.received, self.local = refs[4:]
+
+    def mine(self, y, x, lanes):
+        return self.blocks.at[2 * y + x, pl.ds(self.offset, self.rows), lanes]
 
     remote = Chunk.remote
     halves = Chunk.halves
 
-    def load(self):
-        rows = pl.ds(self.offset, self.rows)
-        return pltpu.make_async_copy(self.source.at[:, :, rows, :], self.mine, self.local.at[0])
-
     def wide_copies(self):
         p, (left, right) = self.place, self.halves()
-        return [
-            self.remote(0, self.mine.at[:, 1 - p.x, :, left], self.middle[0], "x"),
-            self.remote(1, self.mine.at[1 - p.y, :, :, right], self.middle[1], "y"),
-        ]
+        copies = []
+        for a in range(2):
+            copies.append(
+                self.remote(a, self.mine(a, 1 - p.x, left), self.middle[0].at[a], "x")
+            )
+            copies.append(
+                self.remote(2 + a, self.mine(1 - p.y, a, right), self.middle[1].at[a], "y")
+            )
+        return copies
 
     def narrow_copies(self):
         p, (left, right) = self.place, self.halves()
         return [
-            self.remote(2, self.mine.at[1 - p.y, p.x, :, left], self.middle[2], "y"),
-            self.remote(3, self.mine.at[p.y, 1 - p.x, :, right], self.middle[3], "x"),
+            self.remote(4, self.mine(1 - p.y, p.x, left), self.middle[2], "y"),
+            self.remote(5, self.mine(p.y, 1 - p.x, right), self.middle[3], "x"),
         ]
 
     def out_copy(self):
         p = self.place
+        whole = pl.ds(0, self.columns)
         return pltpu.make_async_copy(
-            self.mine.at[p.y, p.x], self.result.at[pl.ds(self.offset, self.rows), :], self.local.at[1]
+            self.mine(p.y, p.x, whole),
+            self.result.at[pl.ds(self.offset, self.rows), :],
+            self.local.at[0],
         )
 
     def stage_start(self):
-        self.load().start()
-
-    def stage_load(self):
-        self.load().wait()
         for copy in self.wide_copies():
             copy.start()
 
@@ -878,8 +786,8 @@
         for copy in self.wide_copies():
             copy.wait_recv()
         for a in range(2):
-            add_into(self.mine.at[a, p.x, :, left], self.middle[0].at[a])
-            add_into(self.mine.at[p.y, a, :, right], self.middle[1].at[a])
+            add_into(self.mine(a, p.x, left), self.middle[0].at[a])
+            add_into(self.mine(p.y, a, right), self.middle[1].at[a])
         for copy in self.narrow_copies():
             copy.start()
 
@@ -887,8 +795,8 @@
         p, (left, right) = self.place, self.halves()
         for copy in self.narrow_copies():
             copy.wait_recv()
-        add_into(self.mine.at[p.y, p.x, :, left], self.middle[2])
-        add_into(self.mine.at[p.y, p.x, :, right], self.middle[3])
+        add_into(self.mine(p.y, p.x, left), self.middle[2])
+        add_into(self.mine(p.y, p.x, right), self.middle[3])
         self.out_copy().start()
 
     def stage_end(self):
@@ -899,73 +807,353 @@
     def plan(self):
         piece = 2 * self.rows * self.columns
         return [
-            (self.stage_load, [("x", piece), ("y", piece)]),
             (self.stage_wide, [("x", piece / 2), ("y", piece / 2)]),
             (self.stage_narrow, [("core", 0.0)]),
             (self.stage_end, []),
         ]
 
     def opening(self):
-        return [("core", 0.0)]
-
-
-def stage_order(chunks):
-    free, ready, order = {}, [], []
-
-    def send(transfers, now):
-        ends = [now]
+        piece = 2 * self.rows * self.columns
+        return [("x", piece), ("y", piece)]
+
+
+class Steps:
+    def __init__(self, start):
+        self.now, self.free, self.waiting = start, {}, []
+
+    def send(self, transfers):
+        ends = [self.now]
         for link, size in transfers:
-            start = max(now, free.get(link, 0.0))
-            free[link] = start + size / LINK_RATE.get(link, LINK_RATE["z"])
-            ends.append(free[link] + 2.0)
+            start = max(self.now, self.free.get(link, 0.0))
+            self.free[link] = start + size / LINK_RATE.get(link, LINK_RATE["z"])
+            ends.append(self.free[link] + 2.0)
         return max(ends)
 
-    for number, chunk in enumerate(chunks):
-        ready.append((send(chunk.opening(), 0.0), number, 0))
-    now = 0.0
-    while ready:
-        ready.sort()
-        when, number, index = ready.pop(0)
-        now = max(now, when) + 0.3
-        stage, transfers = chunks[number].plan()[index]
-        order.append((now, stage))
-        if index + 1 < len(chunks[number].plan()):
-            ready.append((send(transfers, now), number, index + 1))
-    return order
-
-
-def bind_chunks(chunks, place, sources, results, refs):
+    def open(self, chunks):
+        for chunk in chunks:
+            self.waiting.append((self.send(chunk.opening()), len(self.waiting), chunk, 0))
+
+    def due(self, everything=False):
+        stages = []
+        while self.waiting:
+            self.waiting.sort(key=lambda entry: entry[:2])
+            when, number, chunk, index = self.waiting[0]
+            if when > self.now and not everything:
+                break
+            self.waiting.pop(0)
+            self.now = max(self.now, when) + 0.4
+            stage, transfers = chunk.plan()[index]
+            stages.append(stage)
+            if index + 1 < len(chunk.plan()):
+                self.waiting.append((self.send(transfers), number, chunk, index + 1))
+        return stages
+
+    def spend(self, duration):
+        self.now += duration
+
+
+def back_kernel(
+    chunks,
+    first_chunks,
+    heads,
+    flag_ref,
+    g_ref,
+    q_hbm,
+    k_hbm,
+    v_hbm,
+    memory_hbm,
+    every_hbm,
+    down_ref,
+    gate_ref,
+    up_ref,
+    out_ref,
+    w_ref,
+    mix_ref,
+    log_ref,
+    table_ref,
+    sum_down,
+    sum_gate,
+    sum_up,
+    sum_out,
+    sum_qkv,
+    sum_first,
+    q,
+    k,
+    v,
+    upstream,
+    shared,
+    dk,
+    dv,
+    total,
+    delta,
+    part_qkv,
+    trade_sent,
+    trade_received,
+    local,
+    *refs,
+):
+    place = Place()
+    seq = lax.axis_index("seq")
+    tokens = g_ref.shape[0]
+    width = heads * HEAD_DIM
     used = 0
-    for chunk in chunks:
+    sources = [down_ref, gate_ref, up_ref, out_ref, part_qkv, shared]
+    results = [sum_down, sum_gate, sum_up, sum_out, sum_qkv, sum_first]
+    for chunk in chunks + first_chunks:
         count = len(chunk.scratch())
         chunk.bind(place, sources[chunk.term], results[chunk.term], refs[used : used + count])
         used += count
 
-
-def exchange_kernel(chunks, peers, count, *refs):
-    sources, results = refs[:count], refs[count : 2 * count]
-    place = Place()
-    bind_chunks(chunks, place, sources, results, refs[2 * count :])
-    place.greet(peers)
+    def owner_at(turn):
+        low, high = lax.rem(turn, 2), lax.div(turn, 2)
+        x = place.x + low - 2 * place.x * low
+        y = place.y + high - 2 * place.y * high
+        return 2 * y + x
+
+    def columns(owner):
+        return pl.ds(pl.multiple_of(owner * width, HEAD_DIM), width)
+
+    def span(block):
+        return pl.ds(pl.multiple_of(block * tokens, tokens), tokens)
+
+    def lanes(head):
+        return pl.ds(pl.multiple_of(head * HEAD_DIM, HEAD_DIM), HEAD_DIM)
+
+    across = {"x": seq + 1 - 2 * place.x, "y": seq + 2 - 4 * place.y, "xy": 3 - seq}
+    trades = [
+        pltpu.make_async_remote_copy(
+            src_ref=g_ref.at[:, columns(across[peer])],
+            dst_ref=upstream.at[span(seq), :],
+            send_sem=trade_sent.at[slot],
+            recv_sem=trade_received.at[slot],
+            device_id=place.peer[peer],
+            device_id_type=pl.DeviceIdType.MESH,
+        )
+        for slot, peer in enumerate(("x", "y", "xy"))
+    ]
+    loads = [
+        pltpu.make_async_copy(g_ref.at[:, columns(seq)], upstream.at[span(seq), :], local.at[0]),
+        pltpu.make_async_copy(q_hbm, q, local.at[1]),
+        pltpu.make_async_copy(k_hbm, k, local.at[2]),
+        pltpu.make_async_copy(v_hbm, v, local.at[3]),
+        pltpu.make_async_copy(memory_hbm, shared, local.at[4]),
+    ]
+    load_every = pltpu.make_async_copy(every_hbm, shared, local.at[5])
+
+    def tables(rows):
+        both = table_ref[rows, :]
+        swapped = pltpu.roll(both, HEAD_DIM // 2, 1)
+        first = lax.broadcasted_iota(jnp.int32, both.shape, 1) < HEAD_DIM // 2
+        return jnp.where(first, both, swapped), jnp.where(first, swapped, -both)
+
+    def turn_back(matrix, rows):
+        cosine, sine = tables(rows)
+        return turn_block(matrix, cosine, sine).astype(jnp.bfloat16)
+
+    def memory_part(head, block):
+        rows, mine = span(block), lanes(head)
+        query, grads = q[rows, mine], upstream[rows, mine]
+        row_delta = jnp.sum(
+            grads.astype(jnp.float32) * mix_ref[rows, mine].astype(jnp.float32), axis=1, keepdims=True
+        )
+        delta[...] = jnp.broadcast_to(row_delta, delta.shape)
+        closed = (1 - flag_ref[0]).astype(jnp.float32) * 1e30
+        log_total = log_ref[rows, mine][:, :1] + closed
+        result = jnp.zeros(total.shape, jnp.float32)
+        for slot in range(shared.shape[0]):
+            for run in range(2):
+
+                def tile(kind):
+                    start = pl.multiple_of((2 * run + kind) * width + head * HEAD_DIM, HEAD_DIM)
+                    return shared[slot, :, pl.ds(start, HEAD_DIM)]
+
+                keys, values = tile(0), tile(1)
+                probs = jnp.exp2(product_nt(query, keys) - log_total)
+                dscores = probs * (product_nt(grads, values) - row_delta)
+                result = result + product(dscores.astype(jnp.bfloat16), keys)
+        total[...] = result
+
+    def own_part(head, block):
+        rows, mine = span(block), lanes(head)
+        query, grads = q[rows, mine], upstream[rows, mine]
+        log_total, row_delta = log_ref[rows, mine][:, :1], delta[:, :1]
+
+        def turn(other, result, diagonal):
+            keys = k[span(other), mine]
+            scores = product_nt(query, keys)
+            if diagonal:
+                scores = causal(scores)
+            probs = jnp.exp2(scores - log_total)
+            dscores = (probs * (product_nt(grads, v[span(other), mine]) - row_delta)).astype(
+                jnp.bfloat16
+            )
+            dv[span(other), :] += product_tn(probs.astype(jnp.bfloat16), grads)
+            dk[span(other), :] += product_tn(dscores, query)
+            return result + product(dscores, keys)
+
+        result = turn(block, total[...], True)
+        result = lax.fori_loop(0, block, lambda other, r: turn(other, r, False), result)
+        q[rows, mine] = turn_back(result * SCORE_SCALE, rows)
+
+    def close_head(head):
+        mine = lanes(head)
+
+        def turn(block, carry):
+            rows = span(block)
+            k[rows, mine] = turn_back(dk[rows, :] * LN2, rows)
+            v[rows, mine] = dv[rows, :].astype(jnp.bfloat16)
+            return carry
+
+        lax.fori_loop(0, 4, turn, 0)
+
+    def multiply_qkv(index, carry):
+        cut = pl.ds(pl.multiple_of(index * width, HEAD_DIM), width)
+        for kind, part in enumerate((q, k, v)):
+            term = None
+            for block in range(shared.shape[0]):
+                product_part = product_tn(shared[block, :, cut], part[block * tokens : (block + 1) * tokens, :])
+                term = product_part if term is None else term + product_part
+            term = term.astype(jnp.bfloat16)
+            half = term.shape[0] // 2
+            place_y, place_x = lax.div(index, 2), lax.rem(index, 2)
+            for core in range(2):
+                part_qkv[place_y, place_x, core, :, kind * width : (kind + 1) * width] = term[
+                    core * half : (core + 1) * half, :
+                ]
+        return carry
+
+    def multiply_first(block, carry):
+        rows = span(block)
+        result = None
+        for kind, part in enumerate((q, k, v)):
+            term = product_nt(part[rows, :], w_ref[:, kind * width : (kind + 1) * width])
+            result = term if result is None else result + term
+        shared[block] = result.astype(jnp.bfloat16)
+        return carry
+
+    place.greet(("core", "x", "y", "xy", "pair"))
+    for copy in trades + loads:
+        copy.start()
     for chunk in chunks:
         chunk.stage_start()
-    for _, stage in stage_order(chunks):
-        stage()
-
-
-def exchange(chunks, terms, shapes, collective_id, name):
+    steps = Steps(3.0)
+    steps.free.update(x=11.0, y=11.0)
+    steps.open(chunks)
+    for copy in loads:
+        copy.wait()
+    slots = []
+    for unit in range(2 * 4 * heads):
+        slots.append(steps.due())
+        steps.spend(4.3 if unit % 2 == 0 else 3.2)
+
+    def run(stages):
+        for stage in stages:
+            stage()
+
+    def unit(index, carry):
+        head, turn = lax.div(index, 4), lax.rem(index, 4)
+        block = owner_at(turn)
+        for number in range(4 * heads):
+            if slots[2 * number] or number in (1, 2, 3):
+
+                @pl.when(index == number)
+                def _(number=number):
+                    run(slots[2 * number])
+                    if number in (1, 2, 3):
+                        trades[number - 1].wait_recv()
+
+        @pl.when(turn == 0)
+        def _():
+            dk[...] = jnp.zeros_like(dk)
+            dv[...] = jnp.zeros_like(dv)
+
+        memory_part(head, block)
+        for number in range(4 * heads):
+            if slots[2 * number + 1]:
+
+                @pl.when(index == number)
+                def _(number=number):
+                    run(slots[2 * number + 1])
+
+        own_part(head, block)
+
+        @pl.when(turn == 3)
+        def _():
+            close_head(head)
+
+        return carry
+
+    lax.fori_loop(0, 4 * heads, unit, 0)
+    load_every.start()
+    run(steps.due())
+    load_every.wait()
+    lax.fori_loop(0, 4, multiply_qkv, 0)
+    steps.spend(8.0)
+    qkv_chunks = [chunk for chunk in first_chunks if chunk.term == 4]
+    row_chunks = [chunk for chunk in first_chunks if chunk.term == 5]
+    for chunk in qkv_chunks:
+        chunk.stage_start()
+    steps.open(qkv_chunks)
+    run(steps.due())
+    lax.fori_loop(0, 4, multiply_first, 0)
+    steps.spend(6.0)
+    for chunk in row_chunks:
+        chunk.stage_start()
+    steps.open(row_chunks)
+    run(steps.due(True))
+    for copy in trades:
+        copy.wait_send()
+
+
+def back(flag, grads, queries, keys, values, memory, every, terms, w_heads, attended, log_totals, table, collective_id):
+    tokens, depth = grads.shape
+    length, width = queries.shape
+    low = jnp.bfloat16
+    chunks, shapes = [], []
+    for index, term in enumerate(terms):
+        rows, columns = term.shape[0] // 8, term.shape[1]
+        parts = 2 if rows % 32 == 0 and index < 3 else 1
+        chunks += [Chunk(index, n * rows // parts, rows // parts, columns) for n in range(parts)]
+        shapes.append((2, rows, columns))
+    rows = depth // 8
+    first_chunks = [Chunk(4, n * rows // 2, rows // 2, 3 * width, True) for n in range(2)]
+    first_chunks += [RowChunk(5, n * tokens // 4, tokens // 4, depth) for n in range(4)]
+    shapes += [(2, rows, 12 * width), (tokens, depth)]
     anywhere = pl.BlockSpec(memory_space=pl.ANY)
+    inside = pl.BlockSpec(memory_space=pltpu.VMEM)
+    scratch = (
+        [pltpu.VMEM((length, width), low)] * 4
+        + [pltpu.VMEM((4, tokens, depth), low)]
+        + [pltpu.VMEM((length, HEAD_DIM), jnp.float32)] * 2
+        + [pltpu.VMEM((tokens, HEAD_DIM), jnp.float32)] * 2
+        + [pltpu.VMEM((2, 2, 2, rows, 3 * width), low)]
+        + [pltpu.SemaphoreType.DMA((3,))] * 2
+        + [pltpu.SemaphoreType.DMA((6,))]
+    )
     return pl.pallas_call(
-        functools.partial(exchange_kernel, chunks, ("core", "x", "y", "xy", "pair"), len(terms)),
-        in_specs=[anywhere] * len(terms),
-        out_specs=[anywhere] * len(terms),
-        out_shape=[jax.ShapeDtypeStruct(shape, jnp.bfloat16) for shape in shapes],
-        scratch_shapes=[ref for chunk in chunks for ref in chunk.scratch()],
+        functools.partial(back_kernel, chunks, first_chunks, width // HEAD_DIM),
+        in_specs=[pl.BlockSpec(memory_space=pltpu.SMEM)] + [anywhere] * 10 + [inside] * 4,
+        out_specs=[anywhere] * len(shapes),
+        out_shape=[jax.ShapeDtypeStruct(shape, low) for shape in shapes],
+        scratch_shapes=scratch + [ref for chunk in chunks + first_chunks for ref in chunk.scratch()],
         compiler_params=pltpu.CompilerParams(
-            collective_id=collective_id, has_side_effects=True, vmem_limit_bytes=VMEM_BYTES
+            collective_id=collective_id, has_side_effects=True, vmem_limit_bytes=VMEM_MOST
         ),
-        name=name,
-    )(*terms)
+        name="back",
+    )(
+        flag,
+        grads,
+        queries,
+        keys,
+        values,
+        memory,
+        every,
+        *[term.reshape((2, 2, 2, term.shape[0] // 8, term.shape[1])) for term in terms],
+        w_heads,
+        attended,
+        log_totals,
+        table,
+    )
 
 
 class Line:
@@ -1341,13 +1529,13 @@
     ).reshape(D, 3 * width)
     cosine, sine = turn_tables(lax.iota(jnp.int32, length).astype(jnp.float32))
     cosine, sine = cosine[:, 0, :], sine[:, 0, :]
+    table = jnp.concatenate([cosine[:, : HEAD_DIM // 2], sine[:, : HEAD_DIM // 2]], axis=1)
     first_half = lax.broadcasted_iota(jnp.int32, sine.shape, 1) < HEAD_DIM // 2
     sine = jnp.where(first_half, -sine, sine)
     every_low, memory, queries, keys, values, mixed, row_max, row_sum = front(
-        first_low, mem_keys[0], mem_values[0], w_heads, cosine, sine, seg_size, seq_size, 3
-    )
-    every_low = every_low.reshape(length, D)
-    heads_low, heads_out, log_totals = memory_forward(
+        first_low, mem_keys[0], mem_values[0], w_heads, cosine, sine, seg_size, seq_size, 1
+    )
+    heads_low, chosen_memory, log_totals = memory_forward(
         chosen, queries, mixed, row_max, row_sum, memory
     )
     attended_low = lax.all_to_all(heads_low, "seq", 0, 1, tiled=True)
@@ -1377,41 +1565,25 @@
     residual_low = grad_residual.astype(low)
     term_out = product_tn(attended_low, residual_low).astype(low)
     grad_attended = product_nt(residual_low, w_out).astype(low)
-    grad_heads = lax.all_to_all(grad_attended, "seq", 1, 0, tiled=True)
-
-    start, delta = memory_backward(chosen, queries, grad_heads, heads_out, log_totals, memory)
-    grad_projected = own_backward(
-        queries, keys, values, grad_heads, log_totals, delta, start, cosine, sine
-    )
-    terms = [term_down, term_gate, term_up, term_out]
-    pieces = [(term.shape[0] // (2 * seq_size), term.shape[1]) for term in terms]
-    chunks = []
-    for index, (rows, columns) in enumerate(pieces):
-        parts = 2 if rows % 32 == 0 and index < 3 else 1
-        chunks += [Chunk(index, n * rows // parts, rows // parts, columns) for n in range(parts)]
-    sums = exchange(
-        chunks,
-        [term.reshape((2, 2, 2) + piece) for term, piece in zip(terms, pieces)],
-        [(2,) + piece for piece in pieces],
-        1,
-        "sum_terms",
+    *sums, qkv_rows, first_rows = back(
+        flag.astype(jnp.int32),
+        grad_attended,
+        queries,
+        keys,
+        values,
+        chosen_memory,
+        every_low,
+        [term_down, term_gate, term_up, term_out],
+        w_heads,
+        heads_low,
+        log_totals,
+        table,
+        2,
     )
     grad_down, grad_gate, grad_up, grad_out = [
-        total.reshape(2 * piece[0], piece[1]).astype(jnp.float32) for total, piece in zip(sums, pieces)
+        total.reshape(2 * total.shape[1], total.shape[2]).astype(jnp.float32) for total in sums
     ]
-
-    part_first = product_nt(grad_projected, w_heads).astype(low)
-    part_qkv = product_tn(every_low, grad_projected).astype(low)
-    rows = D // (2 * seq_size)
-    qkv_rows, first_rows = exchange(
-        [Chunk(0, n * rows // 2, rows // 2, 3 * width, True) for n in range(2)]
-        + [RowChunk(1, n * tokens // 4, tokens // 4, D) for n in range(4)],
-        [part_qkv.reshape(2, 2, 2, rows, 3 * width), part_first.reshape(2, 2, tokens, D)],
-        [(2, rows, 3 * D), (tokens, D)],
-        2,
-        "sum_first",
-    )
-    grad_qkv = qkv_rows.reshape(2 * rows, 3 * D).astype(jnp.float32)
+    grad_qkv = qkv_rows.reshape(width, 3 * D).astype(jnp.float32)
     grad_inputs = norm_input_grad(
         inputs, first_inverse, norm1_gain, first_rows.astype(jnp.float32)
     )

time: 523 us -> 424 us (0.81); the launches traced: 514 us -> 421 us
  Pallas kernels: 368 us -> 297 us
  matrix products: 76.8 us -> 62.5 us
    pallas_call x4 -> x1, Pallas kernels: 263 us -> 190 us  [back(): pl.pallas_call(functools.partial(back_kernel, chunks, first_chunks, width...]
    dot_general x5 -> x4, matrix products: 30.1 us -> 22.4 us  [product_nt(): lax.dot_general(former, latter, (((1,), (1,)), ((), ())), preferred_eleme...]
    dot_general x5 -> x4, matrix products: 26.5 us -> 19.9 us  [product_tn(): lax.dot_general(former, latter, (((0,), (0,)), ((), ())), preferred_eleme...]
  transfers between devices with their start and end apart: 2 -> 1, of which waited for: 1 -> 1; matrix products, arithmetic and copies ran while one was open for 4% -> 0% of each run, Pallas kernels for 28% -> 0%
where the time goes in v1:
time: 424 us; the launch traced here: 421 us
  Pallas kernels  297 us (70%)
  matrix products  62.5 us (15%)
  other arithmetic  30.4 us (7%)
  local copies, waits for them, and re-layouts  16.8 us (4%)
  waiting for transfers between devices  8.11 us (2%)
  starting transfers between devices  4.49 us (1%)
    pallas_call x1, Pallas kernels, back(): pl.pallas_call(functools.partial(back_kernel, chunks, first_chunks, width...  190 us
    pallas_call x1, Pallas kernels, front(): pl.pallas_call(functools.partial(front_kernel, width // HEAD_DIM), in_spe...  94.6 us
    dot_general x4, matrix products, product_nt(): lax.dot_general(former, latter, (((1,), (1,)), ((), ())), preferred_eleme...  22.4 us
    dot_general x4, matrix products, product(): return jnp.dot(former, latter, preferred_element_type=jnp.float32)  20.2 us
    dot_general x4, matrix products, product_tn(): lax.dot_general(former, latter, (((0,), (0,)), ((), ())), preferred_eleme...  19.9 us
    pallas_call x1, Pallas kernels, memory_forward(): pl.pallas_call(functools.partial(memory_forward_kernel, count), grid_spec...  12.4 us
    unnamed x53, local copies, waits for them, and re-layouts  9.17 us
  transfers between devices with their start and end apart: 1, of which 1 were waited for; matrix products, arithmetic and copies ran while one was open for 0% of the time, Pallas kernels for 0%

profile of v1, /device:TPU:0, one launch (start us, length us, event | category | flops | bytes accessed | tf_op | source)
XLA Modules:
  0.0 420.7 jit_solution(8184013781761156999)
XLA Ops:
  2.8 1.5 fusion.1
  4.9 8.6 %copy.26 = bf16[1024,3072]{0,1:T(8,128)(2,1)} copy(bf16[1024,3072]{1,0:T(8,128)(2,1)} %param.17) | data formatting | bytes 12582912 | tf_op args[4]
  13.5 1.5 constant_dynamic-slice_fusion
  15.0 1.6 copy.27.w_ref
  17.0 1.3 fusion.3.x_ref
  18.3 4.9 %fusion.13 = (f32[2048,128]{1,0:T(8,128)S(1)}, f32[2048,128]{1,0:T(8,128)}, f32[2048,128]{1,0:T(8,128)}) fusion(f32[2048,64]{1,0:T(8,128)S(1)} %broadcast_multiply_fusion, pred[128]{0:T(512)(128)(4,1)S(1)} %iota_compare_fusion), kind=kLoop, calls=%fused_computation.44 | loop fusion | flops 786432 | bytes 3670144 | tf_op jit(solution)/shard_map/sin | solution.py:55
  24.4 94.6 %front.1 = (bf16[4,512,1024]{2,1,0:T(8,128)(2,1)}, bf16[8,1024,512]{2,1,0:T(8,128)(2,1)}, bf16[2048,256]{1,0:T(8,128)(2,1)}, bf16[2048,256]{1,0:T(8,128)(2,1)}, ...) custom-call(bf16[512,1024]{1,0:T(8,128)(2,1)} %fusion.3.x_ref, ...), custom_call_target="tpu_custom_call" | custom-call | tf_op jit(solution)/shard_map/front/pallas_call | solution.py:1462
  119.0 12.4 %memory_forward.1 = (bf16[2048,256]{1,0:T(8,128)(2,1)}, bf16[4,512,1024]{2,1,0:T(8,128)(2,1)}, f32[2048,256]{1,0:T(8,128)}) custom-call(s32[5]{0:T(128)} %pad_add_fusion.chosen, bf16[2048,256]{1,0:T(8,128)(2,1)} %get-tuple-element.26.q_ref.q_hbm, f32[2048,256]{1,0:T(8,128)} %get-tuple-element.27.mix_ref, f32[2048,256]{1,0:T(8,128)} %get-tuple-element.28.max_ref, ...), custom_call_target="tpu_custom_call" | custom-call | flops 17179869184 | bytes 18874368 | tf_op jit(solution)/shard_map/memory_forward/pallas_call | solution.py:403
  131.5 2.4 copy.28
  133.8 4.5 %all-to-all-start = ((bf16[4,512,256]{1,2,0:T(8,128)(2,1)}), bf16[4,512,256]{1,2,0:T(8,128)(2,1)}, u32[]{:S(2)}, u32[]{:S(2)}) async-start(bf16[4,512,256]{1,2,0:T(8,128)(2,1)} %copy.28), calls=%async_computation | async-start | bytes 2097152 | tf_op jit(solution)/shard_map/all_to_all | solution.py:1541
  138.3 1.4 pad_maximum_fusion.1.table_ref
  139.7 8.1 %all-to-all-done = bf16[4,512,256]{1,2,0:T(8,128)(2,1)} async-done(((bf16[4,512,256]{1,2,0:T(8,128)(2,1)}), bf16[4,512,256]{1,2,0:T(8,128)(2,1)}, u32[]{:S(2)}, u32[]{:S(2)}) %all-to-all-start) | async-done | bytes 1048608 | tf_op jit(solution)/shard_map/all_to_all | solution.py:1541
  147.8 3.3 multiply_reduce_fusion.4
  151.4 7.8 %fusion.18 = f32[512,2816]{1,0:T(8,128)} fusion(bf16[512,1024]{1,0:T(8,128)(2,1)S(1)} %multiply_convert_fusion.3, bf16[1024,2816]{1,0:T(8,128)(2,1)} %param.20), kind=kOutput, calls=%fused_computation.65 | convolution fusion | flops 2952790016 | bytes 12582912 | tf_op jit(solution)/shard_map/dot_general | solution.py:22
  159.2 5.0 %fusion.17 = f32[512,2816]{1,0:T(8,128)} fusion(bf16[512,1024]{1,0:T(8,128)(2,1)S(1)} %multiply_convert_fusion.3, bf16[1024,2816]{1,0:T(8,128)(2,1)S(1)} %bitcast.84), kind=kOutput, calls=%fused_computation.64 | convolution fusion | flops 2952790016 | bytes 12582912 | tf_op jit(solution)/shard_map/dot_general | solution.py:22
  164.2 11.8 %multiply_convert_fusion = (bf16[512,2816]{1,0:T(8,128)(2,1)S(1)}, bf16[512,2816]{1,0:T(8,128)(2,1)}, bf16[512,2816]{1,0:T(8,128)(2,1)}) fusion(f32[512,2816]{1,0:T(8,128)} %fusion.17, f32[512,2816]{1,0:T(8,128)} %fusion.18, bf16[2816,1024]{1,0:T(8,128)(2,1)} %param.21, bf16[1,512,1024]{2,1,0:T(8,128)(2,1)S(1)} %copy-done.11), kind=kOutput, calls=%fused_computation | convolution fusion | flops 2974416896 | bytes 27000832 | tf_op jit(solution)/shard_map/dot_general | solution.py:26
  176.0 5.0 %fusion.19 = f32[512,1024]{1,0:T(8,128)S(1)} fusion(bf16[512,2816]{1,0:T(8,128)(2,1)} %get-tuple-element.50, bf16[1024,2816]{1,0:T(8,128)(2,1)S(1)} %bitcast.84), kind=kOutput, calls=%fused_computation.66 | convolution fusion | flops 2952790016 | bytes 10747904 | tf_op jit(solution)/shard_map/dot_general | solution.py:26
  181.0 3.4 multiply_reduce_fusion.3
  185.0 4.6 %convolution_convert_fusion.3 = bf16[1024,1024]{1,0:T(8,128)(2,1)} fusion(bf16[512,1024]{0,1:T(8,128)(2,1)} %bitcast.9, f32[512,1024]{1,0:T(8,128)S(1)} %convert_add_fusion.1), kind=kOutput, calls=%fused_computation.31 | convolution fusion | flops 1075314688 | bytes 5242880 | tf_op jit(solution)/shard_map/dot_general | solution.py:32
  189.6 2.3 convolution_convert_fusion.4.g_ref
  191.9 5.0 %convolution_convert_fusion = bf16[1024,2816]{1,0:T(8,128)(2,1)} fusion(bf16[512,1024]{1,0:T(8,128)(2,1)S(1)} %multiply_convert_fusion.3, bf16[512,2816]{1,0:T(8,128)(2,1)S(1)} %get-tuple-element.49), kind=kOutput, calls=%fused_computation.5 | convolution fusion | flops 2955673600 | bytes 9699328 | tf_op jit(solution)/shard_map/dot_general | solution.py:32
  196.9 5.1 %convolution_convert_fusion.1 = bf16[1024,2816]{1,0:T(8,128)(2,1)} fusion(bf16[512,1024]{1,0:T(8,128)(2,1)S(1)} %multiply_convert_fusion.3, bf16[512,2816]{1,0:T(8,128)(2,1)S(1)} %copy-done.19), kind=kOutput, calls=%fused_computation.6 | convolution fusion | flops 2955673600 | bytes 9699328 | tf_op jit(solution)/shard_map/dot_general | solution.py:32
  202.0 4.1 fusion.9
  206.1 5.2 %convolution_convert_fusion.2 = bf16[2816,1024]{1,0:T(8,128)(2,1)} fusion(bf16[512,2816]{1,0:T(8,128)(2,1)S(1)} %copy-done.18, bf16[1,512,1024]{2,1,0:T(8,128)(2,1)S(1)} %copy-done.11), kind=kOutput, calls=%fused_computation.7 | convolution fusion | flops 2955673600 | bytes 9699328 | tf_op jit(solution)/shard_map/dot_general | solution.py:32
  211.3 190.2 %back.1 = (bf16[2,352,1024]{2,1,0:T(8,128)(2,1)}, bf16[2,128,2816]{2,1,0:T(8,128)(2,1)}, bf16[2,128,2816]{2,1,0:T(8,128)(2,1)}, bf16[2,128,1024]{2,1,0:T(8,128)(...) custom-call(s32[1]{0:T(128)} %dynamic_slice.28.flag_ref, ...), custom_call_target="tpu_custom_call" | custom-call | tf_op jit(solution)/shard_map/back/pallas_call | solution.py:1133
  401.5 2.1 fusion.8
  403.6 2.1 bitcast_convert_fusion.4
  405.7 3.6 multiply_reduce_fusion
  410.0 2.0 bitcast_convert_fusion.1
  412.1 1.9 fusion.7
  414.4 4.7 %multiply_reduce_fusion.1 = (f32[256]{0:T(256)S(1)}, f32[256,2816]{1,0:T(8,128)}, f32[256]{0:T(256)S(1)}, f32[256,2816]{1,0:T(8,128)}) fusion(bf16[1024,2816]{1,0:T(8,128)(2,1)} %param.20, s32[]{:T(128)S(6)} %select_n.24, bf16[2,128,2816]{2,1,0:T(8,128)(2,1)S(1)} %copy-done.9, bf16[2,128,2816]{2,1,0:T(8,128)(2,1)S(1)} %copy-done.8, bf16[1024,2816]{1,0:T(8,128)(2,1)} %param.19), kind=kLoop, calls=%fused_computation.14 | loop fusion | flops 5766656 | bytes 11536388 | tf_op jit(solution)/shard_map/reduce_sum | solution.py:1597
  419.2 1.3 dynamic-slice_divide_fusion
  (69 shorter events, 6.2 us)
Async XLA Ops:
  4.9 12.1 %copy-start.14 = (f32[512]{0:T(512)}, f32[512]{0:T(512)S(1)}, u32[]{:S(2)}) copy-start(f32[512]{0:T(512)S(1)} %get-tuple-element.56) | copy-start | bytes 6148
  15.0 2.0 copy-start
  15.0 2.0 copy-start.12
  131.5 6.9 %copy-start.2 = (f32[2048,128]{1,0:T(8,128)S(1)}, f32[2048,128]{1,0:T(8,128)}, u32[]{:S(2)}) copy-start(f32[2048,128]{1,0:T(8,128)} %get-tuple-element.54.cos_ref) | copy-start | bytes 3145732
  133.8 14.0 %all-to-all-start = ((bf16[4,512,256]{1,2,0:T(8,128)(2,1)}), bf16[4,512,256]{1,2,0:T(8,128)(2,1)}, u32[]{:S(2)}, u32[]{:S(2)}) async-start(bf16[4,512,256]{1,2,0:T(8,128)(2,1)} %copy.28), calls=%async_computation | async-start | bytes 2097152 | tf_op jit(solution)/shard_map/all_to_all | solution.py:1541
  147.8 3.3 copy-start.17
  151.1 8.1 %slice-start = ((s8[5767168]{0:T(1024)(128)(4,1)}), s8[4194304]{0:T(1024)(128)(4,1)S(1)}, s32[]{:S(2)}) async-start(s8[5767168]{0:T(1024)(128)(4,1)} %bitcast.83), calls=%async_computation.1 | async-start | bytes 8388608
  151.4 7.8 %slice-start.1 = ((s8[5767168]{0:T(1024)(128)(4,1)}), s8[1572864]{0:T(1024)(128)(4,1)S(1)}, s32[]{:S(2)}) async-start(s8[5767168]{0:T(1024)(128)(4,1)} %bitcast.83), calls=%async_computation.2 | async-start | bytes 3145728
  159.2 5.0 %copy-start.11 = (bf16[1,512,1024]{2,1,0:T(8,128)(2,1)S(1)}, bf16[1,512,1024]{2,1,0:T(8,128)(2,1)}, u32[]{:S(2)}) copy-start(bf16[1,512,1024]{2,1,0:T(8,128)(2,1)} %param.14) | copy-start | bytes 3145732
  159.2 21.8 %slice-start.2 = ((s8[5767168]{0:T(1024)(128)(4,1)}), s8[4194304]{0:T(1024)(128)(4,1)S(1)}, s32[]{:S(2)}) async-start(s8[5767168]{0:T(1024)(128)(4,1)} %bitcast.85), calls=%async_computation.3 | async-start | bytes 8388608
  164.2 16.8 %slice-start.3 = ((s8[5767168]{0:T(1024)(128)(4,1)}), s8[1572864]{0:T(1024)(128)(4,1)S(1)}, s32[]{:S(2)}) async-start(s8[5767168]{0:T(1024)(128)(4,1)} %bitcast.85), calls=%async_computation.4 | async-start | bytes 3145728
  185.0 4.6 %copy-start.3 = (f32[512,1024]{1,0:T(8,128)}, f32[512,1024]{1,0:T(8,128)S(1)}, u32[]{:S(2)}) copy-start(f32[512,1024]{1,0:T(8,128)S(1)} %convert_add_fusion.1) | copy-start | bytes 6291460
  185.0 4.6 %copy-start.6 = (bf16[1024,1024]{1,0:T(8,128)(2,1)S(1)}, bf16[1024,1024]{1,0:T(8,128)(2,1)}, u32[]{:S(2)}) copy-start(bf16[1024,1024]{1,0:T(8,128)(2,1)} %param.18) | copy-start | bytes 6291460
  191.9 5.0 %copy-start.19 = (bf16[512,2816]{1,0:T(8,128)(2,1)S(1)}, bf16[512,2816]{1,0:T(8,128)(2,1)}, u32[]{:S(2)}) copy-start(bf16[512,2816]{1,0:T(8,128)(2,1)} %get-tuple-element.50) | copy-start | bytes 8650756
  191.9 10.1 %slice-start.4 = ((s8[5767168]{0:T(1024)(128)(4,1)}), s8[4194304]{0:T(1024)(128)(4,1)S(1)}, s32[]{:S(2)}) async-start(s8[5767168]{0:T(1024)(128)(4,1)} %bitcast.87), calls=%async_computation.5 | async-start | bytes 8388608
  196.9 5.1 %slice-start.5 = ((s8[5767168]{0:T(1024)(128)(4,1)}), s8[1572864]{0:T(1024)(128)(4,1)S(1)}, s32[]{:S(2)}) async-start(s8[5767168]{0:T(1024)(128)(4,1)} %bitcast.87), calls=%async_computation.6 | async-start | bytes 3145728
  196.9 5.1 %copy-start.18 = (bf16[512,2816]{1,0:T(8,128)(2,1)S(1)}, bf16[512,2816]{1,0:T(8,128)(2,1)}, u32[]{:S(2)}) copy-start(bf16[512,2816]{1,0:T(8,128)(2,1)} %get-tuple-element.51) | copy-start | bytes 8650756
  401.5 4.2 %copy-start.7 = (bf16[2,128,3072]{2,1,0:T(8,128)(2,1)S(1)}, bf16[2,128,3072]{2,1,0:T(8,128)(2,1)}, u32[]{:S(2)}) copy-start(bf16[2,128,3072]{2,1,0:T(8,128)(2,1)} %get-tuple-element.38) | copy-start | bytes 4718596
  405.7 3.6 copy-start.13
  405.7 4.3 %copy-start.10 = (bf16[2,352,1024]{2,1,0:T(8,128)(2,1)S(1)}, bf16[2,352,1024]{2,1,0:T(8,128)(2,1)}, u32[]{:S(2)}) copy-start(bf16[2,352,1024]{2,1,0:T(8,128)(2,1)} %get-tuple-element.42) | copy-start | bytes 4325380
  409.3 2.7 copy-start.1
  409.3 2.7 copy-start.4
  409.3 2.7 copy-start.5
  409.3 2.7 copy-start.15
  409.3 2.7 copy-start.16
  412.1 1.9 copy-start.8
  412.1 2.4 copy-start.9

commit v2 on v1

--- a/solution.py
+++ b/solution.py
@@ -3,6 +3,7 @@
 
 import jax
 import jax.numpy as jnp
+import numpy as np
 from jax import lax
 from jax.experimental import pallas as pl
 from jax.experimental.pallas import tpu as pltpu
@@ -324,7 +325,7 @@
     return jnp.where(columns <= rows, scores, masked_score)
 
 
-def attend(query, pairs, diagonal, carried):
+def attend(query, pairs, diagonal, carried, closed=0.0):
     every, lane_max = [], None
     for index, (keys, _) in enumerate(pairs):
         scores = product_nt(query, keys)
@@ -332,12 +333,13 @@
             scores = causal(scores)
         lane_max = lane_fold(jnp.maximum, scores, lane_max)
         every.append(scores)
-    row_max = jnp.max(lane_max, axis=1, keepdims=True)
+    row_max = jnp.max(lane_max, axis=1, keepdims=True) - closed
     if carried is not None:
         row_max = jnp.maximum(row_max, carried[0])
+    shift = row_max + closed
     lane_sum, mixed = None, None
     for scores, (_, values) in zip(every, pairs):
-        probs = jnp.exp2(scores - row_max)
+        probs = jnp.exp2(scores - shift)
         lane_sum = lane_fold(jnp.add, probs, lane_sum)
         part = product(probs.astype(jnp.bfloat16), values)
         mixed = part if mixed is None else mixed + part
@@ -349,84 +351,29 @@
     return row_max, row_sum, mixed
 
 
-def memory_specs(heads, rows, count):
-    specs = []
-    for slot in range(count):
-        specs.append(
-            pl.BlockSpec((1, rows, HEAD_DIM), lambda h, i, chosen, slot=slot: (chosen[slot], 0, h))
-        )
-        specs.append(
-            pl.BlockSpec(
-                (1, rows, HEAD_DIM), lambda h, i, chosen, slot=slot: (chosen[slot], 0, heads + h)
-            )
-        )
-    return specs
-
-
-def memory_forward_kernel(count, chosen, q_ref, mix_ref, max_ref, sum_ref, *rest):
-    blocks = rest[: 2 * count]
-    low_ref, copy_ref, log_ref = rest[2 * count :]
-    head = pl.program_id(0)
-    carried = (max_ref[:, :1], sum_ref[:, :1], mix_ref[...])
-
-    def finish(row_max, row_sum, mixed):
-        low_ref[...] = (mixed * (1.0 / row_sum)).astype(jnp.bfloat16)
-        log_ref[...] = jnp.broadcast_to(row_max + jnp.log2(row_sum), log_ref.shape)
-
-    @pl.when(pl.program_id(1) == 0)
-    def _():
-        rows = copy_ref.shape[1]
-        width = copy_ref.shape[2] // 4
-        for n in range(count):
-            for run in range(2):
-                for kind in range(2):
-                    start = pl.multiple_of((2 * run + kind) * width + head * HEAD_DIM, HEAD_DIM)
-                    copy_ref[n, :, pl.ds(start, HEAD_DIM)] = blocks[2 * n + kind][
-                        0, run * rows : (run + 1) * rows, :
-                    ]
-
-    @pl.when(chosen[count] > 0)
-    def _():
-        pairs = [(blocks[2 * n][0], blocks[2 * n + 1][0]) for n in range(count)]
-        finish(*attend(q_ref[...], pairs, False, carried))
-
-    @pl.when(chosen[count] <= 0)
-    def _():
-        finish(*carried)
-
-
-def memory_forward(chosen, queries, mixed, row_max, row_sum, memory, rows=512):
-    length, width = queries.shape
-    heads, count = width // HEAD_DIM, chosen.shape[0] - 1
-    block = pl.BlockSpec((rows, HEAD_DIM), lambda h, i, chosen: (i, h))
-    pairs = heads * length * count * memory.shape[1]
-    return pl.pallas_call(
-        functools.partial(memory_forward_kernel, count),
-        grid_spec=pltpu.PrefetchScalarGridSpec(
-            num_scalar_prefetch=1,
-            grid=(heads, length // rows),
-            in_specs=[block] * 4 + memory_specs(heads, memory.shape[1], count),
-            out_specs=[
-                block,
-                pl.BlockSpec((count, memory.shape[1] // 2, 4 * width), lambda h, i, chosen: (0, 0, 0)),
-                block,
-            ],
-        ),
-        out_shape=[
-            jax.ShapeDtypeStruct((length, width), jnp.bfloat16),
-            jax.ShapeDtypeStruct((count, memory.shape[1] // 2, 4 * width), jnp.bfloat16),
-            jax.ShapeDtypeStruct((length, width), jnp.float32),
-        ],
-        compiler_params=pltpu.CompilerParams(vmem_limit_bytes=VMEM_BYTES),
-        cost_estimate=pl.CostEstimate(
-            flops=8 * pairs * HEAD_DIM, transcendentals=pairs, bytes_accessed=36 * length * width
-        ),
-        name="memory_forward",
-    )(chosen, queries, mixed, row_max, row_sum, *[memory] * (2 * count))
-
-
 def turn_block(matrix, cosine, sine):
     return matrix * cosine + pltpu.roll(matrix, HEAD_DIM // 2, 1) * sine
+
+
+def turn_factors(both):
+    swapped = pltpu.roll(both, HEAD_DIM // 2, 1)
+    first = lax.broadcasted_iota(jnp.int32, both.shape, 1) < HEAD_DIM // 2
+    return jnp.where(first, both, swapped), jnp.where(first, swapped, -both)
+
+
+def turn_table(length, step=64):
+    frequency = rotary_base ** (-2.0 * np.arange(HEAD_DIM // 2) / HEAD_DIM)
+    coarse = np.arange(length // step)[:, None] * step * frequency
+    fine = np.arange(step)[:, None] * frequency
+
+    def pair(former, latter):
+        return jnp.asarray(np.concatenate([former, latter], axis=1), jnp.float32)
+
+    table = (
+        pair(np.cos(coarse), np.sin(coarse))[:, None, :] * pair(np.cos(fine), np.cos(fine))[None]
+        + pair(-np.sin(coarse), np.cos(coarse))[:, None, :] * pair(np.sin(fine), np.sin(fine))[None]
+    )
+    return table.reshape(length, HEAD_DIM)
 
 
 LINK_RATE = {"core": 300e3, "x": 49e3, "y": 49e3, "z": 49e3}
@@ -483,6 +430,19 @@
         return carry
 
     lax.fori_loop(0, result.shape[0] // step, turn, 0)
+
+
+def weight_copies(whole, part, seq, semaphores, first):
+    width = part.shape[1] // 3
+    depth = whole.shape[1] // 3
+    return [
+        pltpu.make_async_copy(
+            whole.at[:, pl.ds(pl.multiple_of(kind * depth + seq * width, HEAD_DIM), width)],
+            part.at[:, pl.ds(kind * width, width)],
+            semaphores.at[first + kind],
+        )
+        for kind in range(3)
+    ]
 
 
 class Chunk:
@@ -867,7 +827,7 @@
     gate_ref,
     up_ref,
     out_ref,
-    w_ref,
+    w_hbm,
     mix_ref,
     log_ref,
     table_ref,
@@ -877,6 +837,7 @@
     sum_out,
     sum_qkv,
     sum_first,
+    w_ref,
     q,
     k,
     v,
@@ -937,17 +898,11 @@
         pltpu.make_async_copy(k_hbm, k, local.at[2]),
         pltpu.make_async_copy(v_hbm, v, local.at[3]),
         pltpu.make_async_copy(memory_hbm, shared, local.at[4]),
-    ]
+    ] + weight_copies(w_hbm, w_ref, seq, local, 6)
     load_every = pltpu.make_async_copy(every_hbm, shared, local.at[5])
 
-    def tables(rows):
-        both = table_ref[rows, :]
-        swapped = pltpu.roll(both, HEAD_DIM // 2, 1)
-        first = lax.broadcasted_iota(jnp.int32, both.shape, 1) < HEAD_DIM // 2
-        return jnp.where(first, both, swapped), jnp.where(first, swapped, -both)
-
     def turn_back(matrix, rows):
-        cosine, sine = tables(rows)
+        cosine, sine = turn_factors(table_ref[rows, :])
         return turn_block(matrix, cosine, sine).astype(jnp.bfloat16)
 
     def memory_part(head, block):
@@ -957,7 +912,7 @@
             grads.astype(jnp.float32) * mix_ref[rows, mine].astype(jnp.float32), axis=1, keepdims=True
         )
         delta[...] = jnp.broadcast_to(row_delta, delta.shape)
-        closed = (1 - flag_ref[0]).astype(jnp.float32) * 1e30
+        closed = (1 - flag_ref[lax.axis_index("seg")]).astype(jnp.float32) * 1e30
         log_total = log_ref[rows, mine][:, :1] + closed
         result = jnp.zeros(total.shape, jnp.float32)
         for slot in range(shared.shape[0]):
@@ -1105,7 +1060,9 @@
         copy.wait_send()
 
 
-def back(flag, grads, queries, keys, values, memory, every, terms, w_heads, attended, log_totals, table, collective_id):
+def back(
+    flags, grads, queries, keys, values, memory, every, terms, w_qkv, attended, log_totals, table, collective_id
+):
     tokens, depth = grads.shape
     length, width = queries.shape
     low = jnp.bfloat16
@@ -1122,17 +1079,18 @@
     anywhere = pl.BlockSpec(memory_space=pl.ANY)
     inside = pl.BlockSpec(memory_space=pltpu.VMEM)
     scratch = (
-        [pltpu.VMEM((length, width), low)] * 4
+        [pltpu.VMEM((depth, 3 * width), low)]
+        + [pltpu.VMEM((length, width), low)] * 4
         + [pltpu.VMEM((4, tokens, depth), low)]
         + [pltpu.VMEM((length, HEAD_DIM), jnp.float32)] * 2
         + [pltpu.VMEM((tokens, HEAD_DIM), jnp.float32)] * 2
         + [pltpu.VMEM((2, 2, 2, rows, 3 * width), low)]
         + [pltpu.SemaphoreType.DMA((3,))] * 2
-        + [pltpu.SemaphoreType.DMA((6,))]
+        + [pltpu.SemaphoreType.DMA((9,))]
     )
     return pl.pallas_call(
         functools.partial(back_kernel, chunks, first_chunks, width // HEAD_DIM),
-        in_specs=[pl.BlockSpec(memory_space=pltpu.SMEM)] + [anywhere] * 10 + [inside] * 4,
+        in_specs=[pl.BlockSpec(memory_space=pltpu.SMEM)] + [anywhere] * 11 + [inside] * 3,
         out_specs=[anywhere] * len(shapes),
         out_shape=[jax.ShapeDtypeStruct(shape, low) for shape in shapes],
         scratch_shapes=scratch + [ref for chunk in chunks + first_chunks for ref in chunk.scratch()],
@@ -1141,7 +1099,7 @@
         ),
         name="back",
     )(
-        flag,
+        flags,
         grads,
         queries,
         keys,
@@ -1149,7 +1107,7 @@
         memory,
         every,
         *[term.reshape((2, 2, 2, term.shape[0] // 8, term.shape[1])) for term in terms],
-        w_heads,
+        w_qkv,
         attended,
         log_totals,
         table,
@@ -1157,13 +1115,13 @@
 
 
 class Line:
-    def __init__(self, place, seg, slab, memory, runs, refs):
-        self.place, self.seg, self.slab, self.memory, self.runs = place, seg, slab, memory, runs
+    def __init__(self, place, seg, memory, spans, refs):
+        self.place, self.seg, self.memory, self.spans = place, seg, memory, spans
+        self.runs = len(spans)
         self.sent, self.received, self.core_sent, self.core_received = refs
-        self.rows = slab.shape[0] // runs
 
     def span(self, run):
-        return pl.ds(run * self.rows, self.rows)
+        return self.spans[run]
 
     def there(self, way, step):
         return self.place.z >= step if way == 0 else self.place.z + step <= 3
@@ -1181,7 +1139,7 @@
         slot = (way * 3 + step - 1) * self.runs + run
         seg, seq = lax.axis_index("seg"), lax.axis_index("seq")
         return pltpu.make_async_remote_copy(
-            src_ref=self.slab.at[self.span(run), :] if step == 1 else target,
+            src_ref=target,
             dst_ref=target,
             send_sem=self.sent.at[slot],
             recv_sem=self.received.at[slot],
@@ -1206,7 +1164,7 @@
         target = self.memory.at[name, self.span(run), :]
         slot = (way * 3 + step) * self.runs + run
         return pltpu.make_async_remote_copy(
-            src_ref=self.slab.at[self.span(run), :] if step == 0 else target,
+            src_ref=target,
             dst_ref=target,
             send_sem=self.core_sent.at[slot],
             recv_sem=self.core_received.at[slot],
@@ -1214,16 +1172,14 @@
             device_id_type=pl.DeviceIdType.MESH,
         )
 
-    def start(self):
-        for run in range(self.runs):
-            for way in range(2):
-
-                @pl.when(self.goes(way, 1))
-                def _(way=way, run=run):
-                    self.hop(way, 1, run).start()
-
-        for run in range(self.runs):
-            self.share(0, 0, run).start()
+    def start(self, run):
+        for way in range(2):
+
+            @pl.when(self.goes(way, 1))
+            def _(way=way):
+                self.hop(way, 1, run).start()
+
+        self.share(0, 0, run).start()
 
     def advance(self, step, run):
         for way in range(2):
@@ -1259,22 +1215,28 @@
 
 def front_kernel(
     heads,
+    flag_ref,
+    source_ref,
     x_ref,
     mem_k_ref,
     mem_v_ref,
-    w_ref,
-    cos_ref,
-    sin_ref,
+    w_hbm,
+    table_ref,
     every_ref,
-    memory_ref,
+    chosen_ref,
+    attended_ref,
     q_ref,
     k_ref,
     v_ref,
+    low_ref,
+    log_ref,
+    w_ref,
+    rows,
+    memory,
+    listed,
     mix_ref,
     max_ref,
     sum_ref,
-    rows,
-    slab,
     trade_sent,
     trade_received,
     rows_sent,
@@ -1283,6 +1245,8 @@
     line_received,
     core_sent,
     core_received,
+    back_sent,
+    back_received,
     local,
 ):
     place = Place()
@@ -1308,29 +1272,34 @@
     def seat(owner):
         return pl.ds(pl.multiple_of(owner * count, 16), count)
 
-    trades, arrivals = [], []
-    for number, peer in enumerate(("x", "y", "xy")):
+    def owner_at(turn):
+        low, high = lax.rem(turn, 2), lax.div(turn, 2)
+        x = place.x + low - 2 * place.x * low
+        y = place.y + high - 2 * place.y * high
+        return 2 * y + x
+
+    def block_rows(block):
+        return pl.ds(pl.multiple_of(block * tokens, 16), tokens)
+
+    peers = ("x", "y", "xy")
+    trades = []
+    for number, peer in enumerate(peers):
         for kind, source in enumerate((mem_k_ref, mem_v_ref)):
             lanes = pl.ds(kind * width, width)
             trades.append(
                 remote(
                     source.at[:, columns(across[peer])],
-                    slab.at[seat(seq), lanes],
+                    memory.at[seg, seat(seq), lanes],
                     trade_sent,
                     trade_received,
                     2 * number + kind,
                     peer,
                 )
             )
-
-    def trade_arrivals():
-        for copy in trades:
-            copy.wait_recv()
-
     keeps = [
         pltpu.make_async_copy(
             source.at[:, columns(seq)],
-            slab.at[seat(seq), pl.ds(kind * width, width)],
+            memory.at[seg, seat(seq), pl.ds(kind * width, width)],
             local.at[kind],
         )
         for kind, source in enumerate((mem_k_ref, mem_v_ref))
@@ -1338,6 +1307,7 @@
     half = depth // 2
     left, right = pl.ds(0, half), pl.ds(half, half)
     load = pltpu.make_async_copy(x_ref, rows.at[seq], local.at[2])
+    loads = weight_copies(w_hbm, w_ref, seq, local, 3)
     direct = [
         remote(x_ref.at[:, left], rows.at[seq, :, left], rows_sent, rows_received, 0, "x"),
         remote(x_ref.at[:, right], rows.at[seq, :, right], rows_sent, rows_received, 1, "y"),
@@ -1353,47 +1323,100 @@
         ),
     ]
     line = Line(
-        place, seg, slab, memory_ref, 2, (line_sent, line_received, core_sent, core_received)
-    )
-    keep_slab = pltpu.make_async_copy(slab, memory_ref.at[seg], local.at[3])
-    keep_rows = pltpu.make_async_copy(rows, every_ref, local.at[4])
+        place,
+        seg,
+        memory,
+        [seat(owner) for owner in (seq, across["x"], across["y"], across["xy"])],
+        (line_sent, line_received, core_sent, core_received),
+    )
+    keep_rows = pltpu.make_async_copy(rows, every_ref, local.at[6])
+    run_rows = memory.shape[1] // 2
+    keep_chosen = []
+    for run in range(2):
+        span, lanes = pl.ds(run * run_rows, run_rows), pl.ds(2 * run * width, 2 * width)
+        keep_chosen.append(
+            pltpu.make_async_copy(memory.at[seg, span, :], chosen_ref.at[0, :, lanes], local.at[7 + run])
+        )
+        keep_chosen.append(
+            pltpu.make_async_copy(
+                listed.at[:, span, :],
+                chosen_ref.at[pl.ds(1, listed.shape[0]), :, lanes],
+                local.at[9 + run],
+            )
+        )
+    returns = [
+        remote(
+            low_ref.at[block_rows(across[peer]), :],
+            attended_ref.at[:, columns(seq)],
+            back_sent,
+            back_received,
+            slot,
+            peer,
+        )
+        for slot, peer in enumerate(peers)
+    ]
+    keep_attended = pltpu.make_async_copy(
+        low_ref.at[block_rows(seq), :], attended_ref.at[:, columns(seq)], local.at[11]
+    )
 
     def project_rows(owner):
         block = rows[owner]
-        span = pl.ds(pl.multiple_of(owner * tokens, 16), tokens)
-        cosine, sine = cos_ref[span, :], sin_ref[span, :]
+        span = block_rows(owner)
+        cosine, sine = turn_factors(table_ref[span, :])
         scale = SCORE_SCALE / LN2
         queries = product(block, w_ref[:, :width])
         keys = product(block, w_ref[:, width : 2 * width])
         for head in range(heads):
             lanes = slice(head * HEAD_DIM, (head + 1) * HEAD_DIM)
-            q_ref[span, lanes] = turn_block(queries[:, lanes], cosine * scale, sine * scale).astype(
-                jnp.bfloat16
-            )
-            k_ref[span, lanes] = turn_block(keys[:, lanes], cosine, sine).astype(jnp.bfloat16)
+            q_ref[span, lanes] = turn_block(
+                queries[:, lanes], cosine * scale, sine * (-scale)
+            ).astype(jnp.bfloat16)
+            k_ref[span, lanes] = turn_block(keys[:, lanes], cosine, -sine).astype(jnp.bfloat16)
         v_ref[span, :] = product(block, w_ref[:, 2 * width :]).astype(jnp.bfloat16)
+
+    def head_lanes(head, start=0):
+        return pl.ds(pl.multiple_of(start + head * HEAD_DIM, HEAD_DIM), HEAD_DIM)
+
+    def keep(span, lanes, row_max, row_sum, mixed):
+        mix_ref[span, lanes] = mixed
+        max_ref[span, lanes] = jnp.broadcast_to(row_max, mixed.shape)
+        sum_ref[span, lanes] = jnp.broadcast_to(row_sum, mixed.shape)
 
     def own_rows(block):
         def turn(head, carry):
-            lanes = pl.ds(pl.multiple_of(head * HEAD_DIM, HEAD_DIM), HEAD_DIM)
+            lanes = head_lanes(head)
             span = pl.ds(block * tokens, tokens)
             pairs = [
                 (k_ref[pl.ds(n * tokens, tokens), lanes], v_ref[pl.ds(n * tokens, tokens), lanes])
                 for n in range(block + 1)
             ]
-            row_max, row_sum, mixed = attend(q_ref[span, lanes], pairs, True, None)
-            mix_ref[span, lanes] = mixed
-            max_ref[span, lanes] = jnp.broadcast_to(row_max, mixed.shape)
-            sum_ref[span, lanes] = jnp.broadcast_to(row_sum, mixed.shape)
+            keep(span, lanes, *attend(q_ref[span, lanes], pairs, True, None))
             return carry
 
         lax.fori_loop(0, heads, turn, 0)
+
+    closed = (1 - flag_ref[seg]).astype(jnp.float32) * 1e30
+
+    def carried(span, lanes):
+        return max_ref[span, lanes][:, :1], sum_ref[span, lanes][:, :1], mix_ref[span, lanes]
+
+    def own_memory(first, last):
+        def turn(index, carry):
+            head = lax.rem(index, heads)
+            lanes, span = head_lanes(head), block_rows(lax.div(index, heads))
+            pair = (memory[seg, :, lanes], memory[seg, :, head_lanes(head, width)])
+            keep(span, lanes, *attend(q_ref[span, lanes], [pair], False, carried(span, lanes), closed))
+            return carry
+
+        lax.fori_loop(first * heads, last * heads, turn, 0)
 
     barrier = pltpu.get_barrier_semaphore()
 
     def hail(device):
         pl.semaphore_signal(barrier, inc=1, device_id=device, device_id_type=pl.DeviceIdType.MESH)
 
+    for copy in keeps + [load] + loads:
+        copy.start()
     for peer in ("x", "y", "xy", "core"):
         hail(place.peer[peer])
     below, above = place.z >= 1, place.z <= 2
@@ -1408,85 +1431,129 @@
 
     pl.semaphore_wait(barrier, 4 + below.astype(jnp.int32) + above.astype(jnp.int32))
 
-    for copy in keeps + trades:
+    for copy in trades + direct:
         copy.start()
-    load.start()
-    for copy in direct:
-        copy.start()
-    load.wait()
-    project_rows(seq)
     for copy in keeps:
         copy.wait()
-    trade_arrivals()
-    line.start()
-    keep_slab.start()
+    line.start(0)
+    load.wait()
+    for copy in loads:
+        copy.wait()
+    project_rows(seq)
+    for number in range(3):
+        for kind in range(2):
+            trades[2 * number + kind].wait_recv()
+        line.start(number + 1)
+        line.advance(1, number)
     direct[0].wait_recv()
     direct[1].wait_recv()
     for copy in onward:
         copy.start()
-    line.advance(1, 0)
+    line.advance(1, 3)
+    line.advance(2, 0)
     direct[2].wait_recv()
     direct[3].wait_recv()
     project_rows(across["x"])
-    line.advance(1, 1)
+    line.advance(2, 1)
     project_rows(across["y"])
+    line.advance(2, 2)
     for copy in onward:
         copy.wait_recv()
     project_rows(3 - seq)
     keep_rows.start()
-    line.advance(2, 0)
+    line.advance(2, 3)
     own_rows(0)
     own_rows(1)
-    line.advance(2, 1)
+    line.advance(3, 0)
     own_rows(2)
+    line.advance(3, 1)
     own_rows(3)
-    line.advance(3, 0)
-    line.advance(3, 1)
-    keep_slab.wait()
-    keep_rows.wait()
+    line.advance(3, 2)
+    own_memory(0, 2)
+    line.advance(3, 3)
+    own_memory(2, 4)
+    line.finish()
+    for n in range(listed.shape[0]):
+        listed[n] = memory[source_ref[seg, n]]
+
+    def unit(index, carry):
+        turn, head = lax.div(index, heads), lax.rem(index, heads)
+
+        @pl.when(index == heads // 2)
+        def _():
+            for copy in keep_chosen:
+                copy.start()
+
+        for number in range(3):
+
+            @pl.when(index == heads * (3 - number))
+            def _(number=number):
+                returns[number].start()
+
+        lanes, span = head_lanes(head), block_rows(owner_at(3 - turn))
+        pairs = [
+            (listed[n, :, lanes], listed[n, :, head_lanes(head, width)])
+            for n in range(listed.shape[0])
+        ]
+        row_max, row_sum, mixed = attend(
+            q_ref[span, lanes], pairs, False, carried(span, lanes), closed
+        )
+        low_ref[span, lanes] = (mixed * (1.0 / row_sum)).astype(jnp.bfloat16)
+        log_ref[span, lanes] = jnp.broadcast_to(row_max + jnp.log2(row_sum), mixed.shape)
+        return carry
+
+    lax.fori_loop(0, 4 * heads, unit, 0)
+    keep_attended.start()
+    for copy in returns:
+        copy.wait()
+    for copy in keep_chosen + [keep_rows, keep_attended]:
+        copy.wait()
     for copy in trades + direct + onward:
         copy.wait_send()
-    line.finish()
-
-
-def front(first_low, mem_keys, mem_values, w_heads, cosine, sine, seg_size, seq_size, collective_id):
+
+
+def front(
+    flags, sources, first_low, mem_keys, mem_values, w_qkv, table, seg_size, seq_size, collective_id
+):
     tokens, depth = first_low.shape
     length = tokens * seq_size
-    width = w_heads.shape[1] // 3
-    count = mem_keys.shape[0]
+    width = depth // seq_size
+    count = mem_keys.shape[0] * seq_size
+    slots = sources.shape[1]
     anywhere = pl.BlockSpec(memory_space=pl.ANY)
     inside = pl.BlockSpec(memory_space=pltpu.VMEM)
+    scalars = pl.BlockSpec(memory_space=pltpu.SMEM)
     low = jnp.bfloat16
     shape = jax.ShapeDtypeStruct
     dma = pltpu.SemaphoreType.DMA
     return pl.pallas_call(
         functools.partial(front_kernel, width // HEAD_DIM),
-        in_specs=[anywhere] * 3 + [inside] * 3,
-        out_specs=[anywhere] * 2 + [inside] * 6,
+        in_specs=[scalars] * 2 + [anywhere] * 4 + [inside],
+        out_specs=[anywhere] * 3 + [inside] * 5,
         out_shape=[
             shape((seq_size, tokens, depth), low),
-            shape((seg_size, count * seq_size, 2 * width), low),
+            shape((slots + 1, count // 2, 4 * width), low),
+            shape((tokens, depth), low),
         ]
-        + [shape((length, width), low)] * 3
-        + [shape((length, width), jnp.float32)] * 3,
+        + [shape((length, width), low)] * 4
+        + [shape((length, width), jnp.float32)],
         scratch_shapes=[
+            pltpu.VMEM((depth, 3 * width), low),
             pltpu.VMEM((seq_size, tokens, depth), low),
-            pltpu.VMEM((count * seq_size, 2 * width), low),
-            dma((6,)),
-            dma((6,)),
-            dma((6,)),
-            dma((6,)),
-            dma((12,)),
-            dma((12,)),
-            dma((16,)),
-            dma((16,)),
-            dma((5,)),
-        ],
+            pltpu.VMEM((seg_size, count, 2 * width), low),
+            pltpu.VMEM((slots, count, 2 * width), low),
+        ]
+        + [pltpu.VMEM((length, width), jnp.float32)] * 3
+        + [dma((6,))] * 4
+        + [dma((24,))] * 2
+        + [dma((28,))] * 2
+        + [dma((3,))] * 2
+        + [dma((12,))],
         compiler_params=pltpu.CompilerParams(
             collective_id=collective_id, has_side_effects=True, vmem_limit_bytes=VMEM_BYTES
         ),
         name="front",
-    )(first_low, mem_keys, mem_values, w_heads, cosine, sine)
+    )(flags, sources, first_low, mem_keys, mem_values, w_qkv, table)
 
 
 def norm_input_grad(values, inverse, norm_gain, upstream):
@@ -1512,33 +1579,17 @@
     memory_flags,
     sources,
 ):
-    seg_index = lax.axis_index("seg")
     seq_index = lax.axis_index("seq")
     tokens = layer_input.shape[1]
     length = tokens * seq_size
     width = D // seq_size
-    flag = lax.dynamic_index_in_dim(memory_flags, seg_index, 0, keepdims=True)
-    listed = lax.dynamic_index_in_dim(sources, seg_index, 0, keepdims=False)
-    chosen = jnp.concatenate([jnp.reshape(seg_index, (1,)), listed, flag]).astype(jnp.int32)
-
     inputs = layer_input[0].astype(jnp.float32)
     first_norm, first_inverse = norm_forward(inputs, norm1_gain)
     first_low = first_norm.astype(jnp.bfloat16)
-    w_heads = lax.dynamic_index_in_dim(
-        w_qkv.reshape(D, 3, seq_size, width), seq_index, 2, keepdims=False
-    ).reshape(D, 3 * width)
-    cosine, sine = turn_tables(lax.iota(jnp.int32, length).astype(jnp.float32))
-    cosine, sine = cosine[:, 0, :], sine[:, 0, :]
-    table = jnp.concatenate([cosine[:, : HEAD_DIM // 2], sine[:, : HEAD_DIM // 2]], axis=1)
-    first_half = lax.broadcasted_iota(jnp.int32, sine.shape, 1) < HEAD_DIM // 2
-    sine = jnp.where(first_half, -sine, sine)
-    every_low, memory, queries, keys, values, mixed, row_max, row_sum = front(
-        first_low, mem_keys[0], mem_values[0], w_heads, cosine, sine, seg_size, seq_size, 1
-    )
-    heads_low, chosen_memory, log_totals = memory_forward(
-        chosen, queries, mixed, row_max, row_sum, memory
-    )
-    attended_low = lax.all_to_all(heads_low, "seq", 0, 1, tiled=True)
+    table = turn_table(length)
+    every_low, chosen_memory, attended_low, queries, keys, values, heads_low, log_totals = front(
+        memory_flags, sources, first_low, mem_keys[0], mem_values[0], w_qkv, table, seg_size, seq_size, 1
+    )
 
     residual = inputs + product(attended_low, w_out)
     second_norm, second_inverse = norm_forward(residual, norm2_gain)
@@ -1566,7 +1617,7 @@
     term_out = product_tn(attended_low, residual_low).astype(low)
     grad_attended = product_nt(residual_low, w_out).astype(low)
     *sums, qkv_rows, first_rows = back(
-        flag.astype(jnp.int32),
+        memory_flags,
         grad_attended,
         queries,
         keys,
@@ -1574,7 +1625,7 @@
         chosen_memory,
         every_low,
         [term_down, term_gate, term_up, term_out],
-        w_heads,
+        w_qkv,
         heads_low,
         log_totals,
         table,

time: 424 us -> 371 us (0.88)
  Pallas kernels: 297 us -> 277 us
  local copies, waits for them, and re-layouts: 16.8 us -> 2.27 us
  waiting for transfers between devices: 8.11 us -> 0 us
  starting transfers between devices: 4.49 us -> 0 us
    pallas_call x1, Pallas kernels: 190 us -> 163 us  [back(): pl.pallas_call(functools.partial(back_kernel, chunks, first_chunks, width...]
    pallas_call x1, Pallas kernels: 94.6 us -> 114 us  [front(): pl.pallas_call(functools.partial(front_kernel, width // HEAD_DIM), in_spe...]
    pallas_call x1 -> x0, Pallas kernels: 12.4 us -> none  [memory_forward(): pl.pallas_call(functools.partial(memory_forward_kernel, count), grid_spec...]
    all_to_all x1 -> x0, waiting for transfers between devices: 8.11 us -> none  [head_plan(): attended_low = lax.all_to_all(heads_low, 'seq', 0, 1, tiled=True)]
    unnamed x53 -> x51, local copies, waits for them, and re-layouts: 9.17 us -> 2.27 us
    sin x1 -> x0, other arithmetic: 4.88 us -> none  [turn_tables(): return (jnp.cos(angles)[:, None, :], jnp.sin(angles)[:, None, :])]
    all_to_all x1 -> x0, starting transfers between devices: 4.49 us -> none  [head_plan(): attended_low = lax.all_to_all(heads_low, 'seq', 0, 1, tiled=True)]
  transfers between devices with their start and end apart: 1 -> 0, of which waited for: 1 -> 0; matrix products, arithmetic and copies ran while one was open for 0% -> 0% of each run, Pallas kernels for 0% -> 0%
where the time goes in v2:
time: 371 us; the launch traced here: 367 us
  Pallas kernels  277 us (75%)
  matrix products  59.4 us (16%)
  other arithmetic  26.6 us (7%)
    pallas_call x1, Pallas kernels, back(): pl.pallas_call(functools.partial(back_kernel, chunks, first_chunks, width...  163 us
    pallas_call x1, Pallas kernels, front(): pl.pallas_call(functools.partial(front_kernel, width // HEAD_DIM), in_spe...  114 us
    dot_general x4, matrix products, product_nt(): lax.dot_general(former, latter, (((1,), (1,)), ((), ())), preferred_eleme...  21 us
    dot_general x4, matrix products, product(): return jnp.dot(former, latter, preferred_element_type=jnp.float32)  20.5 us
    dot_general x4, matrix products, product_tn(): lax.dot_general(former, latter, (((0,), (0,)), ((), ())), preferred_eleme...  17.9 us
    reduce_sum x2, other arithmetic, gain_rows(): jnp.sum(row_block(weight).astype(jnp.float32) * grad, axis=1)  8.62 us

profile of v2, /device:TPU:0, one launch (start us, length us, event | category | flops | bytes accessed | tf_op | source)
XLA Modules:
  0.0 366.5 jit_solution(37609688068565100)
XLA Ops:
  0.7 1.4 copy.26.source_ref
  2.1 1.5 fusion.1
  3.6 0.6 multiply_multiply_fusion
  4.1 2.5 fusion.3.x_ref
  6.6 1.1 multiply_add_fusion
  7.8 114.1 %front.1 = (bf16[4,512,1024]{2,1,0:T(8,128)(2,1)}, bf16[4,512,1024]{2,1,0:T(8,128)(2,1)}, bf16[512,1024]{1,0:T(8,128)(2,1)}, bf16[2048,256]{1,0:T(8,128)(2,1)}, ...) custom-call(s32[8]{0:T(128)} %flag_ref.3, ...), custom_call_target="tpu_custom_call" | custom-call | tf_op jit(solution)/shard_map/front/pallas_call | solution.py:1529
  121.9 0.0 slice-start.1
  121.9 2.7 multiply_reduce_fusion.4
  124.7 0.2 multiply_convert_fusion.3
  125.0 5.0 %fusion.15 = f32[512,2816]{1,0:T(8,128)} fusion(bf16[512,1024]{1,0:T(8,128)(2,1)S(1)} %multiply_convert_fusion.3, bf16[1024,2816]{1,0:T(8,128)(2,1)S(1)} %bitcast.73), kind=kOutput, calls=%fused_computation.53 | convolution fusion | flops 2952790016 | bytes 12582912 | tf_op jit(solution)/shard_map/dot_general | solution.py:23
  130.0 5.0 %fusion.16 = f32[512,2816]{1,0:T(8,128)} fusion(bf16[512,1024]{1,0:T(8,128)(2,1)S(1)} %multiply_convert_fusion.3, bf16[1024,2816]{1,0:T(8,128)(2,1)S(1)} %bitcast.75), kind=kOutput, calls=%fused_computation.54 | convolution fusion | flops 2952790016 | bytes 12582912 | tf_op jit(solution)/shard_map/dot_general | solution.py:23
  135.0 12.2 %multiply_convert_fusion = (bf16[512,2816]{1,0:T(8,128)(2,1)}, bf16[512,2816]{1,0:T(8,128)(2,1)}, bf16[512,2816]{1,0:T(8,128)(2,1)}) fusion(f32[512,2816]{1,0:T(8,128)} %fusion.15, f32[512,2816]{1,0:T(8,128)} %fusion.16, bf16[2816,1024]{1,0:T(8,128)(2,1)} %param.25, bf16[1,512,1024]{2,1,0:T(8,128)(2,1)S(1)} %copy-done.7), kind=kOutput, calls=%fused_computation | convolution fusion | flops 2974416896 | bytes 27000832 | tf_op jit(solution)/shard_map/dot_general | solution.py:27
  147.2 7.8 %fusion.9 = bf16[1,512,1024]{2,1,0:T(8,128)(2,1)} fusion(f32[512,1024]{1,0:T(8,128)S(1)} %get-tuple-element.51, bf16[512,2816]{1,0:T(8,128)(2,1)} %get-tuple-element.45, bf16[2816,1024]{1,0:T(8,128)(2,1)} %param.25), kind=kOutput, calls=%fused_computation.37 | convolution fusion | flops 2953838592 | bytes 11796480 | tf_op jit(solution)/shard_map/dot_general | solution.py:23
  155.0 3.2 fusion.17
  158.2 3.4 multiply_reduce_fusion.3
  161.5 0.6 convert_add_fusion.1
  162.1 2.3 convolution_convert_fusion.4.g_ref
  164.4 0.7 copy-done.18
  165.1 5.0 %convolution_convert_fusion.2 = bf16[2816,1024]{1,0:T(8,128)(2,1)} fusion(bf16[512,2816]{1,0:T(8,128)(2,1)S(1)} %copy-done.18, bf16[1,512,1024]{2,1,0:T(8,128)(2,1)S(1)} %copy-done.7), kind=kOutput, calls=%fused_computation.7 | convolution fusion | flops 2955673600 | bytes 9699328 | tf_op jit(solution)/shard_map/dot_general | solution.py:33
  170.1 5.1 %convolution_convert_fusion.1 = bf16[1024,2816]{1,0:T(8,128)(2,1)} fusion(bf16[512,1024]{1,0:T(8,128)(2,1)S(1)} %multiply_convert_fusion.3, bf16[512,2816]{1,0:T(8,128)(2,1)S(1)} %copy-done.20), kind=kOutput, calls=%fused_computation.6 | convolution fusion | flops 2955673600 | bytes 9699328 | tf_op jit(solution)/shard_map/dot_general | solution.py:33
  175.2 5.1 %convolution_convert_fusion = bf16[1024,2816]{1,0:T(8,128)(2,1)} fusion(bf16[512,1024]{1,0:T(8,128)(2,1)S(1)} %multiply_convert_fusion.3, bf16[512,2816]{1,0:T(8,128)(2,1)S(1)} %copy-done.17), kind=kOutput, calls=%fused_computation.5 | convolution fusion | flops 2955673600 | bytes 9699328 | tf_op jit(solution)/shard_map/dot_general | solution.py:33
  180.4 2.6 convolution_convert_fusion.3
  183.0 163.0 %back.1 = (bf16[2,352,1024]{2,1,0:T(8,128)(2,1)}, bf16[2,128,2816]{2,1,0:T(8,128)(2,1)}, bf16[2,128,2816]{2,1,0:T(8,128)(2,1)}, bf16[2,128,1024]{2,1,0:T(8,128)(...) custom-call(s32[8]{0:T(128)} %flag_ref.3, bf16[512,1024]{1,0:T(8,128)(2,1)} %convolution_convert_fusion.4.g_ref, ...), custom_call_target="tpu_custom_call" | custom-call | tf_op jit(solution)/shard_map/back/pallas_call | solution.py:1091
  346.0 2.1 fusion.8
  348.1 0.1 copy-done.2
  348.2 3.6 fusion.7
  351.9 3.6 multiply_reduce_fusion
  355.5 1.3 dynamic-slice_divide_fusion.1
  356.8 5.0 %multiply_reduce_fusion.1 = (f32[256]{0:T(256)S(1)}, f32[256,2816]{1,0:T(8,128)}, f32[256]{0:T(256)S(1)}, f32[256,2816]{1,0:T(8,128)}) fusion(bf16[1024,2816]{1,0:T(8,128)(2,1)} %param.24, s32[]{:T(128)S(6)} %select_n.2, bf16[2,128,2816]{2,1,0:T(8,128)(2,1)S(1)} %copy-done.5, bf16[2,128,2816]{2,1,0:T(8,128)(2,1)S(1)} %copy-done.4, bf16[1024,2816]{1,0:T(8,128)(2,1)} %param.23), kind=kLoop, calls=%fused_computation.14 | loop fusion | flops 5766656 | bytes 11536388 | tf_op jit(solution)/shard_map/reduce_sum | solution.py:1648
  361.8 1.3 dynamic-slice_divide_fusion
  363.1 1.1 bitcast_convert_fusion.4
  364.3 2.0 bitcast_convert_fusion.1
  (52 shorter events, 0.1 us)
Async XLA Ops:
  0.6 6.0 %copy-start.9 = (f32[64,128]{1,0:T(8,128)S(1)}, f32[64,128]{1,0:T(8,128)}, u32[]{:S(2)}) copy-start(f32[64,128]{1,0:T(8,128)} %constant.33.clone) | copy-start | bytes 98308
  0.7 6.0 %copy-start.12 = (f32[32,128]{1,0:T(8,128)S(1)}, f32[32,128]{1,0:T(8,128)}, u32[]{:S(2)}) copy-start(f32[32,128]{1,0:T(8,128)} %constant.32.clone) | copy-start | bytes 49156
  0.7 6.0 %copy-start.10 = (f32[64,128]{1,0:T(8,128)S(1)}, f32[64,128]{1,0:T(8,128)}, u32[]{:S(2)}) copy-start(f32[64,128]{1,0:T(8,128)} %constant.31.clone) | copy-start | bytes 98308
  0.7 6.0 %copy-start.13 = (f32[32,128]{1,0:T(8,128)S(1)}, f32[32,128]{1,0:T(8,128)}, u32[]{:S(2)}) copy-start(f32[32,128]{1,0:T(8,128)} %constant.30.clone) | copy-start | bytes 49156
  4.1 3.7 copy-start.11
  7.8 114.1 %copy-start = (bf16[1,512,1024]{2,1,0:T(8,128)(2,1)S(1)}, bf16[1,512,1024]{2,1,0:T(8,128)(2,1)}, u32[]{:S(2)}) copy-start(bf16[1,512,1024]{2,1,0:T(8,128)(2,1)} %param.17) | copy-start | bytes 3145732
  7.8 114.1 %copy-start.15 = (bf16[1024,1024]{1,0:T(8,128)(2,1)S(1)}, bf16[1024,1024]{1,0:T(8,128)(2,1)}, u32[]{:S(2)}) copy-start(bf16[1024,1024]{1,0:T(8,128)(2,1)} %param.22) | copy-start | bytes 6291460
  121.9 3.1 slice-start
  121.9 2.8 copy-start.14
  121.9 3.0 slice-start.1
  124.7 5.3 %slice-start.2 = ((s8[5767168]{0:T(1024)(128)(4,1)}), s8[4194304]{0:T(1024)(128)(4,1)S(1)}, s32[]{:S(2)}) async-start(s8[5767168]{0:T(1024)(128)(4,1)} %bitcast.74), calls=%async_computation.2 | async-start | bytes 8388608
  125.0 5.0 %slice-start.3 = ((s8[5767168]{0:T(1024)(128)(4,1)}), s8[1572864]{0:T(1024)(128)(4,1)S(1)}, s32[]{:S(2)}) async-start(s8[5767168]{0:T(1024)(128)(4,1)} %bitcast.74), calls=%async_computation.3 | async-start | bytes 3145728
  130.0 5.0 %copy-start.7 = (bf16[1,512,1024]{2,1,0:T(8,128)(2,1)S(1)}, bf16[1,512,1024]{2,1,0:T(8,128)(2,1)}, u32[]{:S(2)}) copy-start(bf16[1,512,1024]{2,1,0:T(8,128)(2,1)} %param.18) | copy-start | bytes 3145732
  147.2 7.8 %copy-start.19 = (bf16[512,2816]{1,0:T(8,128)(2,1)S(1)}, bf16[512,2816]{1,0:T(8,128)(2,1)}, u32[]{:S(2)}) copy-start(bf16[512,2816]{1,0:T(8,128)(2,1)} %get-tuple-element.44) | copy-start | bytes 8650756
  155.0 3.2 copy-start.17
  162.1 18.2 %copy-start.1 = (f32[512,1024]{1,0:T(8,128)}, f32[512,1024]{1,0:T(8,128)S(1)}, u32[]{:S(2)}) copy-start(f32[512,1024]{1,0:T(8,128)S(1)} %convert_add_fusion.1) | copy-start | bytes 6291460
  162.1 3.0 copy-start.18
  165.1 5.0 %copy-start.20 = (bf16[512,2816]{1,0:T(8,128)(2,1)S(1)}, bf16[512,2816]{1,0:T(8,128)(2,1)}, u32[]{:S(2)}) copy-start(bf16[512,2816]{1,0:T(8,128)(2,1)} %get-tuple-element.44) | copy-start | bytes 8650756
  175.2 5.2 %copy-start.16 = (bf16[512,1024]{1,0:T(8,128)(2,1)S(1)}, bf16[512,1024]{1,0:T(8,128)(2,1)}, u32[]{:S(2)}) copy-start(bf16[512,1024]{1,0:T(8,128)(2,1)} %get-tuple-element.23) | copy-start | bytes 3145732
  346.0 2.2 copy-start.2
  348.2 3.6 copy-start.3
  351.8 5.0 %copy-start.4 = (bf16[2,128,2816]{2,1,0:T(8,128)(2,1)S(1)}, bf16[2,128,2816]{2,1,0:T(8,128)(2,1)}, u32[]{:S(2)}) copy-start(bf16[2,128,2816]{2,1,0:T(8,128)(2,1)} %get-tuple-element.33) | copy-start | bytes 4325380
  351.8 5.0 %copy-start.5 = (bf16[2,128,2816]{2,1,0:T(8,128)(2,1)S(1)}, bf16[2,128,2816]{2,1,0:T(8,128)(2,1)}, u32[]{:S(2)}) copy-start(bf16[2,128,2816]{2,1,0:T(8,128)(2,1)} %get-tuple-element.34) | copy-start | bytes 4325380
  356.8 6.3 %copy-start.8 = (bf16[2,128,1024]{2,1,0:T(8,128)(2,1)S(1)}, bf16[2,128,1024]{2,1,0:T(8,128)(2,1)}, u32[]{:S(2)}) copy-start(bf16[2,128,1024]{2,1,0:T(8,128)(2,1)} %get-tuple-element.35) | copy-start | bytes 1572868
  356.8 7.5 %copy-start.6 = (bf16[2,352,1024]{2,1,0:T(8,128)(2,1)S(1)}, bf16[2,352,1024]{2,1,0:T(8,128)(2,1)}, u32[]{:S(2)}) copy-start(bf16[2,352,1024]{2,1,0:T(8,128)(2,1)} %get-tuple-element.36) | copy-start | bytes 4325380

commit v3 on v2

--- a/solution.py
+++ b/solution.py
@@ -1562,6 +1562,119 @@
     return inverse * weighted - inverse * inverse * inverse * values * inner_mean
 
 
+def dense_kernel(
+    x_ref,
+    g_ref,
+    attended_ref,
+    out_ref,
+    gain_ref,
+    gate_ref,
+    up_ref,
+    down_ref,
+    output_ref,
+    grad_ref,
+    grad_attended_ref,
+    term_down,
+    term_gate,
+    term_up,
+    term_out,
+    residual_ref,
+    second,
+    second_t,
+    total,
+    grad_second,
+):
+    index = pl.program_id(0)
+    low = jnp.bfloat16
+
+    @pl.when(index == 0)
+    def _():
+        residual = x_ref[...].astype(jnp.float32) + product(attended_ref[...], out_ref[...])
+        residual_ref[...] = residual
+        second_low = norm_forward(residual, gain_ref[...])[0].astype(low)
+        second[...] = second_low
+        second_t[...] = second_low.T
+
+    gate, up = product(second[...], gate_ref[...]), product(second[...], up_ref[...])
+    grad_hidden = product_nt(g_ref[...], down_ref[...])
+    sigmoid_gate = jax.nn.sigmoid(gate)
+    activated = gate * sigmoid_gate
+    hidden = (activated * up).astype(low)
+    grad_gate = (grad_hidden * up * sigmoid_gate * (1.0 + gate * (1.0 - sigmoid_gate))).astype(low)
+    grad_up = (grad_hidden * activated).astype(low)
+    term_down[...] = product_tn(hidden, g_ref[...]).astype(low)
+    term_gate[...] = product(second_t[...], grad_gate).astype(low)
+    term_up[...] = product(second_t[...], grad_up).astype(low)
+    part = product(hidden, down_ref[...])
+    grad_part = product_nt(grad_gate, gate_ref[...]) + product_nt(grad_up, up_ref[...])
+
+    @pl.when(index == 0)
+    def _():
+        total[...] = part
+        grad_second[...] = grad_part
+
+    @pl.when(index > 0)
+    def _():
+        total[...] += part
+        grad_second[...] += grad_part
+
+    @pl.when(index == pl.num_programs(0) - 1)
+    def _():
+        residual = residual_ref[...]
+        output_ref[...] = (residual + total[...]).astype(low)
+        inverse = lax.rsqrt(jnp.mean(residual * residual, axis=-1, keepdims=True) + epsilon)
+        grad = norm_input_grad(residual, inverse, gain_ref[...], grad_second[...])
+        grad = grad + g_ref[...].astype(jnp.float32)
+        grad_ref[...] = grad
+        grad_low = grad.astype(low)
+        term_out[...] = product_tn(attended_ref[...], grad_low).astype(low)
+        grad_attended_ref[...] = product_nt(grad_low, out_ref[...]).astype(low)
+
+
+def dense(x, grads, attended, w_out, gain, w_gate, w_up, w_down, tile=256):
+    tokens, depth = x.shape
+    hidden = w_gate.shape[1]
+    tile = math.gcd(tile, hidden)
+    low = jnp.bfloat16
+    shape = jax.ShapeDtypeStruct
+
+    def whole(rows, columns):
+        return pl.BlockSpec((rows, columns), lambda j: (0, 0))
+
+    across = pl.BlockSpec((depth, tile), lambda j: (0, j))
+    down = pl.BlockSpec((tile, depth), lambda j: (j, 0))
+    activation = whole(tokens, depth)
+    return pl.pallas_call(
+        dense_kernel,
+        grid=(hidden // tile,),
+        in_specs=[activation] * 3 + [whole(depth, depth), whole(1, depth), across, across, down],
+        out_specs=[activation] * 3 + [down, across, across, whole(depth, depth)],
+        out_shape=[
+            shape((tokens, depth), low),
+            shape((tokens, depth), jnp.float32),
+            shape((tokens, depth), low),
+            shape((hidden, depth), low),
+            shape((depth, hidden), low),
+            shape((depth, hidden), low),
+            shape((depth, depth), low),
+        ],
+        scratch_shapes=[
+            pltpu.VMEM((tokens, depth), jnp.float32),
+            pltpu.VMEM((tokens, depth), low),
+            pltpu.VMEM((depth, tokens), low),
+            pltpu.VMEM((tokens, depth), jnp.float32),
+            pltpu.VMEM((tokens, depth), jnp.float32),
+        ],
+        compiler_params=pltpu.CompilerParams(vmem_limit_bytes=VMEM_BYTES),
+        cost_estimate=pl.CostEstimate(
+            flops=16 * tokens * depth * hidden + 6 * tokens * depth * depth,
+            transcendentals=tokens * hidden,
+            bytes_accessed=12 * depth * hidden + 20 * tokens * depth,
+        ),
+        name="dense",
+    )(x, grads, attended, w_out, gain, w_gate, w_up, w_down)
+
+
 def head_plan(
     seg_size,
     seq_size,
@@ -1591,31 +1704,9 @@
         memory_flags, sources, first_low, mem_keys[0], mem_values[0], w_qkv, table, seg_size, seq_size, 1
     )
 
-    residual = inputs + product(attended_low, w_out)
-    second_norm, second_inverse = norm_forward(residual, norm2_gain)
-    second_low = second_norm.astype(jnp.bfloat16)
-    gate_values = product(second_low, w_gate)
-    up_values = product(second_low, w_up)
-    sigmoid_gate = jax.nn.sigmoid(gate_values)
-    activated = gate_values * sigmoid_gate
-    hidden_low = (activated * up_values).astype(jnp.bfloat16)
-    output = (residual + product(hidden_low, w_down)).astype(jnp.bfloat16)
-    upstream = output_grad[0]
-    low = jnp.bfloat16
-    term_down = product_tn(hidden_low, upstream).astype(low)
-    grad_hidden = product_nt(upstream, w_down)
-    grad_gate_low = (
-        grad_hidden * up_values * sigmoid_gate * (1.0 + gate_values * (1.0 - sigmoid_gate))
-    ).astype(low)
-    grad_up_low = (grad_hidden * activated).astype(low)
-    term_gate = product_tn(second_low, grad_gate_low).astype(low)
-    term_up = product_tn(second_low, grad_up_low).astype(low)
-    grad_second = product_nt(grad_gate_low, w_gate) + product_nt(grad_up_low, w_up)
-    grad_residual = norm_input_grad(residual, second_inverse, norm2_gain, grad_second)
-    grad_residual = grad_residual + upstream.astype(jnp.float32)
-    residual_low = grad_residual.astype(low)
-    term_out = product_tn(attended_low, residual_low).astype(low)
-    grad_attended = product_nt(residual_low, w_out).astype(low)
+    output, grad_residual, grad_attended, term_down, term_gate, term_up, term_out = dense(
+        layer_input[0], output_grad[0], attended_low, w_out, norm2_gain[None], w_gate, w_up, w_down
+    )
     *sums, qkv_rows, first_rows = back(
         memory_flags,
         grad_attended,

time: 371 us -> 356 us (0.960)
  matrix products: 59.4 us -> 0 us
  Pallas kernels: 277 us -> 324 us
    dot_general x12 -> x0, matrix products: 59.4 us -> none  [the longest x4 21 us: product_nt(): lax.dot_general(former, latter, (((1,), (1,)), ((), ())), preferred_eleme...]
    pallas_call x0 -> x1, Pallas kernels: none -> 46.8 us  [dense(): pl.pallas_call(dense_kernel, grid=(hidden // tile,), in_specs=[activation...]
where the time goes in v3:
time: 356 us; the launch traced here: 352 us
  Pallas kernels  324 us (91%)
  other arithmetic  25.1 us (7%)
    pallas_call x1, Pallas kernels, back(): pl.pallas_call(functools.partial(back_kernel, chunks, first_chunks, width...  164 us
    pallas_call x1, Pallas kernels, front(): pl.pallas_call(functools.partial(front_kernel, width // HEAD_DIM), in_spe...  114 us
    pallas_call x1, Pallas kernels, dense(): pl.pallas_call(dense_kernel, grid=(hidden // tile,), in_specs=[activation...  46.8 us
    reduce_sum x2, other arithmetic, gain_rows(): jnp.sum(row_block(weight).astype(jnp.float32) * grad, axis=1)  8.4 us

profile of v3, /device:TPU:0, one launch (start us, length us, event | category | flops | bytes accessed | tf_op | source)
XLA Modules:
  0.0 351.6 jit_solution(1276499702767128677)
XLA Ops:
  0.6 0.0 copy-start.8
  0.7 0.0 copy-start.12
  0.7 0.0 copy-start.9
  0.7 0.0 copy-start.13
  0.7 1.4 copy.26.source_ref
  2.1 1.5 fusion
  3.6 0.6 multiply_multiply_fusion
  4.2 2.5 fusion.2.x_ref
  6.7 0.0 copy-done.8
  6.7 0.0 copy-done.12
  6.7 0.0 copy-done.9
  6.7 0.0 copy-done.13
  6.7 1.1 multiply_add_fusion
  7.8 0.0 copy-done.10
  7.8 113.7 %front.1 = (bf16[4,512,1024]{2,1,0:T(8,128)(2,1)}, bf16[4,512,1024]{2,1,0:T(8,128)(2,1)}, bf16[512,1024]{1,0:T(8,128)(2,1)}, bf16[2048,256]{1,0:T(8,128)(2,1)}, ...) custom-call(s32[8]{0:T(128)} %flag_ref.3, ...), custom_call_target="tpu_custom_call" | custom-call | tf_op jit(solution)/shard_map/front/pallas_call | solution.py:1529
  121.5 46.8 %dense.1 = (bf16[512,1024]{1,0:T(8,128)(2,1)}, f32[512,1024]{1,0:T(8,128)}, bf16[512,1024]{1,0:T(8,128)(2,1)}, bf16[2816,1024]{1,0:T(8,128)(2,1)}, bf16[1024,281...) custom-call(bf16[512,1024]{1,0:T(8,128)(2,1)} %bitcast.35, bf16[512,1024]{1,0:T(8,128)(2,1)} %bitcast.45, ...), custom_call_target="tpu_custom_call" | custom-call | flops 26843545600 | bytes 45088768 | tf_op jit(solution)/shard_map/dense/pallas_call | solution.py:1647
  168.3 163.5 %back.1 = (bf16[2,352,1024]{2,1,0:T(8,128)(2,1)}, bf16[2,128,2816]{2,1,0:T(8,128)(2,1)}, bf16[2,128,2816]{2,1,0:T(8,128)(2,1)}, bf16[2,128,1024]{2,1,0:T(8,128)(...) custom-call(s32[8]{0:T(128)} %flag_ref.3, bf16[512,1024]{1,0:T(8,128)(2,1)} %get-tuple-element.32.g_ref, ...), custom_call_target="tpu_custom_call" | custom-call | tf_op jit(solution)/shard_map/back/pallas_call | solution.py:1091
  331.8 0.0 copy-start
  331.8 0.0 copy-start.1
  331.9 0.0 copy-start.7
  331.9 0.0 copy-start.11
  331.9 0.0 copy-start.14
  331.9 2.1 fusion.7
  334.0 0.0 copy-done.1
  334.1 3.6 %fusion.6 = f32[1,512,1024]{2,1,0:T(8,128)} fusion(f32[512,1024]{1,0:T(8,128)} %get-tuple-element.45, bf16[512,1024]{1,0:T(8,128)(2,1)S(1)} %copy-done.1, f32[512]{0:T(512)S(1)} %broadcast_multiply_fusion, f32[512]{0:T(512)S(1)} %copy-done.14, f32[1024]{0:T(1024)S(1)} %copy-done.7, f32[512]{0:T(512)S(1)} %copy-done.11, bf16[1,512,1024]{2,1,0:T(8,128)(2,1)S(1)} %copy-done), kind=kLoop, calls=%fused_computation.13 | loop fusion | flops 4194304 | bytes 6301696 | tf_op jit(solution)/shard_map/broadcast_in_dim | solution.py:1732
  337.7 3.6 %multiply_reduce_fusion = (f32[256]{0:T(256)S(1)}, f32[256,3072]{1,0:T(8,128)}) fusion(bf16[1024,3072]{1,0:T(8,128)(2,1)} %w_hbm.3, s32[]{:T(128)S(6)} %select_n.2, bf16[2,128,3072]{2,1,0:T(8,128)(2,1)S(1)} %copy-done.2), kind=kLoop, calls=%fused_computation.4 | loop fusion | flops 3145472 | bytes 6292484 | tf_op jit(solution)/shard_map/reduce_sum | solution.py:1739
  341.3 0.6 dynamic-slice_divide_fusion.1
  342.0 0.0 copy-done.3
  342.0 4.8 %multiply_reduce_fusion.1 = (f32[256]{0:T(256)S(1)}, f32[256,2816]{1,0:T(8,128)}, f32[256]{0:T(256)S(1)}, f32[256,2816]{1,0:T(8,128)}) fusion(bf16[1024,2816]{1,0:T(8,128)(2,1)} %up_ref.1, s32[]{:T(128)S(6)} %select_n.2, bf16[2,128,2816]{2,1,0:T(8,128)(2,1)S(1)} %copy-done.4, bf16[2,128,2816]{2,1,0:T(8,128)(2,1)S(1)} %copy-done.3, bf16[1024,2816]{1,0:T(8,128)(2,1)} %gate_ref.1), kind=kLoop, calls=%fused_computation.5 | loop fusion | flops 5766656 | bytes 11536388 | tf_op jit(solution)/shard_map/reduce_sum | solution.py:1739
  346.8 1.4 dynamic-slice_divide_fusion
  348.2 1.1 bitcast_convert_fusion.4
  349.3 2.0 bitcast_convert_fusion.1
  (15 shorter events, 0.0 us)
Async XLA Ops:
  0.6 6.0 %copy-start.8 = (f32[64,128]{1,0:T(8,128)S(1)}, f32[64,128]{1,0:T(8,128)}, u32[]{:S(2)}) copy-start(f32[64,128]{1,0:T(8,128)} %constant.29.clone) | copy-start | bytes 98308
  0.7 6.0 %copy-start.12 = (f32[32,128]{1,0:T(8,128)S(1)}, f32[32,128]{1,0:T(8,128)}, u32[]{:S(2)}) copy-start(f32[32,128]{1,0:T(8,128)} %constant.28.clone) | copy-start | bytes 49156
  0.7 6.0 %copy-start.9 = (f32[64,128]{1,0:T(8,128)S(1)}, f32[64,128]{1,0:T(8,128)}, u32[]{:S(2)}) copy-start(f32[64,128]{1,0:T(8,128)} %constant.27.clone) | copy-start | bytes 98308
  0.7 6.0 %copy-start.13 = (f32[32,128]{1,0:T(8,128)S(1)}, f32[32,128]{1,0:T(8,128)}, u32[]{:S(2)}) copy-start(f32[32,128]{1,0:T(8,128)} %constant.26.clone) | copy-start | bytes 49156
  4.2 3.7 %copy-start.10 = (f32[512]{0:T(512)}, f32[512]{0:T(512)S(1)}, u32[]{:S(2)}) copy-start(f32[512]{0:T(512)S(1)} %get-tuple-element.58) | copy-start | bytes 6148
  331.8 2.2 copy-start
  331.8 2.2 copy-start.1
  331.9 2.2 copy-start.7
  331.9 2.2 copy-start.11
  331.9 2.2 copy-start.14
  334.1 3.6 %copy-start.2 = (bf16[2,128,3072]{2,1,0:T(8,128)(2,1)S(1)}, bf16[2,128,3072]{2,1,0:T(8,128)(2,1)}, u32[]{:S(2)}) copy-start(bf16[2,128,3072]{2,1,0:T(8,128)(2,1)} %get-tuple-element.46) | copy-start | bytes 4718596
  337.7 4.3 %copy-start.3 = (bf16[2,128,2816]{2,1,0:T(8,128)(2,1)S(1)}, bf16[2,128,2816]{2,1,0:T(8,128)(2,1)}, u32[]{:S(2)}) copy-start(bf16[2,128,2816]{2,1,0:T(8,128)(2,1)} %get-tuple-element.47) | copy-start | bytes 4325380
  337.7 4.3 %copy-start.4 = (bf16[2,128,2816]{2,1,0:T(8,128)(2,1)S(1)}, bf16[2,128,2816]{2,1,0:T(8,128)(2,1)}, u32[]{:S(2)}) copy-start(bf16[2,128,2816]{2,1,0:T(8,128)(2,1)} %get-tuple-element.48) | copy-start | bytes 4325380
  342.0 6.2 %copy-start.6 = (bf16[2,128,1024]{2,1,0:T(8,128)(2,1)S(1)}, bf16[2,128,1024]{2,1,0:T(8,128)(2,1)}, u32[]{:S(2)}) copy-start(bf16[2,128,1024]{2,1,0:T(8,128)(2,1)} %get-tuple-element.49) | copy-start | bytes 1572868
  346.8 2.6 copy-start.5

commit v4 on v3

--- a/solution.py
+++ b/solution.py
@@ -680,103 +680,6 @@
         return [("core", 8 * self.rows * self.columns)]
 
 
-class RowChunk:
-    def __init__(self, term, offset, rows, columns):
-        self.term, self.offset, self.rows, self.columns = term, offset, rows, columns
-
-    def scratch(self):
-        rows, columns, half = self.rows, self.columns, self.columns // 2
-        low = jnp.bfloat16
-        return [
-            pltpu.VMEM((2, rows, half), low),
-            pltpu.VMEM((2, rows, half), low),
-            pltpu.VMEM((rows, half), low),
-            pltpu.VMEM((rows, half), low),
-            pltpu.SemaphoreType.DMA((6,)),
-            pltpu.SemaphoreType.DMA((6,)),
-            pltpu.SemaphoreType.DMA((1,)),
-        ]
-
-    def bind(self, place, source, result, refs):
-        self.place, self.result = place, result
-        self.blocks = source
-        self.middle = refs[:4]
-        self.sent, self.received, self.local = refs[4:]
-
-    def mine(self, y, x, lanes):
-        return self.blocks.at[2 * y + x, pl.ds(self.offset, self.rows), lanes]
-
-    remote = Chunk.remote
-    halves = Chunk.halves
-
-    def wide_copies(self):
-        p, (left, right) = self.place, self.halves()
-        copies = []
-        for a in range(2):
-            copies.append(
-                self.remote(a, self.mine(a, 1 - p.x, left), self.middle[0].at[a], "x")
-            )
-            copies.append(
-                self.remote(2 + a, self.mine(1 - p.y, a, right), self.middle[1].at[a], "y")
-            )
-        return copies
-
-    def narrow_copies(self):
-        p, (left, right) = self.place, self.halves()
-        return [
-            self.remote(4, self.mine(1 - p.y, p.x, left), self.middle[2], "y"),
-            self.remote(5, self.mine(p.y, 1 - p.x, right), self.middle[3], "x"),
-        ]
-
-    def out_copy(self):
-        p = self.place
-        whole = pl.ds(0, self.columns)
-        return pltpu.make_async_copy(
-            self.mine(p.y, p.x, whole),
-            self.result.at[pl.ds(self.offset, self.rows), :],
-            self.local.at[0],
-        )
-
-    def stage_start(self):
-        for copy in self.wide_copies():
-            copy.start()
-
-    def stage_wide(self):
-        p, (left, right) = self.place, self.halves()
-        for copy in self.wide_copies():
-            copy.wait_recv()
-        for a in range(2):
-            add_into(self.mine(a, p.x, left), self.middle[0].at[a])
-            add_into(self.mine(p.y, a, right), self.middle[1].at[a])
-        for copy in self.narrow_copies():
-            copy.start()
-
-    def stage_narrow(self):
-        p, (left, right) = self.place, self.halves()
-        for copy in self.narrow_copies():
-            copy.wait_recv()
-        add_into(self.mine(p.y, p.x, left), self.middle[2])
-        add_into(self.mine(p.y, p.x, right), self.middle[3])
-        self.out_copy().start()
-
-    def stage_end(self):
-        self.out_copy().wait()
-        for copy in self.wide_copies() + self.narrow_copies():
-            copy.wait_send()
-
-    def plan(self):
-        piece = 2 * self.rows * self.columns
-        return [
-            (self.stage_wide, [("x", piece / 2), ("y", piece / 2)]),
-            (self.stage_narrow, [("core", 0.0)]),
-            (self.stage_end, []),
-        ]
-
-    def opening(self):
-        piece = 2 * self.rows * self.columns
-        return [("x", piece), ("y", piece)]
-
-
 class Steps:
     def __init__(self, start):
         self.now, self.free, self.waiting = start, {}, []
@@ -814,7 +717,7 @@
 
 def back_kernel(
     chunks,
-    first_chunks,
+    qkv_chunks,
     heads,
     flag_ref,
     g_ref,
@@ -827,40 +730,23 @@
     gate_ref,
     up_ref,
     out_ref,
-    w_hbm,
     mix_ref,
     log_ref,
     table_ref,
-    sum_down,
-    sum_gate,
-    sum_up,
-    sum_out,
-    sum_qkv,
-    sum_first,
-    w_ref,
-    q,
-    k,
-    v,
-    upstream,
-    shared,
-    dk,
-    dv,
-    total,
-    delta,
-    part_qkv,
-    trade_sent,
-    trade_received,
-    local,
     *refs,
 ):
+    results, rows_ref, refs = refs[: 4 + heads], refs[4 + heads], refs[5 + heads :]
+    q, k, v, upstream, shared, every, dk, dv, total, delta, part_qkv = refs[:11]
+    trade_sent, trade_received, rows_sent, rows_received, local = refs[11:16]
+    refs = refs[16:]
     place = Place()
     seq = lax.axis_index("seq")
     tokens = g_ref.shape[0]
     width = heads * HEAD_DIM
+    depth = g_ref.shape[1]
     used = 0
-    sources = [down_ref, gate_ref, up_ref, out_ref, part_qkv, shared]
-    results = [sum_down, sum_gate, sum_up, sum_out, sum_qkv, sum_first]
-    for chunk in chunks + first_chunks:
+    sources = [down_ref, gate_ref, up_ref, out_ref] + [part_qkv.at[head] for head in range(heads)]
+    for chunk in chunks + [chunk for group in qkv_chunks for chunk in group]:
         count = len(chunk.scratch())
         chunk.bind(place, sources[chunk.term], results[chunk.term], refs[used : used + count])
         used += count
@@ -881,6 +767,26 @@
         return pl.ds(pl.multiple_of(head * HEAD_DIM, HEAD_DIM), HEAD_DIM)
 
     across = {"x": seq + 1 - 2 * place.x, "y": seq + 2 - 4 * place.y, "xy": 3 - seq}
+    peers = ("x", "y", "xy")
+
+    def finished(head, kind, peer):
+        part = (q, k, v)[kind]
+        mine = pl.ds(head * HEAD_DIM, HEAD_DIM)
+        start = pl.multiple_of(kind * depth + seq * width + head * HEAD_DIM, HEAD_DIM)
+        target = rows_ref.at[:, pl.ds(start, HEAD_DIM)]
+        number = 3 * head + kind
+        if peer is None:
+            return pltpu.make_async_copy(part.at[span(seq), mine], target, local.at[6 + number])
+        slot = 3 * number + peers.index(peer)
+        return pltpu.make_async_remote_copy(
+            src_ref=part.at[span(across[peer]), mine],
+            dst_ref=target,
+            send_sem=rows_sent.at[slot],
+            recv_sem=rows_received.at[slot],
+            device_id=place.peer[peer],
+            device_id_type=pl.DeviceIdType.MESH,
+        )
+
     trades = [
         pltpu.make_async_remote_copy(
             src_ref=g_ref.at[:, columns(across[peer])],
@@ -890,7 +796,7 @@
             device_id=place.peer[peer],
             device_id_type=pl.DeviceIdType.MESH,
         )
-        for slot, peer in enumerate(("x", "y", "xy"))
+        for slot, peer in enumerate(peers)
     ]
     loads = [
         pltpu.make_async_copy(g_ref.at[:, columns(seq)], upstream.at[span(seq), :], local.at[0]),
@@ -898,8 +804,8 @@
         pltpu.make_async_copy(k_hbm, k, local.at[2]),
         pltpu.make_async_copy(v_hbm, v, local.at[3]),
         pltpu.make_async_copy(memory_hbm, shared, local.at[4]),
-    ] + weight_copies(w_hbm, w_ref, seq, local, 6)
-    load_every = pltpu.make_async_copy(every_hbm, shared, local.at[5])
+    ]
+    load_every = pltpu.make_async_copy(every_hbm, every, local.at[5])
 
     def turn_back(matrix, rows):
         cosine, sine = turn_factors(table_ref[rows, :])
@@ -961,33 +867,41 @@
 
         lax.fori_loop(0, 4, turn, 0)
 
-    def multiply_qkv(index, carry):
-        cut = pl.ds(pl.multiple_of(index * width, HEAD_DIM), width)
-        for kind, part in enumerate((q, k, v)):
+    def multiply_qkv(head):
+        mine = slice(head * HEAD_DIM, (head + 1) * HEAD_DIM)
+
+        def turn(index, carry):
+            cut = pl.ds(pl.multiple_of(index * width, HEAD_DIM), width)
             term = None
-            for block in range(shared.shape[0]):
-                product_part = product_tn(shared[block, :, cut], part[block * tokens : (block + 1) * tokens, :])
+            for block in range(every.shape[0]):
+                rows = slice(block * tokens, (block + 1) * tokens)
+                parts = jnp.concatenate([part[rows, mine] for part in (q, k, v)], axis=1)
+                product_part = product_tn(every[block, :, cut], parts)
                 term = product_part if term is None else term + product_part
             term = term.astype(jnp.bfloat16)
             half = term.shape[0] // 2
             place_y, place_x = lax.div(index, 2), lax.rem(index, 2)
             for core in range(2):
-                part_qkv[place_y, place_x, core, :, kind * width : (kind + 1) * width] = term[
-                    core * half : (core + 1) * half, :
-                ]
-        return carry
-
-    def multiply_first(block, carry):
-        rows = span(block)
-        result = None
-        for kind, part in enumerate((q, k, v)):
-            term = product_nt(part[rows, :], w_ref[:, kind * width : (kind + 1) * width])
-            result = term if result is None else result + term
-        shared[block] = result.astype(jnp.bfloat16)
-        return carry
+                part_qkv[head, place_y, place_x, core] = term[core * half : (core + 1) * half, :]
+            return carry
+
+        lax.fori_loop(0, 4, turn, 0)
+
+    def send_unit(number):
+        head, turn = number // 4, number % 4
+        finished(head, 0, ((None,) + peers)[turn]).start()
+        if turn == 3:
+            for kind in (1, 2):
+                for peer in peers + (None,):
+                    finished(head, kind, peer).start()
+            if head == 0:
+                load_every.wait()
+            multiply_qkv(head)
+            for chunk in qkv_chunks[head]:
+                chunk.stage_start()
 
     place.greet(("core", "x", "y", "xy", "pair"))
-    for copy in trades + loads:
+    for copy in trades + loads + [load_every]:
         copy.start()
     for chunk in chunks:
         chunk.stage_start()
@@ -997,7 +911,16 @@
     for copy in loads:
         copy.wait()
     slots = []
+    piece = 2 * tokens * HEAD_DIM
+
+    def close(head):
+        steps.send([("x", 4 * piece), ("y", 4 * piece)])
+        steps.spend(5.0)
+        steps.open(qkv_chunks[head])
+
     for unit in range(2 * 4 * heads):
+        if unit > 0 and unit % 8 == 0:
+            close(unit // 8 - 1)
         slots.append(steps.due())
         steps.spend(4.3 if unit % 2 == 0 else 3.2)
 
@@ -1009,10 +932,12 @@
         head, turn = lax.div(index, 4), lax.rem(index, 4)
         block = owner_at(turn)
         for number in range(4 * heads):
-            if slots[2 * number] or number in (1, 2, 3):
+            if slots[2 * number] or number > 0:
 
                 @pl.when(index == number)
                 def _(number=number):
+                    if number > 0:
+                        send_unit(number - 1)
                     run(slots[2 * number])
                     if number in (1, 2, 3):
                         trades[number - 1].wait_recv()
@@ -1039,32 +964,21 @@
         return carry
 
     lax.fori_loop(0, 4 * heads, unit, 0)
-    load_every.start()
-    run(steps.due())
-    load_every.wait()
-    lax.fori_loop(0, 4, multiply_qkv, 0)
-    steps.spend(8.0)
-    qkv_chunks = [chunk for chunk in first_chunks if chunk.term == 4]
-    row_chunks = [chunk for chunk in first_chunks if chunk.term == 5]
-    for chunk in qkv_chunks:
-        chunk.stage_start()
-    steps.open(qkv_chunks)
-    run(steps.due())
-    lax.fori_loop(0, 4, multiply_first, 0)
-    steps.spend(6.0)
-    for chunk in row_chunks:
-        chunk.stage_start()
-    steps.open(row_chunks)
+    send_unit(4 * heads - 1)
+    close(heads - 1)
     run(steps.due(True))
     for copy in trades:
         copy.wait_send()
-
-
-def back(
-    flags, grads, queries, keys, values, memory, every, terms, w_qkv, attended, log_totals, table, collective_id
-):
+    for head in range(heads):
+        for kind in range(3):
+            for peer in peers + (None,):
+                finished(head, kind, peer).wait()
+
+
+def back(flags, grads, queries, keys, values, memory, every, terms, attended, log_totals, table, collective_id):
     tokens, depth = grads.shape
     length, width = queries.shape
+    heads = width // HEAD_DIM
     low = jnp.bfloat16
     chunks, shapes = [], []
     for index, term in enumerate(terms):
@@ -1072,28 +986,32 @@
         parts = 2 if rows % 32 == 0 and index < 3 else 1
         chunks += [Chunk(index, n * rows // parts, rows // parts, columns) for n in range(parts)]
         shapes.append((2, rows, columns))
-    rows = depth // 8
-    first_chunks = [Chunk(4, n * rows // 2, rows // 2, 3 * width, True) for n in range(2)]
-    first_chunks += [RowChunk(5, n * tokens // 4, tokens // 4, depth) for n in range(4)]
-    shapes += [(2, rows, 12 * width), (tokens, depth)]
+    rows, columns = depth // 8, 3 * HEAD_DIM
+    qkv_chunks = [
+        [Chunk(4 + head, n * rows // 2, rows // 2, columns, True) for n in range(2)]
+        for head in range(heads)
+    ]
+    shapes += [(2, rows, 4 * columns)] * heads + [(tokens, 3 * depth)]
     anywhere = pl.BlockSpec(memory_space=pl.ANY)
     inside = pl.BlockSpec(memory_space=pltpu.VMEM)
+    dma = pltpu.SemaphoreType.DMA
     scratch = (
-        [pltpu.VMEM((depth, 3 * width), low)]
-        + [pltpu.VMEM((length, width), low)] * 4
-        + [pltpu.VMEM((4, tokens, depth), low)]
+        [pltpu.VMEM((length, width), low)] * 4
+        + [pltpu.VMEM((4, tokens, depth), low)] * 2
         + [pltpu.VMEM((length, HEAD_DIM), jnp.float32)] * 2
         + [pltpu.VMEM((tokens, HEAD_DIM), jnp.float32)] * 2
-        + [pltpu.VMEM((2, 2, 2, rows, 3 * width), low)]
-        + [pltpu.SemaphoreType.DMA((3,))] * 2
-        + [pltpu.SemaphoreType.DMA((9,))]
-    )
+        + [pltpu.VMEM((heads, 2, 2, 2, rows, columns), low)]
+        + [dma((3,))] * 2
+        + [dma((9 * heads,))] * 2
+        + [dma((6 + 3 * heads,))]
+    )
+    every_chunk = chunks + [chunk for group in qkv_chunks for chunk in group]
     return pl.pallas_call(
-        functools.partial(back_kernel, chunks, first_chunks, width // HEAD_DIM),
-        in_specs=[pl.BlockSpec(memory_space=pltpu.SMEM)] + [anywhere] * 11 + [inside] * 3,
+        functools.partial(back_kernel, chunks, qkv_chunks, heads),
+        in_specs=[pl.BlockSpec(memory_space=pltpu.SMEM)] + [anywhere] * 10 + [inside] * 3,
         out_specs=[anywhere] * len(shapes),
         out_shape=[jax.ShapeDtypeStruct(shape, low) for shape in shapes],
-        scratch_shapes=scratch + [ref for chunk in chunks + first_chunks for ref in chunk.scratch()],
+        scratch_shapes=scratch + [ref for chunk in every_chunk for ref in chunk.scratch()],
         compiler_params=pltpu.CompilerParams(
             collective_id=collective_id, has_side_effects=True, vmem_limit_bytes=VMEM_MOST
         ),
@@ -1107,7 +1025,6 @@
         memory,
         every,
         *[term.reshape((2, 2, 2, term.shape[0] // 8, term.shape[1])) for term in terms],
-        w_qkv,
         attended,
         log_totals,
         table,
@@ -1675,6 +1592,167 @@
     )(x, grads, attended, w_out, gain, w_gate, w_up, w_down)
 
 
+def tail_kernel(
+    heads,
+    down_hbm,
+    gate_hbm,
+    up_hbm,
+    out_hbm,
+    *refs,
+):
+    qkv_hbm, refs = refs[:heads], refs[heads:]
+    turned_hbm, x_hbm, grad_hbm, w_hbm, w_gate_hbm, w_up_hbm, gain1_ref, gain2_ref = refs[:8]
+    input_out, norm1_ref, norm2_ref, qkv_out, out_out, gate_out, up_out, down_out = refs[8:16]
+    down, gate, up, out = refs[16:20]
+    qkv, refs = refs[20 : 20 + heads], refs[20 + heads :]
+    turned, x, grad, w, w_gate, w_up = refs[:6]
+    input_wide, qkv_wide, out_wide, gate_wide, up_wide, down_wide, dots1, dots2, loaded, stored = refs[6:]
+    seq = lax.axis_index("seq")
+    count = gate.shape[0]
+    block = pl.ds(pl.multiple_of(seq * count, count), count)
+    pairs = [
+        (gate_hbm, gate),
+        (w_gate_hbm.at[block, :], w_gate),
+        (up_hbm, up),
+        (w_up_hbm.at[block, :], w_up),
+        (down_hbm, down),
+        (out_hbm, out),
+        (turned_hbm, turned),
+        (w_hbm, w),
+        *zip(qkv_hbm, qkv),
+        (x_hbm, x),
+        (grad_hbm, grad),
+    ]
+    loads = [
+        pltpu.make_async_copy(source, target, loaded.at[n]) for n, (source, target) in enumerate(pairs)
+    ]
+    wides = [gate_wide, up_wide, down_wide, out_wide, qkv_wide, input_wide]
+    outs = [gate_out, up_out, down_out, out_out, qkv_out, input_out]
+    stores = [
+        pltpu.make_async_copy(source, target, stored.at[n])
+        for n, (source, target) in enumerate(zip(wides, outs))
+    ]
+    for copy in loads:
+        copy.start()
+
+    def by_rows(count, step, body):
+        def turn(index, carry):
+            body(pl.ds(pl.multiple_of(index * step, step), step))
+            return carry
+
+        lax.fori_loop(0, count // step, turn, 0)
+
+    def widen(former, latter):
+        def body(rows):
+            latter[rows, :] = former[rows, :].astype(jnp.float32)
+
+        by_rows(former.shape[0], 16, body)
+
+    def dot_rows(values, weights):
+        return lane_fold(jnp.add, values * weights.astype(jnp.float32), None)
+
+    def gate_body(rows):
+        values = gate[rows, :].astype(jnp.float32)
+        gate_wide[rows, :] = values
+        dots2[rows, :] = dot_rows(values, w_gate[rows, :])
+
+    def up_body(rows):
+        values = up[rows, :].astype(jnp.float32)
+        up_wide[rows, :] = values
+        dots2[rows, :] += dot_rows(values, w_up[rows, :])
+
+    def qkv_body(rows):
+        running = None
+        weights = pl.ds(pl.multiple_of(seq * count + rows.start, 16), rows.size)
+        for number in range(qkv[0].shape[1] // HEAD_DIM):
+            for head in range(heads):
+                start = (number * heads + head) * HEAD_DIM
+                lanes = slice(start, start + HEAD_DIM)
+                values = qkv[head][rows, number * HEAD_DIM : (number + 1) * HEAD_DIM].astype(jnp.float32)
+                qkv_wide[rows, lanes] = values
+                term = values * w[weights, lanes].astype(jnp.float32)
+                running = term if running is None else running + term
+        dots1[rows, :] = running
+
+    def gain_grads(dots, gain_ref):
+        columns = jnp.broadcast_to(jnp.sum(dots[...], axis=1, keepdims=True), dots.shape)
+        return columns.T[:1, :] / gain_ref[:, block]
+
+    def wait(*numbers):
+        for number in numbers:
+            loads[number].wait()
+
+    wait(0, 1)
+    by_rows(count, 16, gate_body)
+    stores[0].start()
+    wait(2, 3)
+    by_rows(count, 16, up_body)
+    stores[1].start()
+    norm2_ref[...] = gain_grads(dots2, gain2_ref)
+    wait(4)
+    widen(down, down_wide)
+    stores[2].start()
+    wait(5)
+    widen(out, out_wide)
+    stores[3].start()
+    wait(6, 7)
+
+    def first_columns(index, carry):
+        cut = pl.ds(pl.multiple_of(index * count, count), count)
+        input_wide[:, cut] = product_nt(turned[...], w[cut, :])
+        return carry
+
+    lax.fori_loop(0, w.shape[0] // count, first_columns, 0)
+    wait(*range(8, 8 + heads))
+    by_rows(count, 16, qkv_body)
+    stores[4].start()
+    norm1_ref[...] = gain_grads(dots1, gain1_ref)
+    wait(8 + heads, 9 + heads)
+
+    def input_body(rows):
+        values = x[rows, :].astype(jnp.float32)
+        inverse = lax.rsqrt(jnp.mean(values * values, axis=-1, keepdims=True) + epsilon)
+        input_wide[rows, :] = grad[rows, :] + norm_input_grad(
+            values, inverse, gain1_ref[...], input_wide[rows, :]
+        )
+
+    by_rows(x.shape[0], 32, input_body)
+    stores[5].start()
+    for copy in stores:
+        copy.wait()
+
+
+def tail(sums, turned, x, grad, w_qkv, w_gate, w_up, gain1, gain2):
+    down, gate, up, out, *qkv = sums
+    tokens, depth = x.shape
+    count = gate.shape[0]
+    low, wide = jnp.bfloat16, jnp.float32
+    anywhere = pl.BlockSpec(memory_space=pl.ANY)
+    inside = pl.BlockSpec(memory_space=pltpu.VMEM)
+    shapes = [(tokens, depth), (count, w_qkv.shape[1]), out.shape, gate.shape, up.shape, down.shape]
+    results = [shapes[0], (1, count), (1, count)] + shapes[1:]
+    return pl.pallas_call(
+        functools.partial(tail_kernel, len(qkv)),
+        in_specs=[anywhere] * (10 + len(qkv)) + [inside] * 2,
+        out_specs=[anywhere] + [inside] * 2 + [anywhere] * 5,
+        out_shape=[jax.ShapeDtypeStruct(shape, wide) for shape in results],
+        scratch_shapes=[pltpu.VMEM(total.shape, low) for total in sums]
+        + [
+            pltpu.VMEM(turned.shape, low),
+            pltpu.VMEM(x.shape, low),
+            pltpu.VMEM(x.shape, wide),
+            pltpu.VMEM(w_qkv.shape, low),
+            pltpu.VMEM(gate.shape, low),
+            pltpu.VMEM(up.shape, low),
+        ]
+        + [pltpu.VMEM(shape, wide) for shape in shapes]
+        + [pltpu.VMEM((count, HEAD_DIM), wide)] * 2
+        + [pltpu.SemaphoreType.DMA((10 + len(qkv),)), pltpu.SemaphoreType.DMA((6,))],
+        compiler_params=pltpu.CompilerParams(vmem_limit_bytes=VMEM_BYTES),
+        name="tail",
+    )(*sums, turned, x, grad, w_qkv, w_gate, w_up, gain1, gain2)
+
+
 def head_plan(
     seg_size,
     seq_size,
@@ -1707,7 +1785,7 @@
     output, grad_residual, grad_attended, term_down, term_gate, term_up, term_out = dense(
         layer_input[0], output_grad[0], attended_low, w_out, norm2_gain[None], w_gate, w_up, w_down
     )
-    *sums, qkv_rows, first_rows = back(
+    *sums, turned = back(
         memory_flags,
         grad_attended,
         queries,
@@ -1716,38 +1794,20 @@
         chosen_memory,
         every_low,
         [term_down, term_gate, term_up, term_out],
-        w_qkv,
         heads_low,
         log_totals,
         table,
         2,
     )
-    grad_down, grad_gate, grad_up, grad_out = [
-        total.reshape(2 * total.shape[1], total.shape[2]).astype(jnp.float32) for total in sums
-    ]
-    grad_qkv = qkv_rows.reshape(width, 3 * D).astype(jnp.float32)
-    grad_inputs = norm_input_grad(
-        inputs, first_inverse, norm1_gain, first_rows.astype(jnp.float32)
-    )
-    input_grad = (grad_inputs + grad_residual)[None]
-
-    def row_block(whole):
-        return lax.dynamic_slice_in_dim(whole, seq_index * width, width, 0)
-
-    def gain_rows(weights, grads, gain):
-        dots = [
-            jnp.sum(row_block(weight).astype(jnp.float32) * grad, axis=1)
-            for weight, grad in zip(weights, grads)
-        ]
-        return sum(dots[1:], dots[0]) / row_block(gain)
-
-    grad_norm1 = gain_rows([w_qkv], [grad_qkv], norm1_gain)
-    grad_norm2 = gain_rows([w_gate, w_up], [grad_gate, grad_up], norm2_gain)
+    sums = [total.reshape(2 * total.shape[1], total.shape[2]) for total in sums]
+    input_grad, grad_norm1, grad_norm2, grad_qkv, grad_out, grad_gate, grad_up, grad_down = tail(
+        sums, turned, layer_input[0], grad_residual, w_qkv, w_gate, w_up, norm1_gain[None], norm2_gain[None]
+    )
     return (
         output[None],
-        input_grad,
-        grad_norm1,
-        grad_norm2,
+        input_grad[None],
+        grad_norm1[0],
+        grad_norm2[0],
         grad_qkv,
         grad_out,
         grad_gate,

time: 356 us -> 367 us (1.031)
  Pallas kernels: 324 us -> 358 us
  other arithmetic: 25.1 us -> 5.17 us
    pallas_call x1 -> x2, Pallas kernels: 164 us -> 197 us  [the longest x1 178 us: back(): pl.pallas_call(functools.partial(back_kernel, chunks, qkv_chunks, heads),...]
    reduce_sum x3 -> x0, other arithmetic: 10.5 us -> none  [the longest x2 8.4 us: gain_rows(): jnp.sum(row_block(weight).astype(jnp.float32) * grad, axis=1)]
where the time goes in v4:
time: 367 us; the launch traced here: 365 us
  Pallas kernels  358 us (98%)
  other arithmetic  5.17 us (1%)
    pallas_call x1, Pallas kernels, back(): pl.pallas_call(functools.partial(back_kernel, chunks, qkv_chunks, heads),...  178 us
    pallas_call x1, Pallas kernels, front(): pl.pallas_call(functools.partial(front_kernel, width // HEAD_DIM), in_spe...  114 us
    pallas_call x1, Pallas kernels, dense(): pl.pallas_call(dense_kernel, grid=(hidden // tile,), in_specs=[activation...  46.8 us
    pallas_call x1, Pallas kernels, tail(): pl.pallas_call(functools.partial(tail_kernel, len(qkv)), in_specs=[anywhe...  18.8 us

profile of v4, /device:TPU:0, one launch (start us, length us, event | category | flops | bytes accessed | tf_op | source)
XLA Modules:
  0.0 365.2 jit_solution(6864914300199622487)
XLA Ops:
  0.6 0.0 copy-start
  0.7 0.0 copy-start.2
  0.7 0.0 copy-start.1
  0.7 0.0 copy-start.3
  0.7 1.5 fusion
  2.2 1.4 copy.26.source_ref
  3.6 2.5 fusion.2.x_ref
  6.1 0.0 copy-done
  6.1 0.0 copy-done.2
  6.1 0.0 copy-done.1
  6.1 0.0 copy-done.3
  6.1 1.1 multiply_add_fusion
  7.2 113.7 %front.1 = (bf16[4,512,1024]{2,1,0:T(8,128)(2,1)}, bf16[4,512,1024]{2,1,0:T(8,128)(2,1)}, bf16[512,1024]{1,0:T(8,128)(2,1)}, bf16[2048,256]{1,0:T(8,128)(2,1)}, ...) custom-call(s32[8]{0:T(128)} %flag_ref.3, ...), custom_call_target="tpu_custom_call" | custom-call | tf_op jit(solution)/shard_map/front/pallas_call | solution.py:1446
  120.9 46.8 %dense.1 = (bf16[512,1024]{1,0:T(8,128)(2,1)}, f32[512,1024]{1,0:T(8,128)}, bf16[512,1024]{1,0:T(8,128)(2,1)}, bf16[2816,1024]{1,0:T(8,128)(2,1)}, bf16[1024,281...) custom-call(bf16[512,1024]{1,0:T(8,128)(2,1)} %bitcast.25, bf16[512,1024]{1,0:T(8,128)(2,1)} %bitcast.43, ...), custom_call_target="tpu_custom_call" | custom-call | flops 26843545600 | bytes 45088768 | tf_op jit(solution)/shard_map/dense/pallas_call | solution.py:1564
  167.8 178.5 %back.1 = (bf16[2,352,1024]{2,1,0:T(8,128)(2,1)}, bf16[2,128,2816]{2,1,0:T(8,128)(2,1)}, bf16[2,128,2816]{2,1,0:T(8,128)(2,1)}, bf16[2,128,1024]{2,1,0:T(8,128)(...) custom-call(s32[8]{0:T(128)} %flag_ref.3, ...), custom_call_target="tpu_custom_call" | custom-call | tf_op jit(solution)/shard_map/back/pallas_call | solution.py:1009
  346.2 18.8 %tail.1 = (f32[512,1024]{1,0:T(8,128)}, f32[1,256]{1,0:T(1,128)}, f32[1,256]{1,0:T(1,128)}, f32[256,3072]{1,0:T(8,128)}, f32[256,1024]{1,0:T(8,128)}, /*index=5*...) custom-call(bf16[704,1024]{1,0:T(8,128)(2,1)} %bitcast.31, bf16[256,2816]{1,0:T(8,128)(2,1)} %bitcast.32, ...), custom_call_target="tpu_custom_call" | custom-call | tf_op jit(solution)/shard_map/tail/pallas_call | solution.py:1734
  (1 shorter events, 0.0 us)
Async XLA Ops:
  0.6 5.5 %copy-start = (f32[64,128]{1,0:T(8,128)S(1)}, f32[64,128]{1,0:T(8,128)}, u32[]{:S(2)}) copy-start(f32[64,128]{1,0:T(8,128)} %constant.18.clone) | copy-start | bytes 98308
  0.7 5.4 %copy-start.2 = (f32[32,128]{1,0:T(8,128)S(1)}, f32[32,128]{1,0:T(8,128)}, u32[]{:S(2)}) copy-start(f32[32,128]{1,0:T(8,128)} %constant.17.clone) | copy-start | bytes 49156
  0.7 5.4 %copy-start.1 = (f32[64,128]{1,0:T(8,128)S(1)}, f32[64,128]{1,0:T(8,128)}, u32[]{:S(2)}) copy-start(f32[64,128]{1,0:T(8,128)} %constant.16.clone) | copy-start | bytes 98308
  0.7 5.4 %copy-start.3 = (f32[32,128]{1,0:T(8,128)S(1)}, f32[32,128]{1,0:T(8,128)}, u32[]{:S(2)}) copy-start(f32[32,128]{1,0:T(8,128)} %constant.15.clone) | copy-start | bytes 49156

commit v5 on v3

--- a/solution.py
+++ b/solution.py
@@ -1675,6 +1675,180 @@
     )(x, grads, attended, w_out, gain, w_gate, w_up, w_down)
 
 
+def tail_kernel(
+    down_hbm,
+    gate_hbm,
+    up_hbm,
+    out_hbm,
+    qkv_hbm,
+    first_hbm,
+    x_hbm,
+    grad_hbm,
+    w_hbm,
+    w_gate_hbm,
+    w_up_hbm,
+    gain1_ref,
+    gain2_ref,
+    input_out,
+    norm1_ref,
+    norm2_ref,
+    qkv_out,
+    out_out,
+    gate_out,
+    up_out,
+    down_out,
+    down,
+    gate,
+    up,
+    out,
+    qkv,
+    first,
+    x,
+    grad,
+    w,
+    w_gate,
+    w_up,
+    input_wide,
+    qkv_wide,
+    out_wide,
+    gate_wide,
+    up_wide,
+    down_wide,
+    dots1,
+    dots2,
+    loaded,
+    stored,
+):
+    seq = lax.axis_index("seq")
+    count = gate.shape[0]
+    block = pl.ds(pl.multiple_of(seq * count, count), count)
+    pairs = [
+        (gate_hbm, gate),
+        (w_gate_hbm.at[block, :], w_gate),
+        (up_hbm, up),
+        (w_up_hbm.at[block, :], w_up),
+        (down_hbm, down),
+        (out_hbm, out),
+        (w_hbm.at[block, :], w),
+        (qkv_hbm, qkv),
+        (first_hbm, first),
+        (x_hbm, x),
+        (grad_hbm, grad),
+    ]
+    loads = [
+        pltpu.make_async_copy(source, target, loaded.at[n]) for n, (source, target) in enumerate(pairs)
+    ]
+    wides = [gate_wide, up_wide, down_wide, out_wide, qkv_wide, input_wide]
+    outs = [gate_out, up_out, down_out, out_out, qkv_out, input_out]
+    stores = [
+        pltpu.make_async_copy(source, target, stored.at[n])
+        for n, (source, target) in enumerate(zip(wides, outs))
+    ]
+    for copy in loads:
+        copy.start()
+
+    def by_rows(count, step, body):
+        def turn(index, carry):
+            body(pl.ds(pl.multiple_of(index * step, step), step))
+            return carry
+
+        lax.fori_loop(0, count // step, turn, 0)
+
+    def widen(former, latter):
+        def body(rows):
+            latter[rows, :] = former[rows, :].astype(jnp.float32)
+
+        by_rows(former.shape[0], 16, body)
+
+    def dot_rows(values, weights):
+        return lane_fold(jnp.add, values * weights.astype(jnp.float32), None)
+
+    def gate_body(rows):
+        values = gate[rows, :].astype(jnp.float32)
+        gate_wide[rows, :] = values
+        dots2[rows, :] = dot_rows(values, w_gate[rows, :])
+
+    def up_body(rows):
+        values = up[rows, :].astype(jnp.float32)
+        up_wide[rows, :] = values
+        dots2[rows, :] += dot_rows(values, w_up[rows, :])
+
+    def qkv_body(rows):
+        values = qkv[rows, :].astype(jnp.float32)
+        qkv_wide[rows, :] = values
+        dots1[rows, :] = dot_rows(values, w[rows, :])
+
+    def gain_grads(dots, gain_ref):
+        columns = jnp.broadcast_to(jnp.sum(dots[...], axis=1, keepdims=True), dots.shape)
+        return columns.T[:1, :] / gain_ref[:, block]
+
+    def wait(*numbers):
+        for number in numbers:
+            loads[number].wait()
+
+    wait(0, 1)
+    by_rows(count, 16, gate_body)
+    stores[0].start()
+    wait(2, 3)
+    by_rows(count, 16, up_body)
+    stores[1].start()
+    norm2_ref[...] = gain_grads(dots2, gain2_ref)
+    wait(4)
+    widen(down, down_wide)
+    stores[2].start()
+    wait(5)
+    widen(out, out_wide)
+    stores[3].start()
+    wait(6, 7)
+    by_rows(count, 16, qkv_body)
+    stores[4].start()
+    norm1_ref[...] = gain_grads(dots1, gain1_ref)
+    wait(8, 9, 10)
+
+    def input_body(rows):
+        values = x[rows, :].astype(jnp.float32)
+        inverse = lax.rsqrt(jnp.mean(values * values, axis=-1, keepdims=True) + epsilon)
+        input_wide[rows, :] = grad[rows, :] + norm_input_grad(
+            values, inverse, gain1_ref[...], first[rows, :].astype(jnp.float32)
+        )
+
+    by_rows(x.shape[0], 32, input_body)
+    stores[5].start()
+    for copy in stores:
+        copy.wait()
+
+
+def tail(sums, first, x, grad, w_qkv, w_gate, w_up, gain1, gain2):
+    down, gate, up, out, qkv = sums
+    tokens, depth = x.shape
+    count = gate.shape[0]
+    low, wide = jnp.bfloat16, jnp.float32
+    anywhere = pl.BlockSpec(memory_space=pl.ANY)
+    inside = pl.BlockSpec(memory_space=pltpu.VMEM)
+    shapes = [(tokens, depth), qkv.shape, out.shape, gate.shape, up.shape, down.shape]
+    results = [shapes[0], (1, count), (1, count)] + shapes[1:]
+    return pl.pallas_call(
+        tail_kernel,
+        in_specs=[anywhere] * 11 + [inside] * 2,
+        out_specs=[anywhere] + [inside] * 2 + [anywhere] * 5,
+        out_shape=[jax.ShapeDtypeStruct(shape, wide) for shape in results],
+        scratch_shapes=[pltpu.VMEM(total.shape, low) for total in sums]
+        + [
+            pltpu.VMEM(first.shape, low),
+            pltpu.VMEM(x.shape, low),
+            pltpu.VMEM(x.shape, wide),
+            pltpu.VMEM(qkv.shape, low),
+            pltpu.VMEM(gate.shape, low),
+            pltpu.VMEM(up.shape, low),
+        ]
+        + [pltpu.VMEM(shape, wide) for shape in shapes]
+        + [pltpu.VMEM((count, HEAD_DIM), wide)] * 2
+        + [pltpu.SemaphoreType.DMA((11,)), pltpu.SemaphoreType.DMA((6,))],
+        compiler_params=pltpu.CompilerParams(vmem_limit_bytes=VMEM_BYTES),
+        name="tail",
+    )(*sums, first, x, grad, w_qkv, w_gate, w_up, gain1, gain2)
+
+
 def head_plan(
     seg_size,
     seq_size,
@@ -1692,13 +1866,11 @@
     memory_flags,
     sources,
 ):
-    seq_index = lax.axis_index("seq")
     tokens = layer_input.shape[1]
     length = tokens * seq_size
     width = D // seq_size
     inputs = layer_input[0].astype(jnp.float32)
-    first_norm, first_inverse = norm_forward(inputs, norm1_gain)
-    first_low = first_norm.astype(jnp.bfloat16)
+    first_low = norm_forward(inputs, norm1_gain)[0].astype(jnp.bfloat16)
     table = turn_table(length)
     every_low, chosen_memory, attended_low, queries, keys, values, heads_low, log_totals = front(
         memory_flags, sources, first_low, mem_keys[0], mem_values[0], w_qkv, table, seg_size, seq_size, 1
@@ -1722,32 +1894,16 @@
         table,
         2,
     )
-    grad_down, grad_gate, grad_up, grad_out = [
-        total.reshape(2 * total.shape[1], total.shape[2]).astype(jnp.float32) for total in sums
-    ]
-    grad_qkv = qkv_rows.reshape(width, 3 * D).astype(jnp.float32)
-    grad_inputs = norm_input_grad(
-        inputs, first_inverse, norm1_gain, first_rows.astype(jnp.float32)
-    )
-    input_grad = (grad_inputs + grad_residual)[None]
-
-    def row_block(whole):
-        return lax.dynamic_slice_in_dim(whole, seq_index * width, width, 0)
-
-    def gain_rows(weights, grads, gain):
-        dots = [
-            jnp.sum(row_block(weight).astype(jnp.float32) * grad, axis=1)
-            for weight, grad in zip(weights, grads)
-        ]
-        return sum(dots[1:], dots[0]) / row_block(gain)
-
-    grad_norm1 = gain_rows([w_qkv], [grad_qkv], norm1_gain)
-    grad_norm2 = gain_rows([w_gate, w_up], [grad_gate, grad_up], norm2_gain)
+    sums = [total.reshape(2 * total.shape[1], total.shape[2]) for total in sums]
+    sums.append(qkv_rows.reshape(width, 3 * D))
+    input_grad, grad_norm1, grad_norm2, grad_qkv, grad_out, grad_gate, grad_up, grad_down = tail(
+        sums, first_rows, layer_input[0], grad_residual, w_qkv, w_gate, w_up, norm1_gain[None], norm2_gain[None]
+    )
     return (
         output[None],
-        input_grad,
-        grad_norm1,
-        grad_norm2,
+        input_grad[None],
+        grad_norm1[0],
+        grad_norm2[0],
         grad_qkv,
         grad_out,
         grad_gate,

time: 356 us -> 346 us (0.972); the launches traced: 352 us -> 346 us
  other arithmetic: 25.1 us -> 5.17 us
  Pallas kernels: 324 us -> 338 us
    pallas_call x0 -> x1, Pallas kernels: none -> 14.5 us  [tail(): pl.pallas_call(tail_kernel, in_specs=[anywhere] * 11 + [inside] * 2, out_...]
    reduce_sum x3 -> x0, other arithmetic: 10.5 us -> none  [the longest x2 8.4 us: gain_rows(): jnp.sum(row_block(weight).astype(jnp.float32) * grad, axis=1)]
    broadcast_in_dim x1 -> x0, other arithmetic: 3.63 us -> none  [head_plan(): input_grad = (grad_inputs + grad_residual)[None]]
where the time goes in v5:
time: 346 us
  Pallas kernels  338 us (98%)
  other arithmetic  5.17 us (1%)
    pallas_call x1, Pallas kernels, back(): pl.pallas_call(functools.partial(back_kernel, chunks, first_chunks, width...  163 us
    pallas_call x1, Pallas kernels, front(): pl.pallas_call(functools.partial(front_kernel, width // HEAD_DIM), in_spe...  114 us
    pallas_call x1, Pallas kernels, dense(): pl.pallas_call(dense_kernel, grid=(hidden // tile,), in_specs=[activation...  46.8 us
    pallas_call x1, Pallas kernels, tail(): pl.pallas_call(tail_kernel, in_specs=[anywhere] * 11 + [inside] * 2, out_...  14.5 us

profile of v5, /device:TPU:0, one launch (start us, length us, event | category | flops | bytes accessed | tf_op | source)
XLA Modules:
  0.0 345.9 jit_solution(3487443738946075455)
XLA Ops:
  0.6 0.0 copy-start
  0.7 0.0 copy-start.2
  0.7 0.0 copy-start.1
  0.7 0.0 copy-start.3
  0.7 1.5 fusion
  2.2 1.4 copy.26.source_ref
  3.6 2.5 fusion.2.x_ref
  6.1 0.0 copy-done
  6.1 0.0 copy-done.2
  6.1 0.0 copy-done.1
  6.1 0.0 copy-done.3
  6.1 1.1 multiply_add_fusion
  7.2 113.7 %front.1 = (bf16[4,512,1024]{2,1,0:T(8,128)(2,1)}, bf16[4,512,1024]{2,1,0:T(8,128)(2,1)}, bf16[512,1024]{1,0:T(8,128)(2,1)}, bf16[2048,256]{1,0:T(8,128)(2,1)}, ...) custom-call(s32[8]{0:T(128)} %flag_ref.3, ...), custom_call_target="tpu_custom_call" | custom-call | tf_op jit(solution)/shard_map/front/pallas_call | solution.py:1529
  120.9 46.8 %dense.1 = (bf16[512,1024]{1,0:T(8,128)(2,1)}, f32[512,1024]{1,0:T(8,128)}, bf16[512,1024]{1,0:T(8,128)(2,1)}, bf16[2816,1024]{1,0:T(8,128)(2,1)}, bf16[1024,281...) custom-call(bf16[512,1024]{1,0:T(8,128)(2,1)} %bitcast.24, bf16[512,1024]{1,0:T(8,128)(2,1)} %bitcast.41, ...), custom_call_target="tpu_custom_call" | custom-call | flops 26843545600 | bytes 45088768 | tf_op jit(solution)/shard_map/dense/pallas_call | solution.py:1647
  167.7 163.4 %back.1 = (bf16[2,352,1024]{2,1,0:T(8,128)(2,1)}, bf16[2,128,2816]{2,1,0:T(8,128)(2,1)}, bf16[2,128,2816]{2,1,0:T(8,128)(2,1)}, bf16[2,128,1024]{2,1,0:T(8,128)(...) custom-call(s32[8]{0:T(128)} %flag_ref.3, bf16[512,1024]{1,0:T(8,128)(2,1)} %get-tuple-element.40.g_ref, ...), custom_call_target="tpu_custom_call" | custom-call | tf_op jit(solution)/shard_map/back/pallas_call | solution.py:1091
  331.2 14.5 %tail.1 = (f32[512,1024]{1,0:T(8,128)}, f32[1,256]{1,0:T(1,128)}, f32[1,256]{1,0:T(1,128)}, f32[256,3072]{1,0:T(8,128)}, f32[256,1024]{1,0:T(8,128)}, /*index=5*...) custom-call(bf16[704,1024]{1,0:T(8,128)(2,1)} %bitcast.31, bf16[256,2816]{1,0:T(8,128)(2,1)} %bitcast.32, ...), custom_call_target="tpu_custom_call" | custom-call | tf_op jit(solution)/shard_map/tail/pallas_call | solution.py:1830
  (1 shorter events, 0.0 us)
Async XLA Ops:
  0.6 5.5 %copy-start = (f32[64,128]{1,0:T(8,128)S(1)}, f32[64,128]{1,0:T(8,128)}, u32[]{:S(2)}) copy-start(f32[64,128]{1,0:T(8,128)} %constant.18.clone) | copy-start | bytes 98308
  0.7 5.4 %copy-start.2 = (f32[32,128]{1,0:T(8,128)S(1)}, f32[32,128]{1,0:T(8,128)}, u32[]{:S(2)}) copy-start(f32[32,128]{1,0:T(8,128)} %constant.17.clone) | copy-start | bytes 49156
  0.7 5.4 %copy-start.1 = (f32[64,128]{1,0:T(8,128)S(1)}, f32[64,128]{1,0:T(8,128)}, u32[]{:S(2)}) copy-start(f32[64,128]{1,0:T(8,128)} %constant.16.clone) | copy-start | bytes 98308
  0.7 5.4 %copy-start.3 = (f32[32,128]{1,0:T(8,128)S(1)}, f32[32,128]{1,0:T(8,128)}, u32[]{:S(2)}) copy-start(f32[32,128]{1,0:T(8,128)} %constant.15.clone) | copy-start | bytes 49156

commit v6 on v5

--- a/solution.py
+++ b/solution.py
@@ -779,7 +779,7 @@
 
 class Steps:
     def __init__(self, start):
-        self.now, self.free, self.waiting = start, {}, []
+        self.now, self.free, self.waiting, self.held = start, {}, [], []
 
     def send(self, transfers):
         ends = [self.now]
@@ -789,9 +789,10 @@
             ends.append(self.free[link] + 2.0)
         return max(ends)
 
-    def open(self, chunks):
-        for chunk in chunks:
-            self.waiting.append((self.send(chunk.opening()), len(self.waiting), chunk, 0))
+    def open(self, chunks, depth=None):
+        entries = [(self.send(chunk.opening()), n, chunk, 0) for n, chunk in enumerate(chunks)]
+        self.waiting += entries[:depth]
+        self.held += entries[depth:] if depth else []
 
     def due(self, everything=False):
         stages = []
@@ -804,6 +805,9 @@
             self.now = max(self.now, when) + 0.4
             stage, transfers = chunk.plan()[index]
             stages.append(stage)
+            if index == 1 and self.held:
+                ready, *rest = self.held.pop(0)
+                self.waiting.append((max(ready, self.now), *rest))
             if index + 1 < len(chunk.plan()):
                 self.waiting.append((self.send(transfers), number, chunk, index + 1))
         return stages
@@ -993,7 +997,7 @@
         chunk.stage_start()
     steps = Steps(3.0)
     steps.free.update(x=11.0, y=11.0)
-    steps.open(chunks)
+    steps.open(chunks, 3)
     for copy in loads:
         copy.wait()
     slots = []
@@ -1069,11 +1073,11 @@
     chunks, shapes = [], []
     for index, term in enumerate(terms):
         rows, columns = term.shape[0] // 8, term.shape[1]
-        parts = 2 if rows % 32 == 0 and index < 3 else 1
+        parts = (2, 4, 4, 2)[index]
         chunks += [Chunk(index, n * rows // parts, rows // parts, columns) for n in range(parts)]
         shapes.append((2, rows, columns))
     rows = depth // 8
-    first_chunks = [Chunk(4, n * rows // 2, rows // 2, 3 * width, True) for n in range(2)]
+    first_chunks = [Chunk(4, n * rows // 4, rows // 4, 3 * width, True) for n in range(4)]
     first_chunks += [RowChunk(5, n * tokens // 4, tokens // 4, depth) for n in range(4)]
     shapes += [(2, rows, 12 * width), (tokens, depth)]
     anywhere = pl.BlockSpec(memory_space=pl.ANY)

time: 346 us -> 337 us (0.974); the launches traced: 346 us -> 332 us
  Pallas kernels: 338 us -> 325 us
    pallas_call x1, Pallas kernels: 163 us -> 150 us  [back(): pl.pallas_call(functools.partial(back_kernel, chunks, first_chunks, width...]
where the time goes in v6:
time: 337 us; the launch traced here: 332 us
  Pallas kernels  325 us (96%)
  other arithmetic  5.17 us (2%)
    pallas_call x1, Pallas kernels, back(): pl.pallas_call(functools.partial(back_kernel, chunks, first_chunks, width...  150 us
    pallas_call x1, Pallas kernels, front(): pl.pallas_call(functools.partial(front_kernel, width // HEAD_DIM), in_spe...  114 us
    pallas_call x1, Pallas kernels, dense(): pl.pallas_call(dense_kernel, grid=(hidden // tile,), in_specs=[activation...  46.8 us
    pallas_call x1, Pallas kernels, tail(): pl.pallas_call(tail_kernel, in_specs=[anywhere] * 11 + [inside] * 2, out_...  14.5 us

profile of v6, /device:TPU:0, one launch (start us, length us, event | category | flops | bytes accessed | tf_op | source)
XLA Modules:
  0.0 332.2 jit_solution(261788738423494182)
XLA Ops:
  0.6 0.0 copy-start
  0.7 0.0 copy-start.2
  0.7 0.0 copy-start.1
  0.7 0.0 copy-start.3
  0.7 1.5 fusion
  2.2 1.4 copy.26.source_ref
  3.6 2.5 fusion.2.x_ref
  6.1 0.0 copy-done
  6.1 0.0 copy-done.2
  6.1 0.0 copy-done.1
  6.1 0.0 copy-done.3
  6.1 1.1 multiply_add_fusion
  7.2 113.7 %front.1 = (bf16[4,512,1024]{2,1,0:T(8,128)(2,1)}, bf16[4,512,1024]{2,1,0:T(8,128)(2,1)}, bf16[512,1024]{1,0:T(8,128)(2,1)}, bf16[2048,256]{1,0:T(8,128)(2,1)}, ...) custom-call(s32[8]{0:T(128)} %flag_ref.3, ...), custom_call_target="tpu_custom_call" | custom-call | tf_op jit(solution)/shard_map/front/pallas_call | solution.py:1533
  120.9 46.8 %dense.1 = (bf16[512,1024]{1,0:T(8,128)(2,1)}, f32[512,1024]{1,0:T(8,128)}, bf16[512,1024]{1,0:T(8,128)(2,1)}, bf16[2816,1024]{1,0:T(8,128)(2,1)}, bf16[1024,281...) custom-call(bf16[512,1024]{1,0:T(8,128)(2,1)} %bitcast.24, bf16[512,1024]{1,0:T(8,128)(2,1)} %bitcast.41, ...), custom_call_target="tpu_custom_call" | custom-call | flops 26843545600 | bytes 45088768 | tf_op jit(solution)/shard_map/dense/pallas_call | solution.py:1651
  167.7 149.8 %back.1 = (bf16[2,352,1024]{2,1,0:T(8,128)(2,1)}, bf16[2,128,2816]{2,1,0:T(8,128)(2,1)}, bf16[2,128,2816]{2,1,0:T(8,128)(2,1)}, bf16[2,128,1024]{2,1,0:T(8,128)(...) custom-call(s32[8]{0:T(128)} %flag_ref.3, bf16[512,1024]{1,0:T(8,128)(2,1)} %get-tuple-element.40.g_ref, ...), custom_call_target="tpu_custom_call" | custom-call | tf_op jit(solution)/shard_map/back/pallas_call | solution.py:1095
  317.5 14.5 %tail.1 = (f32[512,1024]{1,0:T(8,128)}, f32[1,256]{1,0:T(1,128)}, f32[1,256]{1,0:T(1,128)}, f32[256,3072]{1,0:T(8,128)}, f32[256,1024]{1,0:T(8,128)}, /*index=5*...) custom-call(bf16[704,1024]{1,0:T(8,128)(2,1)} %bitcast.31, bf16[256,2816]{1,0:T(8,128)(2,1)} %bitcast.32, ...), custom_call_target="tpu_custom_call" | custom-call | tf_op jit(solution)/shard_map/tail/pallas_call | solution.py:1834
  (1 shorter events, 0.0 us)
Async XLA Ops:
  0.6 5.5 %copy-start = (f32[64,128]{1,0:T(8,128)S(1)}, f32[64,128]{1,0:T(8,128)}, u32[]{:S(2)}) copy-start(f32[64,128]{1,0:T(8,128)} %constant.18.clone) | copy-start | bytes 98308
  0.7 5.4 %copy-start.2 = (f32[32,128]{1,0:T(8,128)S(1)}, f32[32,128]{1,0:T(8,128)}, u32[]{:S(2)}) copy-start(f32[32,128]{1,0:T(8,128)} %constant.17.clone) | copy-start | bytes 49156
  0.7 5.4 %copy-start.1 = (f32[64,128]{1,0:T(8,128)S(1)}, f32[64,128]{1,0:T(8,128)}, u32[]{:S(2)}) copy-start(f32[64,128]{1,0:T(8,128)} %constant.16.clone) | copy-start | bytes 98308
  0.7 5.4 %copy-start.3 = (f32[32,128]{1,0:T(8,128)S(1)}, f32[32,128]{1,0:T(8,128)}, u32[]{:S(2)}) copy-start(f32[32,128]{1,0:T(8,128)} %constant.15.clone) | copy-start | bytes 49156

commit v7 on v6

--- a/solution.py
+++ b/solution.py
@@ -997,7 +997,7 @@
         chunk.stage_start()
     steps = Steps(3.0)
     steps.free.update(x=11.0, y=11.0)
-    steps.open(chunks, 3)
+    steps.open(chunks, 2)
     for copy in loads:
         copy.wait()
     slots = []

time: 337 us -> 345 us (1.024)
  Pallas kernels: 325 us -> 333 us
    pallas_call x1, Pallas kernels: 150 us -> 158 us  [back(): pl.pallas_call(functools.partial(back_kernel, chunks, first_chunks, width...]
where the time goes in v7:
time: 345 us; the launch traced here: 341 us
  Pallas kernels  333 us (97%)
  other arithmetic  5.17 us (1%)
    pallas_call x1, Pallas kernels, back(): pl.pallas_call(functools.partial(back_kernel, chunks, first_chunks, width...  158 us
    pallas_call x1, Pallas kernels, front(): pl.pallas_call(functools.partial(front_kernel, width // HEAD_DIM), in_spe...  114 us
    pallas_call x1, Pallas kernels, dense(): pl.pallas_call(dense_kernel, grid=(hidden // tile,), in_specs=[activation...  46.8 us
    pallas_call x1, Pallas kernels, tail(): pl.pallas_call(tail_kernel, in_specs=[anywhere] * 11 + [inside] * 2, out_...  14.5 us

profile of v7, /device:TPU:0, one launch (start us, length us, event | category | flops | bytes accessed | tf_op | source)
XLA Modules:
  0.0 340.8 jit_solution(2854717639146645495)
XLA Ops:
  0.6 0.0 copy-start
  0.7 0.0 copy-start.2
  0.7 0.0 copy-start.1
  0.7 0.0 copy-start.3
  0.7 1.5 fusion
  2.2 1.4 copy.26.source_ref
  3.6 2.5 fusion.2.x_ref
  6.1 0.0 copy-done
  6.1 0.0 copy-done.2
  6.1 0.0 copy-done.1
  6.1 0.0 copy-done.3
  6.1 1.1 multiply_add_fusion
  7.2 113.7 %front.1 = (bf16[4,512,1024]{2,1,0:T(8,128)(2,1)}, bf16[4,512,1024]{2,1,0:T(8,128)(2,1)}, bf16[512,1024]{1,0:T(8,128)(2,1)}, bf16[2048,256]{1,0:T(8,128)(2,1)}, ...) custom-call(s32[8]{0:T(128)} %flag_ref.3, ...), custom_call_target="tpu_custom_call" | custom-call | tf_op jit(solution)/shard_map/front/pallas_call | solution.py:1533
  120.9 46.8 %dense.1 = (bf16[512,1024]{1,0:T(8,128)(2,1)}, f32[512,1024]{1,0:T(8,128)}, bf16[512,1024]{1,0:T(8,128)(2,1)}, bf16[2816,1024]{1,0:T(8,128)(2,1)}, bf16[1024,281...) custom-call(bf16[512,1024]{1,0:T(8,128)(2,1)} %bitcast.24, bf16[512,1024]{1,0:T(8,128)(2,1)} %bitcast.41, ...), custom_call_target="tpu_custom_call" | custom-call | flops 26843545600 | bytes 45088768 | tf_op jit(solution)/shard_map/dense/pallas_call | solution.py:1651
  167.7 158.3 %back.1 = (bf16[2,352,1024]{2,1,0:T(8,128)(2,1)}, bf16[2,128,2816]{2,1,0:T(8,128)(2,1)}, bf16[2,128,2816]{2,1,0:T(8,128)(2,1)}, bf16[2,128,1024]{2,1,0:T(8,128)(...) custom-call(s32[8]{0:T(128)} %flag_ref.3, bf16[512,1024]{1,0:T(8,128)(2,1)} %get-tuple-element.40.g_ref, ...), custom_call_target="tpu_custom_call" | custom-call | tf_op jit(solution)/shard_map/back/pallas_call | solution.py:1095
  326.0 14.5 %tail.1 = (f32[512,1024]{1,0:T(8,128)}, f32[1,256]{1,0:T(1,128)}, f32[1,256]{1,0:T(1,128)}, f32[256,3072]{1,0:T(8,128)}, f32[256,1024]{1,0:T(8,128)}, /*index=5*...) custom-call(bf16[704,1024]{1,0:T(8,128)(2,1)} %bitcast.31, bf16[256,2816]{1,0:T(8,128)(2,1)} %bitcast.32, ...), custom_call_target="tpu_custom_call" | custom-call | tf_op jit(solution)/shard_map/tail/pallas_call | solution.py:1834
  (1 shorter events, 0.0 us)
Async XLA Ops:
  0.6 5.5 %copy-start = (f32[64,128]{1,0:T(8,128)S(1)}, f32[64,128]{1,0:T(8,128)}, u32[]{:S(2)}) copy-start(f32[64,128]{1,0:T(8,128)} %constant.18.clone) | copy-start | bytes 98308
  0.7 5.4 %copy-start.2 = (f32[32,128]{1,0:T(8,128)S(1)}, f32[32,128]{1,0:T(8,128)}, u32[]{:S(2)}) copy-start(f32[32,128]{1,0:T(8,128)} %constant.17.clone) | copy-start | bytes 49156
  0.7 5.4 %copy-start.1 = (f32[64,128]{1,0:T(8,128)S(1)}, f32[64,128]{1,0:T(8,128)}, u32[]{:S(2)}) copy-start(f32[64,128]{1,0:T(8,128)} %constant.16.clone) | copy-start | bytes 98308
  0.7 5.4 %copy-start.3 = (f32[32,128]{1,0:T(8,128)S(1)}, f32[32,128]{1,0:T(8,128)}, u32[]{:S(2)}) copy-start(f32[32,128]{1,0:T(8,128)} %constant.15.clone) | copy-start | bytes 49156
